TPU v7x, 256 devices: a whole 4x4x8 slice. The times are simulated.
256 devices in a mesh: date: 8 (over x, y_hi), path: 32 (over z, y_lo, core).
Axes of the slice: x: 4, y: 4 (y_hi: 2, y_lo: 2; y = y_hi * 2 + y_lo), z: 8, core: 2. Of those that a mesh axis runs over, the one named last changes fastest.
Arguments:
- factors: bfloat16 [64, 16, 131072], P('date', None, 'path'), may hold values from -10 to 10
- cashflows: bfloat16 [64, 64, 131072], P('date', None, 'path'), may hold values from -12 to 12
- frequency: bfloat16 [128, 16], replicated, may hold values from -1.5 to 1.5
- phases: float32 [128], replicated, may hold values from -3.140625 to 3.140625
- margin_lag: int32 [64], replicated, may hold values from 1 to 2
- thresholds: int32 [64], replicated, may hold values from 0 to 149
- transfer_min: int32 [64], replicated, may hold values from 0 to 59
Outputs:
- exposure: bfloat16 [64, 64, 131072], P('date', None, 'path')
- profile: float32 [64, 64], P('date')
All inputs are finite; a program needn't handle non-finite values.
Results may differ from a plain program's by a relative error of at most 0.0058.
Values may be sent and summed in bfloat16 or wider, within the bound.
No kernel may reach another device: no remote copies, remote signals or barrier semaphores. Data moves between devices by JAX's collectives and lax.ppermute only.
A program may use at most 128 MiB of HBM per device.

v0:
```python
import jax
import jax.numpy as jnp
from jax import lax
from jax.sharding import PartitionSpec as P

LAG_MAX = 2


ridge_weight = 0.05
root_two = 1.4142135623730951


def shifted_2(value, axis, by):
    length = lax.axis_size(axis)
    pairs = [(i, i + by) for i in range(length) if 0 <= i + by < length]
    return lax.ppermute(value, axis, pairs)


def packed_total(arrays, axis):
    ends = [0]
    for a in arrays:
        ends.append(ends[-1] + a.size)
    total = lax.psum(jnp.concatenate([a.ravel() for a in arrays]), axis)
    return tuple((total[b:e].reshape(a.shape) for a, b, e in zip(arrays, ends, ends[1:])))


def from_everyone(value, axis):
    length = lax.axis_size(axis)
    return lax.all_to_all(
        jnp.broadcast_to(value[None], (length, *value.shape)), axis, 0, 0, tiled=True
    )


def over_copies(value, axis):
    return from_everyone(value, axis).sum(axis=0)


def featurize(frequency, phases, factors):
    angles = jnp.einsum("kr,trp->tkp", frequency, factors, preferred_element_type=jnp.float32)
    angles = angles + phases[None, :, None]
    return (root_two * jnp.cos(angles)).astype(jnp.bfloat16)


def regress(gram_sum, right_sum, paths_all):
    system = (
        gram_sum / paths_all + ridge_weight * jnp.eye(gram_sum.shape[-1], dtype=jnp.float32)[None]
    )
    factor = lax.linalg.cholesky(system)
    solved = lax.linalg.triangular_solve(factor, right_sum / paths_all, left_side=True, lower=True)
    solved = lax.linalg.triangular_solve(
        factor, solved, left_side=True, lower=True, transpose_a=True
    )
    return solved.astype(jnp.bfloat16)


def fitted(coefficients, features):
    return jnp.einsum(
        "tkn,tkp->tnp", coefficients, features, preferred_element_type=jnp.float32
    ).astype(jnp.bfloat16)


def local(factors, cashflows, frequency, phases, margin_lag, thresholds, transfer_min):
    prior_factors = shifted_2(factors[-LAG_MAX:], "date", 1)
    features = featurize(frequency, phases, factors)
    gram_sum = jnp.einsum("tkp,tjp->tkj", features, features, preferred_element_type=jnp.float32)
    right_sum = jnp.einsum("tkp,tnp->tkn", features, cashflows, preferred_element_type=jnp.float32)
    gram_sum, right_sum = packed_total((gram_sum, right_sum), "path")
    paths_all = features.shape[2] * lax.axis_size("path")
    coefficients = regress(gram_sum, right_sum, paths_all)
    values = fitted(coefficients, features)
    prior_coefs = shifted_2(coefficients[-LAG_MAX:], "date", 1)
    prior_values = fitted(prior_coefs, featurize(frequency, phases, prior_factors))
    joined = jnp.concatenate([prior_values, values], axis=0)
    dates_here = values.shape[0]
    lagged = jnp.zeros(values.shape, jnp.float32)
    for lag_value in range(1, LAG_MAX + 1):
        shifted = joined[LAG_MAX - lag_value : LAG_MAX - lag_value + dates_here].astype(jnp.float32)
        lagged = jnp.where((margin_lag == lag_value)[None, :, None], shifted, lagged)
    offset = (thresholds + transfer_min).astype(jnp.float32) / 100.0
    collateral = jnp.maximum(lagged - offset[None, :, None], 0.0)
    exposure = jnp.maximum(values.astype(jnp.float32) - collateral, 0.0)
    profile = over_copies(jnp.sum(exposure, axis=2), "path") / paths_all
    return (exposure.astype(jnp.bfloat16), profile)


def solution(mesh):
    return jax.shard_map(
        local,
        mesh=mesh,
        in_specs=(P("date", None, "path"), P("date", None, "path"), P(), P(), P(), P(), P()),
        out_specs=(P("date", None, "path"), P("date", None)),
        check_vma=False,
    )
```

profile of v0, /device:TPU:2, one launch (start us, length us, event | category | flops | bytes accessed | tf_op | source)
XLA Modules:
  0.0 541.8 jit_solution(3618707060904881406)
XLA Ops:
  7.2 0.0 copy-start
  7.2 0.0 all-reduce.2.cloned.1.call-start
  7.2 0.6 copy-done
  7.9 58.2 %multiply_convert_fusion = bf16[8,4096,128]{2,1,0:T(8,128)(2,1)S(1)} fusion(bf16[8,16,4096]{2,1,0:T(8,128)(2,1)} %param.7, f32[128]{0:T(128)} %param.10, bf16[128,16]{0,1:T(8,128)(2,1)S(1)} %copy-done), kind=kOutput, calls=%fused_computation | convolution fusion | flops 146800640 | bytes 9441792 | tf_op jit(solution)/shard_map/kr,trp->tkp/dot_general | solution.py:39
  66.1 0.0 copy-start.1
  66.1 2.5 fusion.13
  68.6 0.7 copy-done.1
  69.3 0.0 copy-start.2
  69.3 0.0 copy-start.3
  69.3 0.0 copy-start.4
  69.3 4.8 fusion.14
  74.2 0.1 reshape.58
  74.3 0.9 pad_maximum_fusion.1
  75.2 0.0 all-reduce.2.cloned.1.call-update
  75.3 1.0 slice.49
  76.2 5.6 %collective-permute-start.1 = (bf16[2,16,4096]{2,1,0:T(8,128)(2,1)S(1)}, bf16[2,16,4096]{2,1,0:T(8,128)(2,1)S(1)}, u32[]{:S(2)}, u32[]{:S(2)}) collective-permute-start(bf16[2,16,4096]{2,1,0:T(8,128)(2,1)S(1)} %slice.49), channel_id=1, source_target_pairs={{0,32},{32,64},{64,96},{96,128},{128,160},{160,192},{192,224},{1,3... | collective-permute-start | bytes 786440 | tf_op jit(solution)/shard_map/ppermute | solution.py:16
  81.8 0.1 copy.21
  82.0 0.0 copy-done.2
  82.0 0.0 copy-done.3
  82.0 0.0 copy-done.4
  82.0 221.9 %all-reduce.2.cloned.1.call-done = f32[196608]{0:T(1024)} async-done(((f32[196608]{0:T(1024)}), f32[196608]{0:T(1024)}) %all-reduce.2.cloned.1.call-update) | async-done | bytes 786448 | tf_op jit(solution)/shard_map/psum | solution.py:23
  304.0 1.1 slice_multiply_fusion
  305.0 0.2 copy.22
  305.3 0.2 copy.23
  305.5 0.1 fusion.7
  305.6 93.8 %custom-call.8 = f32[8,128,128]{2,1,0:T(8,128)S(1)} custom-call(f32[8,128,128]{2,1,0:T(8,128)S(1)} %fusion.7), custom_call_target="Cholesky" | custom-call | tf_op jit(solution)/shard_map/cholesky | solution.py:48
  399.3 0.1 select_reduce_fusion
  399.4 0.1 compare_reduce_fusion
  399.5 0.1 select_bitcast_fusion
  399.7 0.0 copy-start.5
  399.7 78.6 %custom-call.9 = f32[8,1,128,128]{2,3,1,0:T(8,128)S(1)} custom-call(f32[8,1,128,128]{3,2,1,0:T(8,128)S(1)} %select_bitcast_fusion), custom_call_target="InvertDiagBlocksLowerTriangular" | custom-call | tf_op jit(solution)/shard_map/triangular_solve | solution.py:50
  478.3 1.0 slice_multiply_fusion.1
  479.2 0.1 div.41
  479.4 1.0 fusion.5
  480.4 1.1 convolution_convert_fusion.2
  481.6 4.8 collective-permute-start
  486.4 8.4 %convolution_convert_fusion = bf16[8,64,4096]{2,1,0:T(8,128)(2,1)} fusion(bf16[8,128,64]{1,2,0:T(8,128)(2,1)S(1)} %convolution_convert_fusion.2, bf16[8,4096,128]{2,1,0:T(8,128)(2,1)} %copy-done.1), kind=kOutput, calls=%fused_computation.2 | convolution fusion | flops 538968064 | bytes 12713984 | tf_op jit(solution)/shard_map/tkn,tkp->tnp/dot_general | solution.py:57
  494.7 0.0 collective-permute-done.1
  494.7 0.0 collective-permute-done
  494.7 0.0 copy-done.5
  494.7 14.6 %convolution_convert_fusion.1 = bf16[2,64,4096]{2,1,0:T(8,128)(2,1)S(1)} fusion(bf16[2,128,64]{1,2,0:T(8,128)(2,1)S(1)} %collective-permute-done, bf16[2,16,4096]{2,1,0:T(8,128)(2,1)S(1)} %collective-permute-done.1, f32[128]{0:T(128)S(1)} %copy-done.5, bf16[128,16]{0,1:T(8,128)(2,1)S(1)} %copy-done), kind=kOutput, calls=%fused_computation.9 | convolution fusion | flops 171442176 | bytes 1348096 | tf_op jit(solution)/shard_map/tkn,tkp->tnp/dot_general | solution.py:57
  509.4 7.9 %fusion.12 = (f32[8,64]{1,0:T(8,128)S(1)}, bf16[8,64,4096]{2,1,0:T(8,128)(2,1)}) fusion(f32[64]{0:T(128)S(1)} %convert_multiply_fusion, bf16[8,64,4096]{2,1,0:T(8,128)(2,1)} %convolution_convert_fusion, bf16[2,64,4096]{2,1,0:T(8,128)(2,1)S(1)} %convolution_convert_fusion.1, pred[64]{0:T(512)(128)(4,1)S(1)} %get-tuple-element.5, ...), kind=kLoop, calls=%fused_computation.35 | loop fusion | flops 27262464 | bytes 9439616 | tf_op jit(solution)/shard_map/reduce_sum | solution.py:82
  517.2 0.1 reshape.60
  517.4 15.4 %all_to_all.5 = f32[32,1,512]{2,1,0:T(1,128)S(1)} all-to-all(f32[32,1,512]{2,1,0:T(1,128)S(1)} %reshape.60), channel_id=1, replica_groups=mesh['date'=8,'path'=32] {'path'}, dimensions={0} | all-to-all | bytes 131072 | tf_op jit(solution)/shard_map/all_to_all | solution.py:29
  532.7 0.5 broadcast.86
  533.2 0.8 reduce.4
  534.0 0.1 reshape.61
  534.2 0.6 broadcast_multiply_fusion
  (9 shorter events, 0.1 us)
Async XLA Ops:
  7.2 0.7 copy-start
  7.2 296.8 %all-reduce.2.cloned.1.call-start = ((), (), s32[]{:S(2)}) async-start(), calls=%async_computation.1 | async-start | bytes 1572864 | tf_op jit(solution)/shard_map/psum | solution.py:23
  66.1 3.2 copy-start.1
  69.3 12.7 %copy-start.2 = (s32[64]{0:T(128)S(1)}, s32[64]{0:T(128)}, u32[]{:S(2)}) copy-start(s32[64]{0:T(128)} %param.11) | copy-start | bytes 772
  69.3 12.7 %copy-start.3 = (s32[64]{0:T(128)S(1)}, s32[64]{0:T(128)}, u32[]{:S(2)}) copy-start(s32[64]{0:T(128)} %param.12) | copy-start | bytes 772
  69.3 12.7 %copy-start.4 = (s32[64]{0:T(128)S(1)}, s32[64]{0:T(128)}, u32[]{:S(2)}) copy-start(s32[64]{0:T(128)} %param.13) | copy-start | bytes 772
  76.2 418.5 %collective-permute-start.1 = (bf16[2,16,4096]{2,1,0:T(8,128)(2,1)S(1)}, bf16[2,16,4096]{2,1,0:T(8,128)(2,1)S(1)}, u32[]{:S(2)}, u32[]{:S(2)}) collective-permute-start(bf16[2,16,4096]{2,1,0:T(8,128)(2,1)S(1)} %slice.49), channel_id=1, source_target_pairs={{0,32},{32,64},{64,96},{96,128},{128,160},{160,192},{192,224},{1,3... | collective-permute-start | bytes 786440 | tf_op jit(solution)/shard_map/ppermute | solution.py:16
  399.7 95.1 %copy-start.5 = (f32[128]{0:T(128)S(1)}, f32[128]{0:T(128)}, u32[]{:S(2)}) copy-start(f32[128]{0:T(128)} %param.10) | copy-start | bytes 1540
  481.6 13.2 %collective-permute-start = (bf16[2,128,64]{1,2,0:T(8,128)(2,1)S(1)}, bf16[2,128,64]{1,2,0:T(8,128)(2,1)S(1)}, u32[]{:S(2)}, u32[]{:S(2)}) collective-permute-start(bf16[2,128,64]{1,2,0:T(8,128)(2,1)S(1)} %slice.54), channel_id=1, source_target_pairs={{0,32},{32,64},{64,96},{96,128},{128,160},{160,192},{192,224},{1,3... | collective-permute-start | bytes 98312 | tf_op jit(solution)/shard_map/ppermute | solution.py:16
Sparse Core Ops, SparseCore 0:
  75.4 228.5 all-reduce.1
where the time goes:
time: 550 us; the launch traced here: 542 us
  waiting for transfers between devices  222 us (40%)
  other arithmetic  185 us (34%)
  matrix products  90.7 us (16%)
  blocking collectives  15.4 us (3%)
  between operations  14.5 us (3%)
  starting transfers between devices  10.4 us (2%)
    psum x1, waiting for transfers between devices, packed_total(): total = lax.psum(jnp.concatenate([a.ravel() for a in arrays]), axis)  222 us
    another operation x4, other arithmetic, regress(): factor = lax.linalg.cholesky(system)  94 us
    another operation x3, other arithmetic, regress(): lax.linalg.triangular_solve(factor, solved, left_side=True, lower=True, t...  78.7 us
    dot_general x1, matrix products, featurize(): jnp.einsum('kr,trp->tkp', frequency, factors, preferred_element_type=jnp....  58.2 us
    dot_general x2, matrix products, fitted(): jnp.einsum('tkn,tkp->tnp', coefficients, features, preferred_element_type...  23 us
    all_to_all x1, blocking collectives, from_everyone(): lax.all_to_all(jnp.broadcast_to(value[None], (length, *value.shape)), axi...  15.4 us
  transfers between devices with their start and end apart: 3, of which 1 were waited for; matrix products, arithmetic and copies ran while one was open for 35% of the time, Pallas kernels for 0%

commit v1 on v0

v1 whole, which is shorter than its diff:
```python
import functools

import jax
import jax.numpy as jnp
from jax import lax
from jax.experimental import pallas as pl
from jax.experimental.pallas import tpu as pltpu
from jax.sharding import PartitionSpec as P

LAG_MAX = 2
ridge_weight = 0.05
COS_TERMS = (
    1.4142124652862549,
    -27.915136337280273,
    91.82308197021484,
    -120.5933837890625,
    83.14732360839844,
    -29.807071685791016,
)
ROUNDER = 12582912.0
INV_TWO_PI = 0.15915494309189535
CHUNK = 512


def three_parts(x):
    hi = x.astype(jnp.bfloat16)
    rest = x - hi.astype(jnp.float32)
    mid = rest.astype(jnp.bfloat16)
    low = (rest - mid.astype(jnp.float32)).astype(jnp.bfloat16)
    return hi, mid, low


def turn_weights(freq_ref, phase_ref):
    k, r = freq_ref.shape
    parts = three_parts(freq_ref[...].astype(jnp.float32) * INV_TWO_PI)
    column = jnp.broadcast_to(phase_ref[...] * INV_TWO_PI, (k, k)).T[:, :r]
    place = lax.broadcasted_iota(jnp.int32, (k, r), 1)
    tail = jnp.zeros((k, r), jnp.float32)
    for i, part in enumerate(three_parts(column)):
        tail = jnp.where(place == i, part.astype(jnp.float32), tail)
    return jnp.concatenate([*parts, tail.astype(jnp.bfloat16)], axis=1)


def chunk_features(weights, x):
    ones = jnp.ones(x.shape, jnp.bfloat16)
    turns = jnp.dot(
        weights, jnp.concatenate([x, x, x, ones], axis=0), preferred_element_type=jnp.float32
    )
    part = turns - ((turns + ROUNDER) - ROUNDER)
    s = part * part
    total = jnp.full(s.shape, COS_TERMS[-1], jnp.float32)
    for term in COS_TERMS[-2::-1]:
        total = total * s + term
    return total.astype(jnp.bfloat16)


def features_kernel(freq_ref, phase_ref, factors_ref, features_ref, weights_ref):
    @pl.when(pl.program_id(0) == 0)
    def _():
        weights_ref[...] = turn_weights(freq_ref, phase_ref)

    for at in range(0, factors_ref.shape[2], CHUNK):
        span = pl.ds(at, CHUNK)
        features_ref[0, :, span] = chunk_features(weights_ref[...], factors_ref[0, :, span])


def sums_kernel(freq_ref, phase_ref, factors_ref, flows_ref, features_ref, sums_ref, weights_ref):
    @pl.when(pl.program_id(0) == 0)
    def _():
        weights_ref[...] = turn_weights(freq_ref, phase_ref)

    k = freq_ref.shape[0]
    dims = (((1,), (1,)), ((), ()))
    gram = jnp.zeros((k, k), jnp.float32)
    right = jnp.zeros((flows_ref.shape[1], k), jnp.float32)
    for at in range(0, factors_ref.shape[2], CHUNK):
        span = pl.ds(at, CHUNK)
        feats = chunk_features(weights_ref[...], factors_ref[0, :, span])
        features_ref[0, :, span] = feats
        gram += lax.dot_general(feats, feats, dims, preferred_element_type=jnp.float32)
        right += lax.dot_general(
            flows_ref[0, :, span], feats, dims, preferred_element_type=jnp.float32
        )
    sums_ref[0, :k, :] = gram
    sums_ref[0, k:, :] = right


def whole(a):
    return pl.BlockSpec(a.shape, lambda t: (0,) * a.ndim)


def per_date(a):
    return pl.BlockSpec((1, *a.shape[1:]), lambda t: (t,) + (0,) * (a.ndim - 1))


def params(limit=48 << 20):
    return pltpu.CompilerParams(vmem_limit_bytes=limit)


def features_of(frequency, phases, factors):
    dates, r, paths = factors.shape
    k = frequency.shape[0]
    out = jax.ShapeDtypeStruct((dates, k, paths), jnp.bfloat16)
    return pl.pallas_call(
        features_kernel,
        grid=(dates,),
        in_specs=[whole(frequency), whole(phases), per_date(factors)],
        out_specs=per_date(out),
        out_shape=out,
        scratch_shapes=[pltpu.VMEM((k, 4 * r), jnp.bfloat16)],
        compiler_params=params(),
        cost_estimate=pl.CostEstimate(
            flops=16 * dates * k * paths, bytes_accessed=2 * dates * k * paths, transcendentals=0
        ),
        name="features",
    )(frequency, phases, factors)


def sums_of(frequency, phases, factors, flows):
    dates, r, paths = factors.shape
    k, sets = frequency.shape[0], flows.shape[1]
    outs = (
        jax.ShapeDtypeStruct((dates, k, paths), jnp.bfloat16),
        jax.ShapeDtypeStruct((dates, k + sets, k), jnp.float32),
    )
    return pl.pallas_call(
        sums_kernel,
        grid=(dates,),
        in_specs=[whole(frequency), whole(phases), per_date(factors), per_date(flows)],
        out_specs=tuple(per_date(o) for o in outs),
        out_shape=outs,
        scratch_shapes=[pltpu.VMEM((k, 4 * r), jnp.bfloat16)],
        compiler_params=params(),
        cost_estimate=pl.CostEstimate(
            flops=400 * dates * k * paths, bytes_accessed=4 * dates * k * paths, transcendentals=0
        ),
        name="sums",
    )(frequency, phases, factors, flows)


def solve_kernel(paths_all, one_ref, two_ref, out_ref):
    k = one_ref.shape[1]
    total = (one_ref[...] + two_ref[...]) / paths_all
    row_at = lax.broadcasted_iota(jnp.int32, (k, k), 0)
    lane_at = lax.broadcasted_iota(jnp.int32, (k, k), 1)
    system = total[:k] + jnp.where(row_at == lane_at, ridge_weight, 0.0)
    m = jnp.concatenate([system, total[k:]], axis=0)
    lane = lax.broadcasted_iota(jnp.int32, (1, k), 1)
    for j in range(k):
        top = j // 8 * 8
        row = m[j - (k + 64 - m.shape[0]) : j - (k + 64 - m.shape[0]) + 1, :]
        pivot = 1.0 / row[:, j : j + 1]
        scaled = jnp.where(lane == j, 1.0 - pivot, row * pivot)
        if (j + 1) % 8 == 0:
            m = m[8:, :]
        m = m - m[:, j : j + 1] * scaled
    out_ref[...] = m.astype(jnp.bfloat16)


def solved(one, two, paths_all):
    k = one.shape[1]
    sets = one.shape[0] - k
    return pl.pallas_call(
        functools.partial(solve_kernel, paths_all),
        out_shape=jax.ShapeDtypeStruct((sets, k), jnp.bfloat16),
        compiler_params=params(),
        name="solve",
    )(one, two)


def exposure_kernel(
    paths_all,
    lag_ref,
    threshold_ref,
    transfer_ref,
    coefs_ref,
    prior_coefs_ref,
    features_ref,
    prior_features_ref,
    exposure_ref,
    profile_ref,
    old_ref,
    sums_ref,
):
    t = pl.program_id(0)
    dates = pl.num_programs(0)
    sets, paths = exposure_ref.shape[1:]
    slots = LAG_MAX + 1

    def value(coefs, feats):
        return jnp.dot(coefs, feats, preferred_element_type=jnp.float32).astype(jnp.bfloat16)

    @pl.when(t == 0)
    def _():
        for i in range(LAG_MAX):
            for at in range(0, paths, CHUNK):
                span = pl.ds(at, CHUNK)
                old_ref[i + 1, :, span] = value(prior_coefs_ref[i], prior_features_ref[i, :, span])

    def column(ref):
        return jnp.broadcast_to(ref[...], (128, sets)).T

    offset = (column(threshold_ref) + column(transfer_ref)).astype(jnp.float32) / 100.0
    recent = column(lag_ref) == 1
    wide = (sets, CHUNK)
    offset = jnp.concatenate([offset] * (CHUNK // 128), axis=1)
    recent = jnp.concatenate([recent.astype(jnp.float32)] * (CHUNK // 128), axis=1) > 0.5
    total = jnp.zeros((sets, 128), jnp.float32)
    now = lax.rem(t, slots)
    last = lax.rem(t + LAG_MAX, slots)
    before = lax.rem(t + 1, slots)
    for at in range(0, paths, CHUNK):
        span = pl.ds(at, CHUNK)
        v = value(coefs_ref[0], features_ref[0, :, span])
        lagged = jnp.where(
            recent,
            old_ref[last, :, span].astype(jnp.float32),
            old_ref[before, :, span].astype(jnp.float32),
        )
        old_ref[now, :, span] = v
        collateral = jnp.maximum(lagged - offset, 0.0)
        exposed = jnp.maximum(v.astype(jnp.float32) - collateral, 0.0)
        exposure_ref[0, :, span] = exposed.astype(jnp.bfloat16)
        for i in range(0, CHUNK, 128):
            total += exposed[:, i : i + 128]
    here = jnp.sum(total, axis=1, keepdims=True) / paths_all
    lane = lax.broadcasted_iota(jnp.int32, (sets, 128), 1)

    @pl.when(t == 0)
    def _():
        sums_ref[...] = jnp.zeros(sums_ref.shape, jnp.float32)

    sums_ref[...] = jnp.where(lane == t, here, sums_ref[...])

    @pl.when(t == dates - 1)
    def _():
        profile_ref[...] = sums_ref[...].T[: profile_ref.shape[0]]


def exposures(lag, threshold, transfer, coefs, prior_coefs, features, prior_features, paths_all):
    dates, k, paths = features.shape
    sets = coefs.shape[1]
    outs = (
        jax.ShapeDtypeStruct((dates, sets, paths), jnp.bfloat16),
        jax.ShapeDtypeStruct((dates, sets), jnp.float32),
    )
    args = (lag, threshold, transfer, coefs, prior_coefs, features, prior_features)
    return pl.pallas_call(
        functools.partial(exposure_kernel, paths_all),
        grid=(dates,),
        in_specs=[
            whole(lag),
            whole(threshold),
            whole(transfer),
            per_date(coefs),
            whole(prior_coefs),
            per_date(features),
            whole(prior_features),
        ],
        out_specs=(per_date(outs[0]), whole(outs[1])),
        out_shape=outs,
        scratch_shapes=[
            pltpu.VMEM((LAG_MAX + 1, sets, paths), jnp.bfloat16),
            pltpu.VMEM((sets, 128), jnp.float32),
        ],
        compiler_params=params(),
        cost_estimate=pl.CostEstimate(
            flops=2 * dates * k * sets * paths,
            bytes_accessed=2 * dates * (k + sets) * paths,
            transcendentals=0,
        ),
        name="exposure",
    )(*args)


def by_core(i):
    return i ^ 1


def by_row(i):
    return i ^ 2


def by_near(i):
    return i ^ 4


def by_next(i):
    return i ^ 8


def by_far(i):
    z = i // 4
    return (6 - z + 2 * (z % 2)) % 8 * 4 + i % 4


def swapped(value, partner):
    length = lax.axis_size("path")
    return lax.ppermute(value, "path", [(i, partner(i)) for i in range(length)])


def halved(value, partner, bit):
    other = lax.dynamic_index_in_dim(value, 1 - bit, 0, keepdims=False)
    mine = lax.dynamic_index_in_dim(value, bit, 0, keepdims=False)
    return mine + swapped(other, partner)


def doubled(value, partner, bit):
    other = swapped(value, partner)
    low = jnp.where(bit == 0, value, other)
    high = jnp.where(bit == 0, other, value)
    return jnp.concatenate([low, high], axis=0)


def from_earlier(value):
    length = lax.axis_size("date")
    return lax.ppermute(value, "date", [(i, i + 1) for i in range(length - 1)])


def local(factors, cashflows, frequency, phases, margin_lag, thresholds, transfer_min):
    paths_all = factors.shape[2] * lax.axis_size("path")
    me = lax.axis_index("path")
    core, row, near = me % 2, me // 2 % 2, me // 4 % 2
    prior_factors = from_earlier(factors[-LAG_MAX:])
    phases = phases.reshape(1, -1)
    features, sums = sums_of(frequency, phases, factors, cashflows)
    kept = halved(sums.reshape(2, 4, *sums.shape[1:]), by_core, core)
    kept = halved(kept.reshape(2, 2, *sums.shape[1:]), by_row, row)
    kept = halved(kept, by_near, near)
    kept = kept + swapped(kept, by_next)
    coefs = solved(kept, swapped(kept, by_far), paths_all)
    prior_features = features_of(frequency, phases, prior_factors)
    coefs = doubled(coefs[None], by_near, near)
    coefs = doubled(coefs, by_row, row)
    coefs = doubled(coefs, by_core, core)
    prior_coefs = from_earlier(coefs[-LAG_MAX:])
    exposure, profile = exposures(
        margin_lag.reshape(1, -1),
        thresholds.reshape(1, -1),
        transfer_min.reshape(1, -1),
        coefs,
        prior_coefs,
        features,
        prior_features,
        paths_all,
    )
    for partner in (by_core, by_row, by_near, by_next, by_far):
        profile = profile + swapped(profile, partner)
    return exposure, profile


def solution(mesh):
    return jax.shard_map(
        local,
        mesh=mesh,
        in_specs=(P("date", None, "path"), P("date", None, "path"), P(), P(), P(), P(), P()),
        out_specs=(P("date", None, "path"), P("date", None)),
        check_vma=False,
    )
```

time: 550 us -> 123 us (0.22); the launches traced: 542 us -> 122 us
  waiting for transfers between devices: 222 us -> 36.2 us
  other arithmetic: 185 us -> 0.77 us
  matrix products: 90.7 us -> 0 us
  Pallas kernels: 0 us -> 42.9 us
  starting transfers between devices: 10.4 us -> 35.5 us
  blocking collectives: 15.4 us -> 0 us
  between operations: 14.5 us -> 0.88 us
    psum x1 -> x0, waiting for transfers between devices: 222 us -> none  [packed_total(): total = lax.psum(jnp.concatenate([a.ravel() for a in arrays]), axis)]
    another operation x7 -> x0, other arithmetic: 173 us -> none  [the longest x4 94 us: regress(): factor = lax.linalg.cholesky(system)]
    dot_general x5 -> x0, matrix products: 88.5 us -> none  [the longest x1 58.2 us: featurize(): jnp.einsum('kr,trp->tkp', frequency, factors, preferred_element_type=jnp....]
    pallas_call x0 -> x4, Pallas kernels: none -> 42.9 us  [the longest x1 19.4 us: sums_of(): pl.pallas_call(sums_kernel, grid=(dates,), in_specs=[whole(frequency), wh...]
    ppermute x2 -> x15, waiting for transfers between devices: 0.01 us -> 36.2 us  [the longest x13 26.4 us: swapped(): return lax.ppermute(value, 'path', [(i, partner(i)) for i in range(length)])]
    ppermute x2 -> x15, starting transfers between devices: 10.4 us -> 35.5 us  [the longest x13 26.8 us: swapped(): return lax.ppermute(value, 'path', [(i, partner(i)) for i in range(length)])]
    all_to_all x1 -> x0, blocking collectives: 15.4 us -> none  [from_everyone(): lax.all_to_all(jnp.broadcast_to(value[None], (length, *value.shape)), axi...]
    reduce_sum x2 -> x0, other arithmetic: 7.9 us -> none  [the longest x1 7.86 us: local(): profile = over_copies(jnp.sum(exposure, axis=2), 'path') / paths_all]
  transfers between devices with their start and end apart: 3 -> 15, of which waited for: 1 -> 13; matrix products, arithmetic and copies ran while one was open for 35% -> 1% of each run, Pallas kernels for 0% -> 2%
where the time goes in v1:
time: 123 us; the launch traced here: 122 us
  Pallas kernels  42.9 us (35%)
  waiting for transfers between devices  36.2 us (29%)
  starting transfers between devices  35.5 us (29%)
  local copies, waits for them, and re-layouts  5.92 us (5%)
    ppermute x13, starting transfers between devices, swapped(): return lax.ppermute(value, 'path', [(i, partner(i)) for i in range(length)])  26.8 us
    ppermute x13, waiting for transfers between devices, swapped(): return lax.ppermute(value, 'path', [(i, partner(i)) for i in range(length)])  26.4 us
    pallas_call x1, Pallas kernels, sums_of(): pl.pallas_call(sums_kernel, grid=(dates,), in_specs=[whole(frequency), wh...  19.4 us
    pallas_call x1, Pallas kernels, solved(): pl.pallas_call(functools.partial(solve_kernel, paths_all), out_shape=jax....  10.9 us
    pallas_call x1, Pallas kernels, exposures(): pl.pallas_call(functools.partial(exposure_kernel, paths_all), grid=(dates...  10.1 us
    ppermute x2, waiting for transfers between devices, from_earlier(): return lax.ppermute(value, 'date', [(i, i + 1) for i in range(length - 1)])  9.75 us
    ppermute x2, starting transfers between devices, from_earlier(): return lax.ppermute(value, 'date', [(i, i + 1) for i in range(length - 1)])  8.75 us
    unnamed x15, local copies, waits for them, and re-layouts  4.88 us
  transfers between devices with their start and end apart: 15, of which 13 were waited for; matrix products, arithmetic and copies ran while one was open for 1% of the time, Pallas kernels for 2%

profile of v1, /device:TPU:2, one launch (start us, length us, event | category | flops | bytes accessed | tf_op | source)
XLA Modules:
  0.0 122.2 jit_solution(5296022219279927520)
XLA Ops:
  0.6 0.8 copy.9.freq_ref
  1.4 0.0 copy-start
  1.5 1.2 copy-done
  2.7 0.0 copy-start.4
  2.7 0.7 copy-done.4
  3.3 0.0 copy-start.6
  3.3 2.2 %copy-done.6 = bf16[8,64,4096]{2,1,0:T(8,128)(2,1)S(1)} copy-done((bf16[8,64,4096]{2,1,0:T(8,128)(2,1)S(1)}, bf16[8,64,4096]{2,1,0:T(8,128)(2,1)}, u32[]{:S(2)}) %copy-start.6) | copy-done | bytes 4194328
  5.5 0.0 copy-start.5
  5.5 19.4 %sums.1 = (bf16[8,128,4096]{2,1,0:T(8,128)(2,1)}, f32[8,192,128]{2,1,0:T(8,128)S(1)}) custom-call(bf16[128,16]{1,0:T(8,128)(2,1)S(1)} %copy.9.freq_ref, f32[1,128]{1,0:T(1,128)S(1)} %bitcast.27, bf16[8,16,4096]{2,1,0:T(8,128)(2,1)S(1)} %copy-done, bf16[8,64,4096]{2,1,0:T(8,128)(2,1)S(1)} %copy-done.6), custom_call_target="tpu_custom_call" | custom-call | flops 1677721600 | bytes 16777216 | tf_op jit(solution)/shard_map/sums/pallas_call | solution.py:126
  25.0 0.0 copy-start.1
  25.0 0.0 copy-start.2
  25.0 0.0 copy-start.3
  25.0 0.1 collective-permute-start
  25.1 1.7 %collective-permute-done = f32[4,192,128]{2,1,0:T(8,128)S(1)} collective-permute-done((f32[4,192,128]{2,1,0:T(8,128)S(1)}, f32[4,192,128]{2,1,0:T(8,128)S(1)}, u32[]{:S(2)}, u32[]{:S(2)}) %collective-permute-start) | collective-permute-done | bytes 393248 | tf_op jit(solution)/shard_map/ppermute | solution.py:299
  26.9 1.7 %collective-permute-start.1 = (f32[2,192,128]{2,1,0:T(8,128)S(1)}, f32[2,192,128]{2,1,0:T(8,128)S(1)}, u32[]{:S(2)}, u32[]{:S(2)}) collective-permute-start(f32[2,192,128]{2,1,0:T(8,128)S(1)} %dynamic-slice_bitcast_fusion.1), channel_id=1, source_target_pairs={{0,2},{1,3},{2,0},{3,1},{4,6},{5,7},{6,4},{7,5},{8,10},{9,11},{10,... | collective-permute-start | bytes 589832 | tf_op jit(solution)/shard_map/ppermute | solution.py:299
  28.5 5.4 %collective-permute-done.1 = f32[2,192,128]{2,1,0:T(8,128)S(1)} collective-permute-done((f32[2,192,128]{2,1,0:T(8,128)S(1)}, f32[2,192,128]{2,1,0:T(8,128)S(1)}, u32[]{:S(2)}, u32[]{:S(2)}) %collective-permute-start.1) | collective-permute-done | bytes 196640 | tf_op jit(solution)/shard_map/ppermute | solution.py:299
  34.0 2.0 %collective-permute-start.2 = (f32[192,128]{1,0:T(8,128)S(1)}, f32[192,128]{1,0:T(8,128)S(1)}, u32[]{:S(2)}, u32[]{:S(2)}) collective-permute-start(f32[192,128]{1,0:T(8,128)S(1)} %dynamic-slice_bitcast_fusion.2), channel_id=1, source_target_pairs={{0,4},{1,5},{2,6},{3,7},{4,0},{5,1},{6,2},{7,3},{8,12},{9,13},{10,... | collective-permute-start | bytes 294920 | tf_op jit(solution)/shard_map/ppermute | solution.py:299
  36.0 2.7 %collective-permute-done.2 = f32[192,128]{1,0:T(8,128)S(1)} collective-permute-done((f32[192,128]{1,0:T(8,128)S(1)}, f32[192,128]{1,0:T(8,128)S(1)}, u32[]{:S(2)}, u32[]{:S(2)}) %collective-permute-start.2) | collective-permute-done | bytes 98336 | tf_op jit(solution)/shard_map/ppermute | solution.py:299
  38.7 3.4 %collective-permute-start.3 = (f32[192,128]{1,0:T(8,128)S(1)}, f32[192,128]{1,0:T(8,128)S(1)}, u32[]{:S(2)}, u32[]{:S(2)}) collective-permute-start(f32[192,128]{1,0:T(8,128)S(1)} %bitcast_add_fusion.2), channel_id=1, source_target_pairs={{0,8},{1,9},{2,10},{3,11},{4,12},{5,13},{6,14},{7,15},{8,0},{9,1},... | collective-permute-start | bytes 294920 | tf_op jit(solution)/shard_map/ppermute | solution.py:299
  42.0 2.6 %collective-permute-done.3 = f32[192,128]{1,0:T(8,128)S(1)} collective-permute-done((f32[192,128]{1,0:T(8,128)S(1)}, f32[192,128]{1,0:T(8,128)S(1)}, u32[]{:S(2)}, u32[]{:S(2)}) %collective-permute-start.3) | collective-permute-done | bytes 98336 | tf_op jit(solution)/shard_map/ppermute | solution.py:299
  44.6 6.1 %collective-permute-start.4 = (f32[192,128]{1,0:T(8,128)S(1)}, f32[192,128]{1,0:T(8,128)S(1)}, u32[]{:S(2)}, u32[]{:S(2)}) collective-permute-start(f32[192,128]{1,0:T(8,128)S(1)} %add.75.one_ref), channel_id=1, source_target_pairs={{0,24},{1,25},{2,26},{3,27},{4,28},{5,29},{6,30},{7,31},{8,16},{9,... | collective-permute-start | bytes 294920 | tf_op jit(solution)/shard_map/ppermute | solution.py:299
  50.8 2.7 %collective-permute-done.4.two_ref = f32[192,128]{1,0:T(8,128)S(1)} collective-permute-done((f32[192,128]{1,0:T(8,128)S(1)}, f32[192,128]{1,0:T(8,128)S(1)}, u32[]{:S(2)}, u32[]{:S(2)}) %collective-permute-start.4) | collective-permute-done | bytes 98336 | tf_op jit(solution)/shard_map/ppermute | solution.py:299
  53.4 10.9 %solve.1 = bf16[64,128]{1,0:T(8,128)(2,1)S(1)} custom-call(f32[192,128]{1,0:T(8,128)S(1)} %add.75.one_ref, f32[192,128]{1,0:T(8,128)S(1)} %collective-permute-done.4.two_ref), custom_call_target="tpu_custom_call" | custom-call | tf_op jit(solution)/shard_map/solve/pallas_call | solution.py:163
  64.3 2.6 %collective-permute-start.5 = (bf16[1,64,128]{2,1,0:T(8,128)(2,1)S(1)}, bf16[1,64,128]{2,1,0:T(8,128)(2,1)S(1)}, u32[]{:S(2)}, u32[]{:S(2)}) collective-permute-start(bf16[1,64,128]{2,1,0:T(8,128)(2,1)S(1)} %bitcast.23), channel_id=1, source_target_pairs={{0,4},{1,5},{2,6},{3,7},{4,0},{5,1},{6,2},{7,3},{8,12},{9,13},{10,... | collective-permute-start | bytes 49160 | tf_op jit(solution)/shard_map/ppermute | solution.py:299
  66.9 1.7 %collective-permute-done.5 = bf16[1,64,128]{2,1,0:T(8,128)(2,1)S(1)} collective-permute-done((bf16[1,64,128]{2,1,0:T(8,128)(2,1)S(1)}, bf16[1,64,128]{2,1,0:T(8,128)(2,1)S(1)}, u32[]{:S(2)}, u32[]{:S(2)}) %collective-permute-start.5) | collective-permute-done | bytes 16416 | tf_op jit(solution)/shard_map/ppermute | solution.py:299
  68.6 1.7 %collective-permute-start.6 = (bf16[2,64,128]{2,1,0:T(8,128)(2,1)S(1)}, bf16[2,64,128]{2,1,0:T(8,128)(2,1)S(1)}, u32[]{:S(2)}, u32[]{:S(2)}) collective-permute-start(bf16[2,64,128]{2,1,0:T(8,128)(2,1)S(1)} %pad_maximum_fusion.2), channel_id=1, source_target_pairs={{0,2},{1,3},{2,0},{3,1},{4,6},{5,7},{6,4},{7,5},{8,10},{9,11},{10,... | collective-permute-start | bytes 98312 | tf_op jit(solution)/shard_map/ppermute | solution.py:299
  70.3 1.0 slice.7
  71.3 4.8 %collective-permute-start.9 = (bf16[2,16,4096]{2,1,0:T(8,128)(2,1)S(1)}, bf16[2,16,4096]{2,1,0:T(8,128)(2,1)S(1)}, u32[]{:S(2)}, u32[]{:S(2)}) collective-permute-start(bf16[2,16,4096]{2,1,0:T(8,128)(2,1)S(1)} %slice.7), channel_id=1, source_target_pairs={{0,32},{32,64},{64,96},{96,128},{128,160},{160,192},{192,224},{1,3... | collective-permute-start | bytes 786440 | tf_op jit(solution)/shard_map/ppermute | solution.py:317
  76.1 0.0 collective-permute-done.6
  76.1 0.3 collective-permute-start.7
  76.4 5.5 %collective-permute-done.9.factors_ref = bf16[2,16,4096]{2,1,0:T(8,128)(2,1)S(1)} collective-permute-done((bf16[2,16,4096]{2,1,0:T(8,128)(2,1)S(1)}, bf16[2,16,4096]{2,1,0:T(8,128)(2,1)S(1)}, u32[]{:S(2)}, u32[]{:S(2)}) %collective-permute-start.9) | collective-permute-done | bytes 262176 | tf_op jit(solution)/shard_map/ppermute | solution.py:317
  81.9 0.0 copy-done.5
  81.9 2.5 %features.1.prior_features_ref = bf16[2,128,4096]{2,1,0:T(8,128)(2,1)S(1)} custom-call(bf16[128,16]{1,0:T(8,128)(2,1)S(1)} %copy.9.freq_ref, f32[1,128]{1,0:T(1,128)S(1)} %bitcast.28, bf16[2,16,4096]{2,1,0:T(8,128)(2,1)S(1)} %collective-permute-done.9.factors_ref), custom_call_target="tpu_custom_call" | custom-call | flops 16777216 | bytes 2097152 | tf_op jit(solution)/shard_map/features/pallas_call | solution.py:104
  84.4 0.0 collective-permute-done.7
  84.5 3.9 %collective-permute-start.8 = (bf16[2,64,128]{2,1,0:T(8,128)(2,1)S(1)}, bf16[2,64,128]{2,1,0:T(8,128)(2,1)S(1)}, u32[]{:S(2)}, u32[]{:S(2)}) collective-permute-start(bf16[2,64,128]{2,1,0:T(8,128)(2,1)S(1)} %slice.8), channel_id=1, source_target_pairs={{0,32},{32,64},{64,96},{96,128},{128,160},{160,192},{192,224},{1,3... | collective-permute-start | bytes 98312 | tf_op jit(solution)/shard_map/ppermute | solution.py:317
  88.4 4.2 %collective-permute-done.8.prior_coefs_ref = bf16[2,64,128]{2,1,0:T(8,128)(2,1)S(1)} collective-permute-done((bf16[2,64,128]{2,1,0:T(8,128)(2,1)S(1)}, bf16[2,64,128]{2,1,0:T(8,128)(2,1)S(1)}, u32[]{:S(2)}, u32[]{:S(2)}) %collective-permute-start.8) | collective-permute-done | bytes 32800 | tf_op jit(solution)/shard_map/ppermute | solution.py:317
  92.7 0.0 copy-done.1
  92.7 0.0 copy-done.2
  92.7 0.0 copy-done.3
  92.7 10.1 %exposure.1 = (bf16[8,64,4096]{2,1,0:T(8,128)(2,1)}, f32[8,64]{1,0:T(8,128)S(1)}) custom-call(s32[1,64]{1,0:T(1,128)S(1)} %bitcast.24, s32[1,64]{1,0:T(1,128)S(1)} %bitcast.25, s32[1,64]{1,0:T(1,128)S(1)} %bitcast.26, bf16[8,64,128]{2,1,0:T(8,128)(2,1)S(1)} %pad_maximum_fusion.coefs_ref, bf16[2,64,128]{2,1,0:T(8,128)(2,1)S(1)} %collective-permute-done.8.prior_coefs_ref, ...), custom_call_target="tpu_custom_call" | custom-call | flops 536870912 | bytes 12582912 | tf_op jit(solution)/shard_map/exposure/pallas_call | solution.py:248
  102.8 0.0 collective-permute-start.10
  102.8 1.2 collective-permute-done.10
  104.0 0.5 collective-permute-start.11
  104.5 3.1 %collective-permute-done.11 = f32[8,64]{1,0:T(8,128)S(1)} collective-permute-done((f32[8,64]{1,0:T(8,128)S(1)}, f32[8,64]{1,0:T(8,128)S(1)}, u32[]{:S(2)}, u32[]{:S(2)}) %collective-permute-start.11) | collective-permute-done | bytes 2080 | tf_op jit(solution)/shard_map/ppermute | solution.py:299
  107.6 2.0 %collective-permute-start.12 = (f32[8,64]{1,0:T(8,128)S(1)}, f32[8,64]{1,0:T(8,128)S(1)}, u32[]{:S(2)}, u32[]{:S(2)}) collective-permute-start(f32[8,64]{1,0:T(8,128)S(1)} %add.77), channel_id=1, source_target_pairs={{0,4},{1,5},{2,6},{3,7},{4,0},{5,1},{6,2},{7,3},{8,12},{9,13},{10,... | collective-permute-start | bytes 6152 | tf_op jit(solution)/shard_map/ppermute | solution.py:299
  109.6 1.6 %collective-permute-done.12 = f32[8,64]{1,0:T(8,128)S(1)} collective-permute-done((f32[8,64]{1,0:T(8,128)S(1)}, f32[8,64]{1,0:T(8,128)S(1)}, u32[]{:S(2)}, u32[]{:S(2)}) %collective-permute-start.12) | collective-permute-done | bytes 2080 | tf_op jit(solution)/shard_map/ppermute | solution.py:299
  111.2 3.1 %collective-permute-start.13 = (f32[8,64]{1,0:T(8,128)S(1)}, f32[8,64]{1,0:T(8,128)S(1)}, u32[]{:S(2)}, u32[]{:S(2)}) collective-permute-start(f32[8,64]{1,0:T(8,128)S(1)} %add.78), channel_id=1, source_target_pairs={{0,8},{1,9},{2,10},{3,11},{4,12},{5,13},{6,14},{7,15},{8,0},{9,1},... | collective-permute-start | bytes 6152 | tf_op jit(solution)/shard_map/ppermute | solution.py:299
  114.3 1.6 %collective-permute-done.13 = f32[8,64]{1,0:T(8,128)S(1)} collective-permute-done((f32[8,64]{1,0:T(8,128)S(1)}, f32[8,64]{1,0:T(8,128)S(1)}, u32[]{:S(2)}, u32[]{:S(2)}) %collective-permute-start.13) | collective-permute-done | bytes 2080 | tf_op jit(solution)/shard_map/ppermute | solution.py:299
  115.9 3.5 %collective-permute-start.14 = (f32[8,64]{1,0:T(8,128)S(1)}, f32[8,64]{1,0:T(8,128)S(1)}, u32[]{:S(2)}, u32[]{:S(2)}) collective-permute-start(f32[8,64]{1,0:T(8,128)S(1)} %add.79), channel_id=1, source_target_pairs={{0,24},{1,25},{2,26},{3,27},{4,28},{5,29},{6,30},{7,31},{8,16},{9,... | collective-permute-start | bytes 6152 | tf_op jit(solution)/shard_map/ppermute | solution.py:299
  119.4 2.2 %collective-permute-done.14 = f32[8,64]{1,0:T(8,128)S(1)} collective-permute-done((f32[8,64]{1,0:T(8,128)S(1)}, f32[8,64]{1,0:T(8,128)S(1)}, u32[]{:S(2)}, u32[]{:S(2)}) %collective-permute-start.14) | collective-permute-done | bytes 2080 | tf_op jit(solution)/shard_map/ppermute | solution.py:299
  121.6 0.6 add.80
  (18 shorter events, 0.2 us)
Async XLA Ops:
  1.4 1.2 %copy-start = (bf16[8,16,4096]{2,1,0:T(8,128)(2,1)S(1)}, bf16[8,16,4096]{2,1,0:T(8,128)(2,1)}, u32[]{:S(2)}) copy-start(bf16[8,16,4096]{2,1,0:T(8,128)(2,1)} %factors_ref.1) | copy-start | bytes 3145732
  2.7 0.7 copy-start.4
  3.3 2.2 %copy-start.6 = (bf16[8,64,4096]{2,1,0:T(8,128)(2,1)S(1)}, bf16[8,64,4096]{2,1,0:T(8,128)(2,1)}, u32[]{:S(2)}) copy-start(bf16[8,64,4096]{2,1,0:T(8,128)(2,1)} %flows_ref.1) | copy-start | bytes 12582916
  5.5 76.4 %copy-start.5 = (f32[128]{0:T(128)S(1)}, f32[128]{0:T(128)}, u32[]{:S(2)}) copy-start(f32[128]{0:T(128)} %param.10) | copy-start | bytes 1540
  25.0 67.7 %copy-start.1 = (s32[64]{0:T(128)S(1)}, s32[64]{0:T(128)}, u32[]{:S(2)}) copy-start(s32[64]{0:T(128)} %param.11) | copy-start | bytes 772
  25.0 67.7 %copy-start.2 = (s32[64]{0:T(128)S(1)}, s32[64]{0:T(128)}, u32[]{:S(2)}) copy-start(s32[64]{0:T(128)} %param.12) | copy-start | bytes 772
  25.0 67.7 %copy-start.3 = (s32[64]{0:T(128)S(1)}, s32[64]{0:T(128)}, u32[]{:S(2)}) copy-start(s32[64]{0:T(128)} %param.13) | copy-start | bytes 772
  25.0 1.8 %collective-permute-start = (f32[4,192,128]{2,1,0:T(8,128)S(1)}, f32[4,192,128]{2,1,0:T(8,128)S(1)}, u32[]{:S(2)}, u32[]{:S(2)}) collective-permute-start(f32[4,192,128]{2,1,0:T(8,128)S(1)} %dynamic-slice_bitcast_fusion), channel_id=1, source_target_pairs={{0,1},{1,0},{2,3},{3,2},{4,5},{5,4},{6,7},{7,6},{8,9},{9,8},{10,11... | collective-permute-start | bytes 1179656 | tf_op jit(solution)/shard_map/ppermute | solution.py:299
  26.9 7.0 %collective-permute-start.1 = (f32[2,192,128]{2,1,0:T(8,128)S(1)}, f32[2,192,128]{2,1,0:T(8,128)S(1)}, u32[]{:S(2)}, u32[]{:S(2)}) collective-permute-start(f32[2,192,128]{2,1,0:T(8,128)S(1)} %dynamic-slice_bitcast_fusion.1), channel_id=1, source_target_pairs={{0,2},{1,3},{2,0},{3,1},{4,6},{5,7},{6,4},{7,5},{8,10},{9,11},{10,... | collective-permute-start | bytes 589832 | tf_op jit(solution)/shard_map/ppermute | solution.py:299
  34.0 4.7 %collective-permute-start.2 = (f32[192,128]{1,0:T(8,128)S(1)}, f32[192,128]{1,0:T(8,128)S(1)}, u32[]{:S(2)}, u32[]{:S(2)}) collective-permute-start(f32[192,128]{1,0:T(8,128)S(1)} %dynamic-slice_bitcast_fusion.2), channel_id=1, source_target_pairs={{0,4},{1,5},{2,6},{3,7},{4,0},{5,1},{6,2},{7,3},{8,12},{9,13},{10,... | collective-permute-start | bytes 294920 | tf_op jit(solution)/shard_map/ppermute | solution.py:299
  38.7 5.9 %collective-permute-start.3 = (f32[192,128]{1,0:T(8,128)S(1)}, f32[192,128]{1,0:T(8,128)S(1)}, u32[]{:S(2)}, u32[]{:S(2)}) collective-permute-start(f32[192,128]{1,0:T(8,128)S(1)} %bitcast_add_fusion.2), channel_id=1, source_target_pairs={{0,8},{1,9},{2,10},{3,11},{4,12},{5,13},{6,14},{7,15},{8,0},{9,1},... | collective-permute-start | bytes 294920 | tf_op jit(solution)/shard_map/ppermute | solution.py:299
  44.6 8.8 %collective-permute-start.4 = (f32[192,128]{1,0:T(8,128)S(1)}, f32[192,128]{1,0:T(8,128)S(1)}, u32[]{:S(2)}, u32[]{:S(2)}) collective-permute-start(f32[192,128]{1,0:T(8,128)S(1)} %add.75.one_ref), channel_id=1, source_target_pairs={{0,24},{1,25},{2,26},{3,27},{4,28},{5,29},{6,30},{7,31},{8,16},{9,... | collective-permute-start | bytes 294920 | tf_op jit(solution)/shard_map/ppermute | solution.py:299
  64.3 4.3 %collective-permute-start.5 = (bf16[1,64,128]{2,1,0:T(8,128)(2,1)S(1)}, bf16[1,64,128]{2,1,0:T(8,128)(2,1)S(1)}, u32[]{:S(2)}, u32[]{:S(2)}) collective-permute-start(bf16[1,64,128]{2,1,0:T(8,128)(2,1)S(1)} %bitcast.23), channel_id=1, source_target_pairs={{0,4},{1,5},{2,6},{3,7},{4,0},{5,1},{6,2},{7,3},{8,12},{9,13},{10,... | collective-permute-start | bytes 49160 | tf_op jit(solution)/shard_map/ppermute | solution.py:299
  68.6 7.5 %collective-permute-start.6 = (bf16[2,64,128]{2,1,0:T(8,128)(2,1)S(1)}, bf16[2,64,128]{2,1,0:T(8,128)(2,1)S(1)}, u32[]{:S(2)}, u32[]{:S(2)}) collective-permute-start(bf16[2,64,128]{2,1,0:T(8,128)(2,1)S(1)} %pad_maximum_fusion.2), channel_id=1, source_target_pairs={{0,2},{1,3},{2,0},{3,1},{4,6},{5,7},{6,4},{7,5},{8,10},{9,11},{10,... | collective-permute-start | bytes 98312 | tf_op jit(solution)/shard_map/ppermute | solution.py:299
  71.3 10.7 %collective-permute-start.9 = (bf16[2,16,4096]{2,1,0:T(8,128)(2,1)S(1)}, bf16[2,16,4096]{2,1,0:T(8,128)(2,1)S(1)}, u32[]{:S(2)}, u32[]{:S(2)}) collective-permute-start(bf16[2,16,4096]{2,1,0:T(8,128)(2,1)S(1)} %slice.7), channel_id=1, source_target_pairs={{0,32},{32,64},{64,96},{96,128},{128,160},{160,192},{192,224},{1,3... | collective-permute-start | bytes 786440 | tf_op jit(solution)/shard_map/ppermute | solution.py:317
  76.1 8.3 %collective-permute-start.7 = (bf16[4,64,128]{2,1,0:T(8,128)(2,1)S(1)}, bf16[4,64,128]{2,1,0:T(8,128)(2,1)S(1)}, u32[]{:S(2)}, u32[]{:S(2)}) collective-permute-start(bf16[4,64,128]{2,1,0:T(8,128)(2,1)S(1)} %pad_maximum_fusion.1), channel_id=1, source_target_pairs={{0,1},{1,0},{2,3},{3,2},{4,5},{5,4},{6,7},{7,6},{8,9},{9,8},{10,11... | collective-permute-start | bytes 196616 | tf_op jit(solution)/shard_map/ppermute | solution.py:299
  84.5 8.2 %collective-permute-start.8 = (bf16[2,64,128]{2,1,0:T(8,128)(2,1)S(1)}, bf16[2,64,128]{2,1,0:T(8,128)(2,1)S(1)}, u32[]{:S(2)}, u32[]{:S(2)}) collective-permute-start(bf16[2,64,128]{2,1,0:T(8,128)(2,1)S(1)} %slice.8), channel_id=1, source_target_pairs={{0,32},{32,64},{64,96},{96,128},{128,160},{160,192},{192,224},{1,3... | collective-permute-start | bytes 98312 | tf_op jit(solution)/shard_map/ppermute | solution.py:317
  102.8 1.2 collective-permute-start.10
  104.0 3.6 %collective-permute-start.11 = (f32[8,64]{1,0:T(8,128)S(1)}, f32[8,64]{1,0:T(8,128)S(1)}, u32[]{:S(2)}, u32[]{:S(2)}) collective-permute-start(f32[8,64]{1,0:T(8,128)S(1)} %add.76), channel_id=1, source_target_pairs={{0,2},{1,3},{2,0},{3,1},{4,6},{5,7},{6,4},{7,5},{8,10},{9,11},{10,... | collective-permute-start | bytes 6152 | tf_op jit(solution)/shard_map/ppermute | solution.py:299
  107.6 3.6 %collective-permute-start.12 = (f32[8,64]{1,0:T(8,128)S(1)}, f32[8,64]{1,0:T(8,128)S(1)}, u32[]{:S(2)}, u32[]{:S(2)}) collective-permute-start(f32[8,64]{1,0:T(8,128)S(1)} %add.77), channel_id=1, source_target_pairs={{0,4},{1,5},{2,6},{3,7},{4,0},{5,1},{6,2},{7,3},{8,12},{9,13},{10,... | collective-permute-start | bytes 6152 | tf_op jit(solution)/shard_map/ppermute | solution.py:299
  111.2 4.7 %collective-permute-start.13 = (f32[8,64]{1,0:T(8,128)S(1)}, f32[8,64]{1,0:T(8,128)S(1)}, u32[]{:S(2)}, u32[]{:S(2)}) collective-permute-start(f32[8,64]{1,0:T(8,128)S(1)} %add.78), channel_id=1, source_target_pairs={{0,8},{1,9},{2,10},{3,11},{4,12},{5,13},{6,14},{7,15},{8,0},{9,1},... | collective-permute-start | bytes 6152 | tf_op jit(solution)/shard_map/ppermute | solution.py:299
  115.9 5.7 %collective-permute-start.14 = (f32[8,64]{1,0:T(8,128)S(1)}, f32[8,64]{1,0:T(8,128)S(1)}, u32[]{:S(2)}, u32[]{:S(2)}) collective-permute-start(f32[8,64]{1,0:T(8,128)S(1)} %add.79), channel_id=1, source_target_pairs={{0,24},{1,25},{2,26},{3,27},{4,28},{5,29},{6,30},{7,31},{8,16},{9,... | collective-permute-start | bytes 6152 | tf_op jit(solution)/shard_map/ppermute | solution.py:299

commit v2 on v1

v2 whole, which is shorter than its diff:
```python
import functools

import jax
import jax.numpy as jnp
from jax import lax
from jax.experimental import pallas as pl
from jax.experimental.pallas import tpu as pltpu
from jax.sharding import PartitionSpec as P

LAG_MAX = 2
ridge_weight = 0.05
COS_TERMS = (
    1.4142124652862549,
    -27.915136337280273,
    91.82308197021484,
    -120.5933837890625,
    83.14732360839844,
    -29.807071685791016,
)
ROUNDER = 12582912.0
INV_TWO_PI = 0.15915494309189535
CHUNK = 512


def three_parts(x):
    hi = x.astype(jnp.bfloat16)
    rest = x - hi.astype(jnp.float32)
    mid = rest.astype(jnp.bfloat16)
    low = (rest - mid.astype(jnp.float32)).astype(jnp.bfloat16)
    return hi, mid, low


def turn_weights(freq_ref, phase_ref):
    r, k = freq_ref.shape
    rows = three_parts(freq_ref[...].astype(jnp.float32) * INV_TWO_PI)
    phase = three_parts(phase_ref[...] * INV_TWO_PI)
    rows = [part.astype(jnp.float32) for part in rows + phase]
    rest = jnp.zeros((r - len(phase), k), jnp.float32)
    return jnp.concatenate([*rows, rest], axis=0).T.astype(jnp.bfloat16)


def chunk_turns(weights, x):
    ones = jnp.ones(x.shape, jnp.bfloat16)
    return jnp.dot(
        weights, jnp.concatenate([x, x, x, ones], axis=0), preferred_element_type=jnp.float32
    )


def cosines(turns):
    part = turns - ((turns + ROUNDER) - ROUNDER)
    s = part * part
    total = jnp.full(s.shape, COS_TERMS[-1], jnp.float32)
    for term in COS_TERMS[-2::-1]:
        total = total * s + term
    return total.astype(jnp.bfloat16)


def features_kernel(freq_ref, phase_ref, factors_ref, features_ref, weights_ref):
    @pl.when(pl.program_id(0) == 0)
    def _():
        weights_ref[...] = turn_weights(freq_ref, phase_ref)

    for at in range(0, factors_ref.shape[2], CHUNK):
        span = pl.ds(at, CHUNK)
        features_ref[0, :, span] = cosines(chunk_turns(weights_ref[...], factors_ref[0, :, span]))


def sums_kernel(freq_ref, phase_ref, factors_ref, flows_ref, features_ref, sums_ref, weights_ref):
    @pl.when(pl.program_id(0) == 0)
    def _():
        weights_ref[...] = turn_weights(freq_ref, phase_ref)

    spans = [pl.ds(at, CHUNK) for at in range(0, factors_ref.shape[2], CHUNK)]
    weights = weights_ref[...]

    def turns_of(i):
        return chunk_turns(weights, factors_ref[0, :, spans[i]])

    def add_products(sums, i, feats):
        both = jnp.concatenate([feats, flows_ref[0, :, spans[i]]], axis=0)
        product = lax.dot_general(
            both, feats, (((1,), (1,)), ((), ())), preferred_element_type=jnp.float32
        )
        return product if sums is None else sums + product

    sums, before = None, None
    turns = turns_of(0)
    for i, span in enumerate(spans):
        later = turns_of(i + 1) if i + 1 < len(spans) else None
        if i:
            sums = add_products(sums, i - 1, before)
        before = cosines(turns)
        features_ref[0, :, span] = before
        turns = later
    sums_ref[0] = add_products(sums, len(spans) - 1, before)


def whole(a):
    return pl.BlockSpec(a.shape, lambda t: (0,) * a.ndim)


def per_date(a):
    return pl.BlockSpec((1, *a.shape[1:]), lambda t: (t,) + (0,) * (a.ndim - 1))


def in_hbm(a):
    return pltpu.with_memory_space_constraint(a, pltpu.HBM)


def params(limit=48 << 20):
    return pltpu.CompilerParams(vmem_limit_bytes=limit)


def features_of(frequency, phases, factors):
    dates, r, paths = factors.shape
    k = frequency.shape[1]
    out = jax.ShapeDtypeStruct((dates, k, paths), jnp.bfloat16)
    return pl.pallas_call(
        features_kernel,
        grid=(dates,),
        in_specs=[whole(frequency), whole(phases), per_date(factors)],
        out_specs=per_date(out),
        out_shape=out,
        scratch_shapes=[pltpu.VMEM((k, 4 * r), jnp.bfloat16)],
        compiler_params=params(),
        cost_estimate=pl.CostEstimate(
            flops=16 * dates * k * paths, bytes_accessed=2 * dates * k * paths, transcendentals=0
        ),
        name="features",
    )(frequency, phases, factors)


def sums_of(frequency, phases, factors, flows):
    dates, r, paths = factors.shape
    k, sets = frequency.shape[1], flows.shape[1]
    outs = (
        jax.ShapeDtypeStruct((dates, k, paths), jnp.bfloat16),
        jax.ShapeDtypeStruct((dates, k + sets, k), jnp.float32),
    )
    return pl.pallas_call(
        sums_kernel,
        grid=(dates,),
        in_specs=[whole(frequency), whole(phases), per_date(factors), per_date(flows)],
        out_specs=tuple(per_date(o) for o in outs),
        out_shape=outs,
        scratch_shapes=[pltpu.VMEM((k, 4 * r), jnp.bfloat16)],
        compiler_params=params(),
        cost_estimate=pl.CostEstimate(
            flops=400 * dates * k * paths, bytes_accessed=4 * dates * k * paths, transcendentals=0
        ),
        name="sums",
    )(frequency, phases, factors, flows)


def solve_kernel(paths_all, one_ref, two_ref, out_ref):
    k = one_ref.shape[1]
    total = (one_ref[...] + two_ref[...]) / paths_all
    row_at = lax.broadcasted_iota(jnp.int32, (k, k), 0)
    lane_at = lax.broadcasted_iota(jnp.int32, (k, k), 1)
    system = total[:k] + jnp.where(row_at == lane_at, ridge_weight, 0.0)
    m = jnp.concatenate([system, total[k:]], axis=0)
    lane = lax.broadcasted_iota(jnp.int32, (1, k), 1)
    for j in range(k):
        top = j // 8 * 8
        row = m[j - (k + 64 - m.shape[0]) : j - (k + 64 - m.shape[0]) + 1, :]
        pivot = 1.0 / row[:, j : j + 1]
        scaled = jnp.where(lane == j, 1.0 - pivot, row * pivot)
        if (j + 1) % 8 == 0:
            m = m[8:, :]
        m = m - m[:, j : j + 1] * scaled
    out_ref[...] = m.astype(jnp.bfloat16)


def solved(one, two, paths_all):
    k = one.shape[1]
    sets = one.shape[0] - k
    return pl.pallas_call(
        functools.partial(solve_kernel, paths_all),
        out_shape=jax.ShapeDtypeStruct((sets, k), jnp.bfloat16),
        compiler_params=params(),
        name="solve",
    )(one, two)


def value_of(coefs, feats):
    return jnp.dot(coefs, feats, preferred_element_type=jnp.float32).astype(jnp.bfloat16)


def limits_of(lag_ref, threshold_ref, transfer_ref):
    def column(ref):
        return jnp.broadcast_to(ref[...], (128, ref.shape[1])).T

    offset = (column(threshold_ref) + column(transfer_ref)).astype(jnp.float32) / 100.0
    recent = jnp.where(column(lag_ref) == 1, 1.0, 0.0)
    times = CHUNK // 128
    return jnp.concatenate([offset] * times, axis=1), jnp.concatenate([recent] * times, axis=1) > 0.5


def exposed_of(v, last, before, offset, recent):
    lagged = jnp.where(recent, last.astype(jnp.float32), before.astype(jnp.float32))
    collateral = jnp.maximum(lagged - offset, 0.0)
    return jnp.maximum(v.astype(jnp.float32) - collateral, 0.0)


def by_lane(exposed):
    return sum(exposed[:, i : i + 128] for i in range(0, exposed.shape[1], 128))


def later_kernel(
    paths_all,
    lag_ref,
    threshold_ref,
    transfer_ref,
    coefs_ref,
    features_ref,
    exposure_ref,
    profile_ref,
    old_ref,
    sums_ref,
):
    t = pl.program_id(0)
    sets, paths = exposure_ref.shape[1:]
    slots = LAG_MAX + 1
    now, last, before = lax.rem(t, slots), lax.rem(t + LAG_MAX, slots), lax.rem(t + 1, slots)

    @pl.when(t == 0)
    def _():
        sums_ref[...] = jnp.zeros(sums_ref.shape, jnp.float32)

    @pl.when(t < LAG_MAX)
    def _():
        for at in range(0, paths, CHUNK):
            span = pl.ds(at, CHUNK)
            old_ref[now, :, span] = value_of(coefs_ref[0], features_ref[0, :, span])

    @pl.when(t >= LAG_MAX)
    def _():
        offset, recent = limits_of(lag_ref, threshold_ref, transfer_ref)
        total = jnp.zeros((sets, 128), jnp.float32)
        for at in range(0, paths, CHUNK):
            span = pl.ds(at, CHUNK)
            v = value_of(coefs_ref[0], features_ref[0, :, span])
            exposed = exposed_of(v, old_ref[last, :, span], old_ref[before, :, span], offset, recent)
            old_ref[now, :, span] = v
            exposure_ref[0, :, span] = exposed.astype(jnp.bfloat16)
            total += by_lane(exposed)
        here = jnp.sum(total, axis=1, keepdims=True) / paths_all
        lane = lax.broadcasted_iota(jnp.int32, (sets, 128), 1)
        sums_ref[...] = jnp.where(lane == t, here, sums_ref[...])

    @pl.when(t == pl.num_programs(0) - 1)
    def _():
        profile_ref[...] = sums_ref[...].T[: profile_ref.shape[0]]


def first_kernel(
    paths_all,
    lag_ref,
    threshold_ref,
    transfer_ref,
    coefs_ref,
    prior_coefs_ref,
    features_ref,
    prior_features_ref,
    profile_in_ref,
    exposure_in_ref,
    exposure_ref,
    profile_ref,
):
    del exposure_in_ref
    sets, paths = exposure_ref.shape[1:]
    offset, recent = limits_of(lag_ref, threshold_ref, transfer_ref)
    totals = [jnp.zeros((sets, 128), jnp.float32)] * LAG_MAX
    for at in range(0, paths, CHUNK):
        span = pl.ds(at, CHUNK)
        v = [value_of(prior_coefs_ref[i], prior_features_ref[i, :, span]) for i in range(LAG_MAX)]
        for t in range(LAG_MAX):
            v.append(value_of(coefs_ref[t], features_ref[t, :, span]))
            exposed = exposed_of(v[-1], v[-2], v[-3], offset, recent)
            exposure_ref[t, :, span] = exposed.astype(jnp.bfloat16)
            totals[t] = totals[t] + by_lane(exposed)
    lane = lax.broadcasted_iota(jnp.int32, (sets, 128), 1)
    sums = jnp.zeros((sets, 128), jnp.float32)
    for t, total in enumerate(totals):
        here = jnp.sum(total, axis=1, keepdims=True) / paths_all
        sums = jnp.where(lane == t, here, sums)
    profile_ref[...] = profile_in_ref[...] + sums.T[: profile_ref.shape[0]]


def later_exposures(limits, coefs, features, paths_all):
    dates, k, paths = features.shape
    sets = coefs.shape[1]
    outs = (
        jax.ShapeDtypeStruct((dates, sets, paths), jnp.bfloat16),
        jax.ShapeDtypeStruct((dates, sets), jnp.float32),
    )
    return pl.pallas_call(
        functools.partial(later_kernel, paths_all),
        grid=(dates,),
        in_specs=[*(whole(a) for a in limits), per_date(coefs), per_date(features)],
        out_specs=(
            pl.BlockSpec((1, sets, paths), lambda t: (jnp.maximum(t, LAG_MAX), 0, 0)),
            whole(outs[1]),
        ),
        out_shape=outs,
        scratch_shapes=[
            pltpu.VMEM((LAG_MAX + 1, sets, paths), jnp.bfloat16),
            pltpu.VMEM((sets, 128), jnp.float32),
        ],
        compiler_params=params(),
        cost_estimate=pl.CostEstimate(
            flops=2 * dates * k * sets * paths,
            bytes_accessed=2 * dates * (k + sets) * paths,
            transcendentals=0,
        ),
        name="later",
    )(*limits, coefs, features)


def first_exposures(
    limits, coefs, prior_coefs, features, prior_features, profile, exposure, paths_all
):
    dates, sets, paths = exposure.shape
    args = (*limits, coefs, prior_coefs, features, prior_features, profile, exposure)

    def leading(a):
        return pl.BlockSpec((LAG_MAX, *a.shape[1:]), lambda t: (0,) * a.ndim)

    return pl.pallas_call(
        functools.partial(first_kernel, paths_all),
        grid=(1,),
        in_specs=[
            *(whole(a) for a in limits),
            leading(coefs),
            leading(prior_coefs),
            leading(features),
            leading(prior_features),
            whole(profile),
            pl.BlockSpec(memory_space=pl.ANY),
        ],
        out_specs=(leading(exposure), whole(profile)),
        out_shape=(
            jax.ShapeDtypeStruct(exposure.shape, exposure.dtype),
            jax.ShapeDtypeStruct(profile.shape, profile.dtype),
        ),
        input_output_aliases={len(args) - 1: 0},
        compiler_params=params(),
        name="first",
    )(*args)


CORE, ROW, NEAR, NEXT, FAR = 1, 2, 4, 8, 24


def swapped(value, step):
    length = lax.axis_size("path")
    return lax.ppermute(value, "path", [(i, i ^ step) for i in range(1, length, 2)])


def to_odd(value):
    return lax.ppermute(value, "path", [(i, i + 1) for i in range(0, lax.axis_size("path"), 2)])


def to_even(value):
    return lax.ppermute(value, "path", [(i + 1, i) for i in range(0, lax.axis_size("path"), 2)])


def halved(value, step, bit):
    value = value.reshape(2, value.shape[0] // 2, *value.shape[1:])
    other = lax.dynamic_index_in_dim(value, 1 - bit, 0, keepdims=False)
    mine = lax.dynamic_index_in_dim(value, bit, 0, keepdims=False)
    return mine + swapped(other, step)


def doubled(value, step, bit):
    other = swapped(value, step)
    low = jnp.where(bit == 0, value, other)
    high = jnp.where(bit == 0, other, value)
    return jnp.concatenate([low, high], axis=0)


def from_earlier(value):
    length = lax.axis_size("date")
    return lax.ppermute(value, "date", [(i, i + 1) for i in range(length - 1)])


def local(factors, cashflows, frequency, phases, margin_lag, thresholds, transfer_min):
    paths_all = factors.shape[2] * lax.axis_size("path")
    me = lax.axis_index("path")
    odd, row, near = me & 1, (me >> 1) & 1, (me >> 2) & 1
    following = ((me >> 3) ^ (me >> 4)) & 1
    prior_factors = from_earlier(factors[-LAG_MAX:])
    phases = phases.reshape(1, -1)
    frequency = frequency.T
    features, sums = sums_of(frequency, phases, in_hbm(factors), in_hbm(cashflows))
    kept = sums + to_odd(sums)
    kept = halved(kept, ROW, row)
    prior_features = features_of(frequency, phases, prior_factors)
    kept, prior_features = lax.optimization_barrier((kept, prior_features))
    kept = halved(kept, NEAR, near)
    kept = halved(kept, NEXT, following)[0]
    coefs = solved(kept, swapped(kept, FAR), paths_all)
    coefs = doubled(coefs[None], NEXT, following)
    coefs = doubled(coefs, NEAR, near)
    coefs = doubled(coefs, ROW, row)
    coefs = jnp.where(odd == 1, coefs, to_even(coefs))
    prior_coefs = from_earlier(coefs[-LAG_MAX:])
    limits = tuple(a.reshape(1, -1) for a in (margin_lag, thresholds, transfer_min))
    exposure, profile = later_exposures(limits, coefs, features, paths_all)
    exposure, profile = first_exposures(
        limits, coefs, prior_coefs, features, prior_features, profile, exposure, paths_all
    )
    profile = profile + to_odd(profile)
    for step in (ROW, NEAR, NEXT, FAR):
        profile = profile + swapped(profile, step)
    return exposure, jnp.where(odd == 1, profile, to_even(profile))


def solution(mesh):
    return jax.shard_map(
        local,
        mesh=mesh,
        in_specs=(P("date", None, "path"), P("date", None, "path"), P(), P(), P(), P(), P()),
        out_specs=(P("date", None, "path"), P("date", None)),
        check_vma=False,
    )
```

time: 123 us -> 137 us (1.11)
  waiting for transfers between devices: 36.2 us -> 64.8 us
  starting transfers between devices: 35.5 us -> 23.4 us
  local copies, waits for them, and re-layouts: 5.92 us -> 3.15 us
  Pallas kernels: 42.9 us -> 40.9 us
    ppermute x13 -> x15, waiting for transfers between devices: 26.4 us -> 57.5 us  [the longest x2 54.8 us: to_even(): lax.ppermute(value, 'path', [(i + 1, i) for i in range(0, lax.axis_size('...]
    ppermute x13 -> x15, starting transfers between devices: 26.8 us -> 14.2 us  [the longest x11 8.1 us: swapped(): lax.ppermute(value, 'path', [(i, i ^ step) for i in range(1, length, 2)])]
    pallas_call x1, Pallas kernels: 19.4 us -> 14.6 us  [sums_of(): pl.pallas_call(sums_kernel, grid=(dates,), in_specs=[whole(frequency), wh...]
    unnamed x15 -> x14, local copies, waits for them, and re-layouts: 4.88 us -> 1.36 us
    pallas_call x1 -> x2, Pallas kernels: 10.1 us -> 13 us  [the longest x1 9.17 us: later_exposures(): pl.pallas_call(functools.partial(later_kernel, paths_all), grid=(dates,),...]
    ppermute x2, waiting for transfers between devices: 9.75 us -> 7.32 us  [from_earlier(): return lax.ppermute(value, 'date', [(i, i + 1) for i in range(length - 1)])]
  transfers between devices with their start and end apart: 15 -> 17, of which waited for: 13 -> 5; matrix products, arithmetic and copies ran while one was open for 1% -> 1% of each run, Pallas kernels for 2% -> 9%
where the time goes in v2:
time: 137 us; the launch traced here: 135 us
  waiting for transfers between devices  64.8 us (47%)
  Pallas kernels  40.9 us (30%)
  starting transfers between devices  23.4 us (17%)
  local copies, waits for them, and re-layouts  3.15 us (2%)
  other arithmetic  1.87 us (1%)
    ppermute x2, waiting for transfers between devices, to_even(): lax.ppermute(value, 'path', [(i + 1, i) for i in range(0, lax.axis_size('...  54.8 us
    pallas_call x1, Pallas kernels, sums_of(): pl.pallas_call(sums_kernel, grid=(dates,), in_specs=[whole(frequency), wh...  14.6 us
    pallas_call x1, Pallas kernels, solved(): pl.pallas_call(functools.partial(solve_kernel, paths_all), out_shape=jax....  10.9 us
    ppermute x2, starting transfers between devices, from_earlier(): return lax.ppermute(value, 'date', [(i, i + 1) for i in range(length - 1)])  9.17 us
    pallas_call x1, Pallas kernels, later_exposures(): pl.pallas_call(functools.partial(later_kernel, paths_all), grid=(dates,),...  9.17 us
    ppermute x11, starting transfers between devices, swapped(): lax.ppermute(value, 'path', [(i, i ^ step) for i in range(1, length, 2)])  8.1 us
    ppermute x2, waiting for transfers between devices, from_earlier(): return lax.ppermute(value, 'date', [(i, i + 1) for i in range(length - 1)])  7.32 us
    pallas_call x1, Pallas kernels, first_exposures(): pl.pallas_call(functools.partial(first_kernel, paths_all), grid=(1,), in_...  3.79 us
  transfers between devices with their start and end apart: 17, of which 5 were waited for; matrix products, arithmetic and copies ran while one was open for 1% of the time, Pallas kernels for 9%

profile of v2, /device:TPU:2, one launch (start us, length us, event | category | flops | bytes accessed | tf_op | source)
XLA Modules:
  0.0 135.2 jit_solution(11298727587768426632)
XLA Ops:
  0.6 0.0 copy-start
  0.6 0.7 copy-done
  1.3 0.0 copy-start.5
  1.3 0.7 copy-done.5
  2.0 0.0 copy-start.1
  2.0 0.0 copy-start.6
  2.0 14.6 %sums.1 = (bf16[8,128,4096]{2,1,0:T(8,128)(2,1)}, f32[8,192,128]{2,1,0:T(8,128)S(1)}) custom-call(bf16[16,128]{1,0:T(8,128)(2,1)S(1)} %bitcast.21, f32[1,128]{1,0:T(1,128)S(1)} %bitcast.29, bf16[8,16,4096]{2,1,0:T(8,128)(2,1)} %factors_ref.1, bf16[8,64,4096]{2,1,0:T(8,128)(2,1)} %flows_ref.1), custom_call_target="tpu_custom_call" | custom-call | flops 1677721600 | bytes 16777216 | tf_op jit(solution)/shard_map/sums/pallas_call | solution.py:140
  16.6 1.8 %collective-permute-start = (f32[8,192,128]{2,1,0:T(8,128)S(1)}, f32[8,192,128]{2,1,0:T(8,128)S(1)}, u32[]{:S(2)}, u32[]{:S(2)}) collective-permute-start(f32[8,192,128]{2,1,0:T(8,128)S(1)} %get-tuple-element.10), channel_id=1, source_target_pairs={{0,1},{2,3},{4,5},{6,7},{8,9},{10,11},{12,13},{14,15},{16,17},{18,... | collective-permute-start | bytes 2359304 | tf_op jit(solution)/shard_map/ppermute | solution.py:361
  18.4 1.8 %collective-permute-done = f32[8,192,128]{2,1,0:T(8,128)S(1)} collective-permute-done((f32[8,192,128]{2,1,0:T(8,128)S(1)}, f32[8,192,128]{2,1,0:T(8,128)S(1)}, u32[]{:S(2)}, u32[]{:S(2)}) %collective-permute-start) | collective-permute-done | bytes 786464 | tf_op jit(solution)/shard_map/ppermute | solution.py:361
  20.2 0.1 add.51
  20.3 0.0 copy-start.2
  20.3 0.0 copy-start.3
  20.4 0.0 copy-start.4
  20.4 0.8 dynamic-slice_bitcast_fusion
  21.2 1.5 %collective-permute-start.1 = (f32[4,192,128]{2,1,0:T(8,128)}, f32[4,192,128]{2,1,0:T(8,128)}, u32[]{:S(2)}, u32[]{:S(2)}) collective-permute-start(f32[4,192,128]{2,1,0:T(8,128)} %dynamic-slice_bitcast_fusion), channel_id=1, source_target_pairs={{1,3},{3,1},{5,7},{7,5},{9,11},{11,9},{13,15},{15,13},{17,19},{19,... | collective-permute-start | bytes 1179656 | tf_op jit(solution)/shard_map/ppermute | solution.py:357
  22.6 1.0 slice.6
  23.6 5.1 %collective-permute-start.2 = (bf16[2,16,4096]{2,1,0:T(8,128)(2,1)S(1)}, bf16[2,16,4096]{2,1,0:T(8,128)(2,1)S(1)}, u32[]{:S(2)}, u32[]{:S(2)}) collective-permute-start(bf16[2,16,4096]{2,1,0:T(8,128)(2,1)S(1)} %slice.6), channel_id=1, source_target_pairs={{0,32},{32,64},{64,96},{96,128},{128,160},{160,192},{192,224},{1,3... | collective-permute-start | bytes 786440 | tf_op jit(solution)/shard_map/ppermute | solution.py:384
  28.7 7.3 %collective-permute-done.2.factors_ref = bf16[2,16,4096]{2,1,0:T(8,128)(2,1)S(1)} collective-permute-done((bf16[2,16,4096]{2,1,0:T(8,128)(2,1)S(1)}, bf16[2,16,4096]{2,1,0:T(8,128)(2,1)S(1)}, u32[]{:S(2)}, u32[]{:S(2)}) %collective-permute-start.2) | collective-permute-done | bytes 262176 | tf_op jit(solution)/shard_map/ppermute | solution.py:384
  36.0 0.0 copy-done.1
  36.0 0.0 copy-done.6
  36.0 2.4 %features.1.prior_features_ref = bf16[2,128,4096]{2,1,0:T(8,128)(2,1)S(1)} custom-call(bf16[16,128]{1,0:T(8,128)(2,1)S(1)} %bitcast.22, f32[1,128]{1,0:T(1,128)S(1)} %bitcast.30, bf16[2,16,4096]{2,1,0:T(8,128)(2,1)S(1)} %collective-permute-done.2.factors_ref), custom_call_target="tpu_custom_call" | custom-call | flops 16777216 | bytes 2097152 | tf_op jit(solution)/shard_map/features/pallas_call | solution.py:118
  38.5 0.0 collective-permute-done.1
  38.5 1.0 bitcast_add_fusion
  39.5 0.7 collective-permute-start.3
  40.2 0.0 collective-permute-done.3
  40.3 0.7 collective-permute-start.4
  41.0 0.0 collective-permute-done.4
  41.0 0.7 collective-permute-start.5
  41.7 0.0 collective-permute-done.5.two_ref
  41.7 10.9 %solve.1 = bf16[64,128]{1,0:T(8,128)(2,1)S(1)} custom-call(f32[192,128]{1,0:T(8,128)S(1)} %add_bitcast_fusion.one_ref, f32[192,128]{1,0:T(8,128)S(1)} %collective-permute-done.5.two_ref), custom_call_target="tpu_custom_call" | custom-call | tf_op jit(solution)/shard_map/solve/pallas_call | solution.py:177
  52.6 0.7 collective-permute-start.6
  53.3 0.0 collective-permute-done.6
  53.3 0.7 collective-permute-start.7
  54.0 0.0 collective-permute-done.7
  54.1 0.7 collective-permute-start.8
  54.7 0.0 collective-permute-done.8
  54.8 1.3 collective-permute-start.9
  56.1 36.2 %collective-permute-done.9 = bf16[8,64,128]{2,1,0:T(8,128)(2,1)S(1)} collective-permute-done((bf16[8,64,128]{2,1,0:T(8,128)(2,1)S(1)}, bf16[8,64,128]{2,1,0:T(8,128)(2,1)S(1)}, u32[]{:S(2)}, u32[]{:S(2)}) %collective-permute-start.9) | collective-permute-done | bytes 131104 | tf_op jit(solution)/shard_map/ppermute | solution.py:365
  92.3 4.1 %collective-permute-start.10 = (bf16[2,64,128]{2,1,0:T(8,128)(2,1)S(1)}, bf16[2,64,128]{2,1,0:T(8,128)(2,1)S(1)}, u32[]{:S(2)}, u32[]{:S(2)}) collective-permute-start(bf16[2,64,128]{2,1,0:T(8,128)(2,1)S(1)} %slice.8), channel_id=1, source_target_pairs={{0,32},{32,64},{64,96},{96,128},{128,160},{160,192},{192,224},{1,3... | collective-permute-start | bytes 98312 | tf_op jit(solution)/shard_map/ppermute | solution.py:384
  96.4 0.0 copy-done.2
  96.4 0.0 copy-done.3
  96.4 0.0 copy-done.4
  96.4 9.2 %later.1 = (bf16[8,64,4096]{2,1,0:T(8,128)(2,1)}, f32[8,64]{1,0:T(8,128)S(1)}) custom-call(s32[1,64]{1,0:T(1,128)S(1)} %bitcast.23, s32[1,64]{1,0:T(1,128)S(1)} %bitcast.25, s32[1,64]{1,0:T(1,128)S(1)} %bitcast.27, bf16[8,64,128]{2,1,0:T(8,128)(2,1)S(1)} %broadcast_select_fusion.coefs_ref, bf16[8,128,4096]{2,1,0:T(8,128)(2,1)} %get-tuple-element.12.features_ref), custom_call_target="tpu_custom_call" | custom-call | flops 536870912 | bytes 12582912 | tf_op jit(solution)/shard_map/later/pallas_call | solution.py:297
  105.6 0.0 collective-permute-done.10.prior_coefs_ref
  105.6 3.8 %first.1 = (bf16[8,64,4096]{2,1,0:T(8,128)(2,1)}, f32[8,64]{1,0:T(8,128)S(1)}) custom-call(s32[1,64]{1,0:T(1,128)S(1)} %bitcast.24, s32[1,64]{1,0:T(1,128)S(1)} %bitcast.26, s32[1,64]{1,0:T(1,128)S(1)} %bitcast.28, bf16[8,64,128]{2,1,0:T(8,128)(2,1)S(1)} %broadcast_select_fusion.coefs_ref, ...), custom_call_target="tpu_custom_call", output_to_operand_aliasing={{0}: (8, {})} | custom-call | tf_op jit(solution)/shard_map/first/pallas_call | solution.py:329
  109.4 1.8 %collective-permute-start.11 = (f32[8,64]{1,0:T(8,128)S(1)}, f32[8,64]{1,0:T(8,128)S(1)}, u32[]{:S(2)}, u32[]{:S(2)}) collective-permute-start(f32[8,64]{1,0:T(8,128)S(1)} %get-tuple-element.17), channel_id=1, source_target_pairs={{0,1},{2,3},{4,5},{6,7},{8,9},{10,11},{12,13},{14,15},{16,17},{18,... | collective-permute-start | bytes 6152 | tf_op jit(solution)/shard_map/ppermute | solution.py:361
  111.2 0.8 collective-permute-done.11
  112.0 0.6 collective-permute-start.12
  112.7 0.0 collective-permute-done.12
  112.7 0.7 collective-permute-start.13
  113.3 0.0 collective-permute-done.13
  113.4 0.7 collective-permute-start.14
  114.0 0.0 collective-permute-done.14
  114.1 0.7 collective-permute-start.15
  114.7 0.0 collective-permute-done.15
  114.8 1.3 collective-permute-start.16
  116.1 18.6 %collective-permute-done.16 = f32[8,64]{1,0:T(8,128)S(1)} collective-permute-done((f32[8,64]{1,0:T(8,128)S(1)}, f32[8,64]{1,0:T(8,128)S(1)}, u32[]{:S(2)}, u32[]{:S(2)}) %collective-permute-start.16) | collective-permute-done | bytes 2080 | tf_op jit(solution)/shard_map/ppermute | solution.py:365
  134.6 0.6 broadcast_select_fusion.7
  (17 shorter events, 0.2 us)
Async XLA Ops:
  0.6 0.7 copy-start
  1.3 0.7 copy-start.5
  2.0 34.0 %copy-start.1 = (bf16[128,16]{0,1:T(8,128)(2,1)S(1)}, bf16[128,16]{0,1:T(8,128)(2,1)}, u32[]{:S(2)}) copy-start(bf16[128,16]{0,1:T(8,128)(2,1)} %param.9) | copy-start | bytes 12292
  2.0 34.0 %copy-start.6 = (f32[128]{0:T(128)S(1)}, f32[128]{0:T(128)}, u32[]{:S(2)}) copy-start(f32[128]{0:T(128)} %param.10) | copy-start | bytes 1540
  16.6 3.6 %collective-permute-start = (f32[8,192,128]{2,1,0:T(8,128)S(1)}, f32[8,192,128]{2,1,0:T(8,128)S(1)}, u32[]{:S(2)}, u32[]{:S(2)}) collective-permute-start(f32[8,192,128]{2,1,0:T(8,128)S(1)} %get-tuple-element.10), channel_id=1, source_target_pairs={{0,1},{2,3},{4,5},{6,7},{8,9},{10,11},{12,13},{14,15},{16,17},{18,... | collective-permute-start | bytes 2359304 | tf_op jit(solution)/shard_map/ppermute | solution.py:361
  20.3 76.1 %copy-start.2 = (s32[64]{0:T(128)S(1)}, s32[64]{0:T(128)}, u32[]{:S(2)}) copy-start(s32[64]{0:T(128)} %param.11) | copy-start | bytes 772
  20.3 76.1 %copy-start.3 = (s32[64]{0:T(128)S(1)}, s32[64]{0:T(128)}, u32[]{:S(2)}) copy-start(s32[64]{0:T(128)} %param.12) | copy-start | bytes 772
  20.4 76.1 %copy-start.4 = (s32[64]{0:T(128)S(1)}, s32[64]{0:T(128)}, u32[]{:S(2)}) copy-start(s32[64]{0:T(128)} %param.13) | copy-start | bytes 772
  21.2 17.3 %collective-permute-start.1 = (f32[4,192,128]{2,1,0:T(8,128)}, f32[4,192,128]{2,1,0:T(8,128)}, u32[]{:S(2)}, u32[]{:S(2)}) collective-permute-start(f32[4,192,128]{2,1,0:T(8,128)} %dynamic-slice_bitcast_fusion), channel_id=1, source_target_pairs={{1,3},{3,1},{5,7},{7,5},{9,11},{11,9},{13,15},{15,13},{17,19},{19,... | collective-permute-start | bytes 1179656 | tf_op jit(solution)/shard_map/ppermute | solution.py:357
  23.6 12.4 %collective-permute-start.2 = (bf16[2,16,4096]{2,1,0:T(8,128)(2,1)S(1)}, bf16[2,16,4096]{2,1,0:T(8,128)(2,1)S(1)}, u32[]{:S(2)}, u32[]{:S(2)}) collective-permute-start(bf16[2,16,4096]{2,1,0:T(8,128)(2,1)S(1)} %slice.6), channel_id=1, source_target_pairs={{0,32},{32,64},{64,96},{96,128},{128,160},{160,192},{192,224},{1,3... | collective-permute-start | bytes 786440 | tf_op jit(solution)/shard_map/ppermute | solution.py:384
  39.5 0.7 collective-permute-start.3
  40.3 0.7 collective-permute-start.4
  41.0 0.7 collective-permute-start.5
  52.6 0.7 collective-permute-start.6
  53.3 0.7 collective-permute-start.7
  54.1 0.7 collective-permute-start.8
  54.8 37.5 %collective-permute-start.9 = (bf16[8,64,128]{2,1,0:T(8,128)(2,1)S(1)}, bf16[8,64,128]{2,1,0:T(8,128)(2,1)S(1)}, u32[]{:S(2)}, u32[]{:S(2)}) collective-permute-start(bf16[8,64,128]{2,1,0:T(8,128)(2,1)S(1)} %pad_maximum_fusion), channel_id=1, source_target_pairs={{1,0},{3,2},{5,4},{7,6},{9,8},{11,10},{13,12},{15,14},{17,16},{19,... | collective-permute-start | bytes 393224 | tf_op jit(solution)/shard_map/ppermute | solution.py:365
  92.3 13.3 %collective-permute-start.10 = (bf16[2,64,128]{2,1,0:T(8,128)(2,1)S(1)}, bf16[2,64,128]{2,1,0:T(8,128)(2,1)S(1)}, u32[]{:S(2)}, u32[]{:S(2)}) collective-permute-start(bf16[2,64,128]{2,1,0:T(8,128)(2,1)S(1)} %slice.8), channel_id=1, source_target_pairs={{0,32},{32,64},{64,96},{96,128},{128,160},{160,192},{192,224},{1,3... | collective-permute-start | bytes 98312 | tf_op jit(solution)/shard_map/ppermute | solution.py:384
  109.4 2.6 %collective-permute-start.11 = (f32[8,64]{1,0:T(8,128)S(1)}, f32[8,64]{1,0:T(8,128)S(1)}, u32[]{:S(2)}, u32[]{:S(2)}) collective-permute-start(f32[8,64]{1,0:T(8,128)S(1)} %get-tuple-element.17), channel_id=1, source_target_pairs={{0,1},{2,3},{4,5},{6,7},{8,9},{10,11},{12,13},{14,15},{16,17},{18,... | collective-permute-start | bytes 6152 | tf_op jit(solution)/shard_map/ppermute | solution.py:361
  112.0 0.7 collective-permute-start.12
  112.7 0.7 collective-permute-start.13
  113.4 0.7 collective-permute-start.14
  114.1 0.7 collective-permute-start.15
  114.8 19.9 %collective-permute-start.16 = (f32[8,64]{1,0:T(8,128)S(1)}, f32[8,64]{1,0:T(8,128)S(1)}, u32[]{:S(2)}, u32[]{:S(2)}) collective-permute-start(f32[8,64]{1,0:T(8,128)S(1)} %add.65), channel_id=1, source_target_pairs={{1,0},{3,2},{5,4},{7,6},{9,8},{11,10},{13,12},{15,14},{17,16},{19,... | collective-permute-start | bytes 6152 | tf_op jit(solution)/shard_map/ppermute | solution.py:365

commit v3 on v2

v3 whole, which is shorter than its diff:
```python
import functools

import jax
import jax.numpy as jnp
from jax import lax
from jax.experimental import pallas as pl
from jax.experimental.pallas import tpu as pltpu
from jax.sharding import PartitionSpec as P

LAG_MAX = 2
ridge_weight = 0.05
COS_TERMS = (
    1.4142124652862549,
    -27.915136337280273,
    91.82308197021484,
    -120.5933837890625,
    83.14732360839844,
    -29.807071685791016,
)
ROUNDER = 12582912.0
INV_TWO_PI = 0.15915494309189535
CHUNK = 512


def three_parts(x):
    hi = x.astype(jnp.bfloat16)
    rest = x - hi.astype(jnp.float32)
    mid = rest.astype(jnp.bfloat16)
    low = (rest - mid.astype(jnp.float32)).astype(jnp.bfloat16)
    return hi, mid, low


def turn_weights(freq_ref, phase_ref):
    r, k = freq_ref.shape
    rows = three_parts(freq_ref[...].astype(jnp.float32) * INV_TWO_PI)
    phase = three_parts(phase_ref[...] * INV_TWO_PI)
    rows = [part.astype(jnp.float32) for part in rows + phase]
    rest = jnp.zeros((r - len(phase), k), jnp.float32)
    return jnp.concatenate([*rows, rest], axis=0).T.astype(jnp.bfloat16)


def chunk_turns(weights, x):
    ones = jnp.ones(x.shape, jnp.bfloat16)
    return jnp.dot(
        weights, jnp.concatenate([x, x, x, ones], axis=0), preferred_element_type=jnp.float32
    )


def cosines(turns):
    part = turns - ((turns + ROUNDER) - ROUNDER)
    s = part * part
    total = jnp.full(s.shape, COS_TERMS[-1], jnp.float32)
    for term in COS_TERMS[-2::-1]:
        total = total * s + term
    return total.astype(jnp.bfloat16)


def features_kernel(freq_ref, phase_ref, factors_ref, features_ref):
    weights = turn_weights(freq_ref, phase_ref)
    for i in range(factors_ref.shape[0]):
        for at in range(0, factors_ref.shape[2], CHUNK):
            span = pl.ds(at, CHUNK)
            features_ref[i, :, span] = cosines(chunk_turns(weights, factors_ref[i, :, span]))


def sums_kernel(first_ref, freq_ref, phase_ref, factors_ref, flows_ref, *refs):
    (
        features_ref,
        sums_ref,
        freq_here,
        phase_here,
        factors_here,
        flows_here,
        features_here,
        weight_sems,
        factor_sems,
        flow_sems,
        feature_sems,
    ) = refs[-11:]
    dates, _, paths = factors_here.shape
    small = (
        pltpu.make_async_copy(freq_ref, freq_here, weight_sems.at[0]),
        pltpu.make_async_copy(phase_ref, phase_here, weight_sems.at[1]),
    )
    for copy in small:
        copy.start()
    loads, saves = [], []
    for i in range(dates):
        t = first_ref[0] + i
        loads.append(
            (
                pltpu.make_async_copy(factors_ref.at[t], factors_here.at[i], factor_sems.at[i]),
                pltpu.make_async_copy(flows_ref.at[t], flows_here.at[i], flow_sems.at[i]),
            )
        )
        saves.append(
            pltpu.make_async_copy(features_here.at[i], features_ref.at[t], feature_sems.at[i])
        )
        for copy in loads[-1]:
            copy.start()
    for copy in small:
        copy.wait()
    weights = turn_weights(freq_here, phase_here)
    items = [(i, pl.ds(at, CHUNK)) for i in range(dates) for at in range(0, paths, CHUNK)]
    arrived = set()

    def turns_of(item):
        i, span = item
        if i not in arrived:
            arrived.add(i)
            for copy in loads[i]:
                copy.wait()
        return chunk_turns(weights, factors_here[i, :, span])

    def product_of(item, feats):
        i, span = item
        both = jnp.concatenate([feats, flows_here[i, :, span]], axis=0)
        return lax.dot_general(
            both, feats, (((1,), (1,)), ((), ())), preferred_element_type=jnp.float32
        )

    turns, feats, sums = turns_of(items[0]), None, None
    for at in range(len(items) + 1):
        later = turns_of(items[at + 1]) if at + 1 < len(items) else None
        if at:
            i = items[at - 1][0]
            product = product_of(items[at - 1], feats)
            starts = at == 1 or items[at - 2][0] != i
            sums = product if starts else sums + product
            if at == len(items) or items[at][0] != i:
                sums_ref[i] = sums
                saves[i].start()
        if at < len(items):
            i, span = items[at]
            feats = cosines(turns)
            features_here[i, :, span] = feats
            turns = later
    for copy in saves:
        copy.wait()


ON_CHIP = pl.BlockSpec(memory_space=pltpu.VMEM)
SCALARS = pl.BlockSpec(memory_space=pltpu.SMEM)
IN_HBM = pl.BlockSpec(memory_space=pltpu.HBM)


def in_hbm(a):
    return pltpu.with_memory_space_constraint(a, pltpu.HBM)


def params(mebibytes):
    return pltpu.CompilerParams(vmem_limit_bytes=mebibytes << 20)


def features_of(frequency, phases, factors):
    dates, r, paths = factors.shape
    k = frequency.shape[1]
    return pl.pallas_call(
        features_kernel,
        in_specs=[ON_CHIP, ON_CHIP, ON_CHIP],
        out_specs=ON_CHIP,
        out_shape=jax.ShapeDtypeStruct((dates, k, paths), jnp.bfloat16),
        compiler_params=params(8),
        cost_estimate=pl.CostEstimate(
            flops=2000 * dates * k * paths, bytes_accessed=2 * dates * k * paths, transcendentals=0
        ),
        name="features",
    )(frequency, phases, factors)


def sums_of(first, dates, frequency, phases, factors, flows, features=None):
    dates_all, r, paths = factors.shape
    k, sets = frequency.shape[1], flows.shape[1]
    args = [first.reshape(1), *map(in_hbm, (frequency, phases, factors, flows))]
    aliases = {}
    if features is not None:
        aliases[len(args)] = 0
        args.append(in_hbm(features))
    return pl.pallas_call(
        sums_kernel,
        in_specs=[SCALARS] + [IN_HBM] * (len(args) - 1),
        out_specs=(IN_HBM, ON_CHIP),
        out_shape=(
            pltpu.HBM((dates_all, k, paths), jnp.bfloat16),
            jax.ShapeDtypeStruct((dates, k + sets, k), jnp.float32),
        ),
        scratch_shapes=[
            pltpu.VMEM(frequency.shape, frequency.dtype),
            pltpu.VMEM(phases.shape, phases.dtype),
            pltpu.VMEM((dates, r, paths), jnp.bfloat16),
            pltpu.VMEM((dates, sets, paths), jnp.bfloat16),
            pltpu.VMEM((dates, k, paths), jnp.bfloat16),
            pltpu.SemaphoreType.DMA((2,)),
            pltpu.SemaphoreType.DMA((dates,)),
            pltpu.SemaphoreType.DMA((dates,)),
            pltpu.SemaphoreType.DMA((dates,)),
        ],
        input_output_aliases=aliases,
        compiler_params=params(24),
        cost_estimate=pl.CostEstimate(
            flops=20000 * dates * k * paths, bytes_accessed=4 * dates * k * paths, transcendentals=0
        ),
        name="sums",
    )(*args)


def solve_kernel(paths_all, one_ref, two_ref, out_ref):
    k = one_ref.shape[1]
    total = (one_ref[...] + two_ref[...]) / paths_all
    row_at = lax.broadcasted_iota(jnp.int32, (k, k), 0)
    lane_at = lax.broadcasted_iota(jnp.int32, (k, k), 1)
    system = total[:k] + jnp.where(row_at == lane_at, ridge_weight, 0.0)
    m = jnp.concatenate([system, total[k:]], axis=0)
    lane = lax.broadcasted_iota(jnp.int32, (1, k), 1)
    for j in range(k):
        top = j // 8 * 8
        row = m[j - (k + 64 - m.shape[0]) : j - (k + 64 - m.shape[0]) + 1, :]
        pivot = 1.0 / row[:, j : j + 1]
        scaled = jnp.where(lane == j, 1.0 - pivot, row * pivot)
        if (j + 1) % 8 == 0:
            m = m[8:, :]
        m = m - m[:, j : j + 1] * scaled
    out_ref[...] = m.astype(jnp.bfloat16)


def solved(one, two, paths_all):
    k = one.shape[1]
    sets = one.shape[0] - k
    return pl.pallas_call(
        functools.partial(solve_kernel, paths_all),
        in_specs=[ON_CHIP, ON_CHIP],
        out_specs=ON_CHIP,
        out_shape=jax.ShapeDtypeStruct((sets, k), jnp.bfloat16),
        compiler_params=params(8),
        name="solve",
    )(one, two)


def value_of(coefs, feats):
    return jnp.dot(coefs, feats, preferred_element_type=jnp.float32).astype(jnp.bfloat16)


def limits_of(lag_ref, threshold_ref, transfer_ref):
    def column(ref):
        return jnp.broadcast_to(ref[...], (128, ref.shape[1])).T

    offset = (column(threshold_ref) + column(transfer_ref)).astype(jnp.float32) / 100.0
    recent = jnp.where(column(lag_ref) == 1, 1.0, 0.0)
    times = CHUNK // 128
    return jnp.concatenate([offset] * times, axis=1), jnp.concatenate([recent] * times, axis=1) > 0.5


def exposed_of(v, last, before, offset, recent):
    lagged = jnp.where(recent, last.astype(jnp.float32), before.astype(jnp.float32))
    collateral = jnp.maximum(lagged - offset, 0.0)
    return jnp.maximum(v.astype(jnp.float32) - collateral, 0.0)


def by_lane(exposed):
    return sum(exposed[:, i : i + 128] for i in range(0, exposed.shape[1], 128))


def profile_of(totals, paths_all, dates):
    sets = next(iter(totals.values())).shape[0]
    lane = lax.broadcasted_iota(jnp.int32, (sets, 128), 1)
    sums = jnp.zeros((sets, 128), jnp.float32)
    for t, total in totals.items():
        here = jnp.sum(total, axis=1, keepdims=True) / paths_all
        sums = jnp.where(lane == t, here, sums)
    return sums.T[:dates]


def later_kernel(
    paths_all,
    lag_ref,
    threshold_ref,
    transfer_ref,
    coefs_ref,
    features_ref,
    exposure_ref,
    early_ref,
    profile_ref,
    features_here,
    values_ref,
    staged_ref,
    feature_sems,
    sems,
):
    dates, sets, paths = values_ref.shape
    spans = [pl.ds(at, CHUNK) for at in range(0, paths, CHUNK)]
    loads = [
        pltpu.make_async_copy(features_ref.at[t], features_here.at[t], feature_sems.at[t])
        for t in range(dates)
    ]
    for copy in loads:
        copy.start()
    offset, recent = limits_of(lag_ref, threshold_ref, transfer_ref)
    totals, copies = {}, []
    for t in range(dates):
        loads[t].wait()
        for span in spans:
            values_ref[t, :, span] = value_of(coefs_ref[t], features_here[t, :, span])
        if t < LAG_MAX:
            early_ref[t] = values_ref[t]
            continue
        totals[t] = jnp.zeros((sets, 128), jnp.float32)
        for span in spans:
            exposed = exposed_of(
                *(values_ref[t - back, :, span] for back in range(LAG_MAX + 1)), offset, recent
            )
            staged_ref[t - LAG_MAX, :, span] = exposed.astype(jnp.bfloat16)
            totals[t] += by_lane(exposed)
        at = t - LAG_MAX
        copies.append(pltpu.make_async_copy(staged_ref.at[at], exposure_ref.at[t], sems.at[at]))
        copies[-1].start()
    profile_ref[...] = profile_of(totals, paths_all, dates)
    for copy in copies:
        copy.wait()


def first_kernel(
    paths_all,
    lag_ref,
    threshold_ref,
    transfer_ref,
    prior_coefs_ref,
    prior_features_ref,
    early_ref,
    profile_in_ref,
    exposure_in_ref,
    exposure_ref,
    profile_ref,
    staged_ref,
    sems,
):
    del exposure_in_ref
    sets, paths = early_ref.shape[1:]
    offset, recent = limits_of(lag_ref, threshold_ref, transfer_ref)
    totals = {t: jnp.zeros((sets, 128), jnp.float32) for t in range(LAG_MAX)}
    for at in range(0, paths, CHUNK):
        span = pl.ds(at, CHUNK)
        v = [value_of(prior_coefs_ref[i], prior_features_ref[i, :, span]) for i in range(LAG_MAX)]
        for t in range(LAG_MAX):
            v.append(early_ref[t, :, span])
            exposed = exposed_of(v[-1], v[-2], v[-3], offset, recent)
            staged_ref[t, :, span] = exposed.astype(jnp.bfloat16)
            totals[t] += by_lane(exposed)
    copies = [
        pltpu.make_async_copy(staged_ref.at[t], exposure_ref.at[t], sems.at[t])
        for t in range(LAG_MAX)
    ]
    for copy in copies:
        copy.start()
    profile_ref[...] = profile_in_ref[...] + profile_of(totals, paths_all, profile_ref.shape[0])
    for copy in copies:
        copy.wait()


def later_exposures(limits, coefs, features, paths_all):
    dates, k, paths = features.shape
    sets = coefs.shape[1]
    return pl.pallas_call(
        functools.partial(later_kernel, paths_all),
        in_specs=[ON_CHIP] * (len(limits) + 1) + [IN_HBM],
        out_specs=(IN_HBM, ON_CHIP, ON_CHIP),
        out_shape=(
            pltpu.HBM((dates, sets, paths), jnp.bfloat16),
            jax.ShapeDtypeStruct((LAG_MAX, sets, paths), jnp.bfloat16),
            jax.ShapeDtypeStruct((dates, sets), jnp.float32),
        ),
        scratch_shapes=[
            pltpu.VMEM((dates, k, paths), jnp.bfloat16),
            pltpu.VMEM((dates, sets, paths), jnp.bfloat16),
            pltpu.VMEM((dates - LAG_MAX, sets, paths), jnp.bfloat16),
            pltpu.SemaphoreType.DMA((dates,)),
            pltpu.SemaphoreType.DMA((dates - LAG_MAX,)),
        ],
        compiler_params=params(32),
        cost_estimate=pl.CostEstimate(
            flops=200 * dates * k * sets * paths,
            bytes_accessed=2 * dates * (k + sets) * paths,
            transcendentals=0,
        ),
        name="later",
    )(*limits, coefs, in_hbm(features))


def first_exposures(limits, prior_coefs, prior_features, early, profile, exposure, paths_all):
    args = (*limits, prior_coefs, prior_features, early, profile, exposure)
    return pl.pallas_call(
        functools.partial(first_kernel, paths_all),
        in_specs=[ON_CHIP] * (len(args) - 1) + [IN_HBM],
        out_specs=(IN_HBM, ON_CHIP),
        out_shape=(
            pltpu.HBM(exposure.shape, exposure.dtype),
            jax.ShapeDtypeStruct(profile.shape, profile.dtype),
        ),
        scratch_shapes=[
            pltpu.VMEM(early.shape, jnp.bfloat16),
            pltpu.SemaphoreType.DMA((LAG_MAX,)),
        ],
        input_output_aliases={len(args) - 1: 0},
        compiler_params=params(12),
        name="first",
    )(*args)


CORE, ROW, NEAR, NEXT, FAR = 1, 2, 4, 8, 24


def swapped(value, step):
    return lax.ppermute(value, "path", [(i, i ^ step) for i in range(lax.axis_size("path"))])


def picked(value, at):
    return lax.dynamic_index_in_dim(value, at, 0, keepdims=False)


def doubled(value, step, bit):
    other = swapped(value, step)
    low = jnp.where(bit == 0, value, other)
    high = jnp.where(bit == 0, other, value)
    return jnp.concatenate([low, high], axis=0)


def from_earlier(value):
    length = lax.axis_size("date")
    return lax.ppermute(value, "date", [(i, i + 1) for i in range(length - 1)])


def local(factors, cashflows, frequency, phases, margin_lag, thresholds, transfer_min):
    paths_all = factors.shape[2] * lax.axis_size("path")
    me = lax.axis_index("path")
    core, row, near = me & 1, (me >> 1) & 1, (me >> 2) & 1
    half = factors.shape[0] // 2
    quarter = half // 2
    firsts = (half * (1 - core), half * core + quarter * (1 - row), half * core + quarter * row)
    prior_factors = from_earlier(factors[-LAG_MAX:])
    phases = phases.reshape(1, -1)
    frequency = frequency.T
    features, sums_a = sums_of(firsts[0], half, frequency, phases, factors, cashflows)
    from_core = swapped(sums_a, CORE).reshape(2, quarter, *sums_a.shape[1:])
    first_b, prior_factors = lax.optimization_barrier((firsts[1], prior_factors))
    features, sums_b = sums_of(
        first_b, quarter, frequency, phases, factors, cashflows, features
    )
    from_row = swapped(sums_b + picked(from_core, 1 - row), ROW)
    features, sums_c = sums_of(firsts[2], quarter, frequency, phases, factors, cashflows, features)
    kept = sums_c + picked(from_core, row) + from_row
    kept = picked(kept, near) + swapped(picked(kept, 1 - near), NEAR)
    kept = kept + swapped(kept, NEXT)
    prior_features = features_of(frequency, phases, prior_factors)
    kept, prior_features = lax.optimization_barrier((kept, prior_features))
    coefs = solved(kept, swapped(kept, FAR), paths_all)
    coefs = doubled(coefs[None], NEAR, near)
    coefs = doubled(coefs, ROW, row)
    coefs = doubled(coefs, CORE, core)
    prior_coefs = from_earlier(coefs[-LAG_MAX:])
    limits = tuple(a.reshape(1, -1) for a in (margin_lag, thresholds, transfer_min))
    exposure, early, profile = later_exposures(limits, coefs, features, paths_all)
    exposure, profile = first_exposures(
        limits, prior_coefs, prior_features, early, profile, exposure, paths_all
    )
    for step in (CORE, ROW, NEAR, NEXT, FAR):
        profile = profile + swapped(profile, step)
    return exposure, profile


def solution(mesh):
    return jax.shard_map(
        local,
        mesh=mesh,
        in_specs=(P("date", None, "path"), P("date", None, "path"), P(), P(), P(), P(), P()),
        out_specs=(P("date", None, "path"), P("date", None)),
        check_vma=False,
    )
```

time: 137 us -> 98 us (0.72); the launches traced: 135 us -> 97.7 us
  waiting for transfers between devices: 64.8 us -> 24.4 us
  starting transfers between devices: 23.4 us -> 33.1 us
  Pallas kernels: 40.9 us -> 37.5 us
  local copies, waits for them, and re-layouts: 3.15 us -> 1.02 us
    ppermute x15 -> x13, waiting for transfers between devices: 57.5 us -> 24.4 us  [swapped(): lax.ppermute(value, 'path', [(i, i ^ step) for i in range(lax.axis_size('...]
    ppermute x15 -> x13, starting transfers between devices: 14.2 us -> 24.3 us  [swapped(): lax.ppermute(value, 'path', [(i, i ^ step) for i in range(lax.axis_size('...]
    ppermute x2, waiting for transfers between devices: 7.32 us -> 0.01 us  [from_earlier(): return lax.ppermute(value, 'date', [(i, i + 1) for i in range(length - 1)])]
    pallas_call x5 -> x7, Pallas kernels: 40.9 us -> 37.5 us  [the longest x3 17 us: sums_of(): pl.pallas_call(sums_kernel, in_specs=[SCALARS] + [IN_HBM] * (len(args) -...]
  transfers between devices with their start and end apart: 17 -> 15, of which waited for: 5 -> 12; matrix products, arithmetic and copies ran while one was open for 1% -> 0% of each run, Pallas kernels for 9% -> 25%
where the time goes in v3:
time: 98 us; the launch traced here: 97.7 us
  Pallas kernels  37.5 us (38%)
  starting transfers between devices  33.1 us (34%)
  waiting for transfers between devices  24.4 us (25%)
  local copies, waits for them, and re-layouts  1.02 us (1%)
    ppermute x13, waiting for transfers between devices, swapped(): lax.ppermute(value, 'path', [(i, i ^ step) for i in range(lax.axis_size('...  24.4 us
    ppermute x13, starting transfers between devices, swapped(): lax.ppermute(value, 'path', [(i, i ^ step) for i in range(lax.axis_size('...  24.3 us
    pallas_call x3, Pallas kernels, sums_of(): pl.pallas_call(sums_kernel, in_specs=[SCALARS] + [IN_HBM] * (len(args) -...  17 us
    pallas_call x1, Pallas kernels, solved(): pl.pallas_call(functools.partial(solve_kernel, paths_all), in_specs=[ON_C...  10.9 us
    ppermute x2, starting transfers between devices, from_earlier(): return lax.ppermute(value, 'date', [(i, i + 1) for i in range(length - 1)])  8.84 us
    pallas_call x1, Pallas kernels, later_exposures(): pl.pallas_call(functools.partial(later_kernel, paths_all), in_specs=[ON_C...  5.4 us
    pallas_call x1, Pallas kernels, features_of(): pl.pallas_call(features_kernel, in_specs=[ON_CHIP, ON_CHIP, ON_CHIP], out...  2.26 us
    pallas_call x1, Pallas kernels, first_exposures(): pl.pallas_call(functools.partial(first_kernel, paths_all), in_specs=[ON_C...  1.98 us
  transfers between devices with their start and end apart: 15, of which 12 were waited for; matrix products, arithmetic and copies ran while one was open for 0% of the time, Pallas kernels for 25%

profile of v3, /device:TPU:2, one launch (start us, length us, event | category | flops | bytes accessed | tf_op | source)
XLA Modules:
  0.0 97.7 jit_solution(3388106799616968056)
XLA Ops:
  0.6 1.0 slice.6
  1.6 5.1 %collective-permute-start = (bf16[2,16,4096]{2,1,0:T(8,128)(2,1)S(1)}, bf16[2,16,4096]{2,1,0:T(8,128)(2,1)S(1)}, u32[]{:S(2)}, u32[]{:S(2)}) collective-permute-start(bf16[2,16,4096]{2,1,0:T(8,128)(2,1)S(1)} %slice.6), channel_id=1, source_target_pairs={{0,32},{32,64},{64,96},{96,128},{128,160},{160,192},{192,224},{1,3... | collective-permute-start | bytes 786440 | tf_op jit(solution)/shard_map/ppermute | solution.py:428
  6.7 7.7 %sums.3 = (bf16[8,128,4096]{2,1,0:T(8,128)(2,1)}, f32[4,192,128]{2,1,0:T(8,128)S(1)}) custom-call(s32[1]{0:T(128)} %bitcast.7.first_ref, bf16[16,128]{1,0:T(8,128)(2,1)} %bitcast.29, f32[1,128]{1,0:T(1,128)} %bitcast.33, bf16[8,16,4096]{2,1,0:T(8,128)(2,1)} %factors_ref.5, bf16[8,64,4096]{2,1,0:T(8,128)(2,1)} %flows_ref.5), custom_call_target="tpu_custom_call" | custom-call | flops 41943040000 | bytes 8388608 | tf_op jit(solution)/shard_map/sums/pallas_call | solution.py:179
  14.4 0.1 collective-permute-start.1
  14.5 0.0 collective-permute-done.factors_ref
  14.5 4.6 %sums.4 = (bf16[8,128,4096]{2,1,0:T(8,128)(2,1)}, f32[2,192,128]{2,1,0:T(8,128)S(1)}) custom-call(s32[1]{0:T(128)} %bitcast.6.first_ref, bf16[16,128]{1,0:T(8,128)(2,1)} %bitcast.30, f32[1,128]{1,0:T(1,128)} %bitcast.34, bf16[8,16,4096]{2,1,0:T(8,128)(2,1)} %factors_ref.5, bf16[8,64,4096]{2,1,0:T(8,128)(2,1)} %flows_ref.5, ...), custom_call_target="tpu_custom_call", output_to_operand_aliasing={{0}: (5, {})} | custom-call | flops 20971520000 | bytes 4194304 | tf_op jit(solution)/shard_map/sums/pallas_call | solution.py:179
  19.2 0.0 collective-permute-done.1
  19.2 1.0 %collective-permute-start.2 = (f32[2,192,128]{2,1,0:T(8,128)S(1)}, f32[2,192,128]{2,1,0:T(8,128)S(1)}, u32[]{:S(2)}, u32[]{:S(2)}) collective-permute-start(f32[2,192,128]{2,1,0:T(8,128)S(1)} %bitcast_add_fusion), channel_id=1, source_target_pairs={{0,2},{1,3},{2,0},{3,1},{4,6},{5,7},{6,4},{7,5},{8,10},{9,11},{10,... | collective-permute-start | bytes 589832 | tf_op jit(solution)/shard_map/ppermute | solution.py:412
  20.3 0.0 copy-start.3
  20.3 0.0 copy-start.4
  20.3 4.6 %sums.5 = (bf16[8,128,4096]{2,1,0:T(8,128)(2,1)}, f32[2,192,128]{2,1,0:T(8,128)S(1)}) custom-call(s32[1]{0:T(128)} %bitcast.3.first_ref, bf16[16,128]{1,0:T(8,128)(2,1)} %bitcast.31, f32[1,128]{1,0:T(1,128)} %bitcast.35, bf16[8,16,4096]{2,1,0:T(8,128)(2,1)} %factors_ref.5, bf16[8,64,4096]{2,1,0:T(8,128)(2,1)} %flows_ref.5, ...), custom_call_target="tpu_custom_call", output_to_operand_aliasing={{0}: (5, {})} | custom-call | flops 20971520000 | bytes 4194304 | tf_op jit(solution)/shard_map/sums/pallas_call | solution.py:179
  24.9 1.8 %collective-permute-done.2 = f32[2,192,128]{2,1,0:T(8,128)S(1)} collective-permute-done((f32[2,192,128]{2,1,0:T(8,128)S(1)}, f32[2,192,128]{2,1,0:T(8,128)S(1)}, u32[]{:S(2)}, u32[]{:S(2)}) %collective-permute-start.2) | collective-permute-done | bytes 196640 | tf_op jit(solution)/shard_map/ppermute | solution.py:412
  26.8 2.2 %collective-permute-start.3 = (f32[192,128]{1,0:T(8,128)S(1)}, f32[192,128]{1,0:T(8,128)S(1)}, u32[]{:S(2)}, u32[]{:S(2)}) collective-permute-start(f32[192,128]{1,0:T(8,128)S(1)} %dynamic-slice_bitcast_fusion), channel_id=1, source_target_pairs={{0,4},{1,5},{2,6},{3,7},{4,0},{5,1},{6,2},{7,3},{8,12},{9,13},{10,... | collective-permute-start | bytes 294920 | tf_op jit(solution)/shard_map/ppermute | solution.py:412
  29.0 2.8 %collective-permute-done.3 = f32[192,128]{1,0:T(8,128)S(1)} collective-permute-done((f32[192,128]{1,0:T(8,128)S(1)}, f32[192,128]{1,0:T(8,128)S(1)}, u32[]{:S(2)}, u32[]{:S(2)}) %collective-permute-start.3) | collective-permute-done | bytes 98336 | tf_op jit(solution)/shard_map/ppermute | solution.py:412
  31.8 0.0 copy-start
  31.8 0.0 copy-start.1
  31.8 0.0 copy-start.2
  31.8 3.4 %collective-permute-start.4 = (f32[192,128]{1,0:T(8,128)S(1)}, f32[192,128]{1,0:T(8,128)S(1)}, u32[]{:S(2)}, u32[]{:S(2)}) collective-permute-start(f32[192,128]{1,0:T(8,128)S(1)} %bitcast_add_fusion.2), channel_id=1, source_target_pairs={{0,8},{1,9},{2,10},{3,11},{4,12},{5,13},{6,14},{7,15},{8,0},{9,1},... | collective-permute-start | bytes 294920 | tf_op jit(solution)/shard_map/ppermute | solution.py:412
  35.2 0.0 copy-done.3
  35.2 0.0 copy-done.4
  35.2 2.3 %features.1.prior_features_ref = bf16[2,128,4096]{2,1,0:T(8,128)(2,1)S(1)} custom-call(bf16[16,128]{1,0:T(8,128)(2,1)S(1)} %bitcast.32, f32[1,128]{1,0:T(1,128)S(1)} %bitcast.36, bf16[2,16,4096]{2,1,0:T(8,128)(2,1)S(1)} %collective-permute-done.factors_ref), custom_call_target="tpu_custom_call" | custom-call | flops 2097152000 | bytes 2097152 | tf_op jit(solution)/shard_map/features/pallas_call | solution.py:158
  37.4 1.9 %collective-permute-done.4 = f32[192,128]{1,0:T(8,128)S(1)} collective-permute-done((f32[192,128]{1,0:T(8,128)S(1)}, f32[192,128]{1,0:T(8,128)S(1)}, u32[]{:S(2)}, u32[]{:S(2)}) %collective-permute-start.4) | collective-permute-done | bytes 98336 | tf_op jit(solution)/shard_map/ppermute | solution.py:412
  39.4 4.5 %collective-permute-start.5 = (f32[192,128]{1,0:T(8,128)S(1)}, f32[192,128]{1,0:T(8,128)S(1)}, u32[]{:S(2)}, u32[]{:S(2)}) collective-permute-start(f32[192,128]{1,0:T(8,128)S(1)} %add.62.one_ref), channel_id=1, source_target_pairs={{0,24},{1,25},{2,26},{3,27},{4,28},{5,29},{6,30},{7,31},{8,16},{9,... | collective-permute-start | bytes 294920 | tf_op jit(solution)/shard_map/ppermute | solution.py:412
  43.8 2.6 %collective-permute-done.5.two_ref = f32[192,128]{1,0:T(8,128)S(1)} collective-permute-done((f32[192,128]{1,0:T(8,128)S(1)}, f32[192,128]{1,0:T(8,128)S(1)}, u32[]{:S(2)}, u32[]{:S(2)}) %collective-permute-start.5) | collective-permute-done | bytes 98336 | tf_op jit(solution)/shard_map/ppermute | solution.py:412
  46.5 10.9 %solve.1 = bf16[64,128]{1,0:T(8,128)(2,1)S(1)} custom-call(f32[192,128]{1,0:T(8,128)S(1)} %add.62.one_ref, f32[192,128]{1,0:T(8,128)S(1)} %collective-permute-done.5.two_ref), custom_call_target="tpu_custom_call" | custom-call | tf_op jit(solution)/shard_map/solve/pallas_call | solution.py:229
  57.4 2.6 %collective-permute-start.6 = (bf16[1,64,128]{2,1,0:T(8,128)(2,1)S(1)}, bf16[1,64,128]{2,1,0:T(8,128)(2,1)S(1)}, u32[]{:S(2)}, u32[]{:S(2)}) collective-permute-start(bf16[1,64,128]{2,1,0:T(8,128)(2,1)S(1)} %bitcast.22), channel_id=1, source_target_pairs={{0,4},{1,5},{2,6},{3,7},{4,0},{5,1},{6,2},{7,3},{8,12},{9,13},{10,... | collective-permute-start | bytes 49160 | tf_op jit(solution)/shard_map/ppermute | solution.py:412
  59.9 1.7 %collective-permute-done.6 = bf16[1,64,128]{2,1,0:T(8,128)(2,1)S(1)} collective-permute-done((bf16[1,64,128]{2,1,0:T(8,128)(2,1)S(1)}, bf16[1,64,128]{2,1,0:T(8,128)(2,1)S(1)}, u32[]{:S(2)}, u32[]{:S(2)}) %collective-permute-start.6) | collective-permute-done | bytes 16416 | tf_op jit(solution)/shard_map/ppermute | solution.py:412
  61.7 0.7 collective-permute-start.7
  62.3 3.3 %collective-permute-done.7 = bf16[2,64,128]{2,1,0:T(8,128)(2,1)S(1)} collective-permute-done((bf16[2,64,128]{2,1,0:T(8,128)(2,1)S(1)}, bf16[2,64,128]{2,1,0:T(8,128)(2,1)S(1)}, u32[]{:S(2)}, u32[]{:S(2)}) %collective-permute-start.7) | collective-permute-done | bytes 32800 | tf_op jit(solution)/shard_map/ppermute | solution.py:412
  65.7 0.1 collective-permute-start.8
  65.8 1.2 %collective-permute-done.8 = bf16[4,64,128]{2,1,0:T(8,128)(2,1)S(1)} collective-permute-done((bf16[4,64,128]{2,1,0:T(8,128)(2,1)S(1)}, bf16[4,64,128]{2,1,0:T(8,128)(2,1)S(1)}, u32[]{:S(2)}, u32[]{:S(2)}) %collective-permute-start.8) | collective-permute-done | bytes 65568 | tf_op jit(solution)/shard_map/ppermute | solution.py:412
  67.1 3.7 %collective-permute-start.9 = (bf16[2,64,128]{2,1,0:T(8,128)(2,1)S(1)}, bf16[2,64,128]{2,1,0:T(8,128)(2,1)S(1)}, u32[]{:S(2)}, u32[]{:S(2)}) collective-permute-start(bf16[2,64,128]{2,1,0:T(8,128)(2,1)S(1)} %slice.8), channel_id=1, source_target_pairs={{0,32},{32,64},{64,96},{96,128},{128,160},{160,192},{192,224},{1,3... | collective-permute-start | bytes 98312 | tf_op jit(solution)/shard_map/ppermute | solution.py:428
  70.8 0.0 copy-done
  70.8 0.0 copy-done.1
  70.9 0.0 copy-done.2
  70.9 5.4 %later.1 = (bf16[8,64,4096]{2,1,0:T(8,128)(2,1)}, bf16[2,64,4096]{2,1,0:T(8,128)(2,1)S(1)}, f32[8,64]{1,0:T(8,128)S(1)}) custom-call(s32[1,64]{1,0:T(1,128)S(1)} %bitcast.23, s32[1,64]{1,0:T(1,128)S(1)} %bitcast.25, s32[1,64]{1,0:T(1,128)S(1)} %bitcast.27, bf16[8,64,128]{2,1,0:T(8,128)(2,1)S(1)} %pad_maximum_fusion.coefs_ref, ...), custom_call_target="tpu_custom_call" | custom-call | flops 53687091200 | bytes 12582912 | tf_op jit(solution)/shard_map/later/pallas_call | solution.py:362
  76.3 0.0 collective-permute-done.9.prior_coefs_ref
  76.3 2.0 %first.1 = (bf16[8,64,4096]{2,1,0:T(8,128)(2,1)}, f32[8,64]{1,0:T(8,128)S(1)}) custom-call(s32[1,64]{1,0:T(1,128)S(1)} %bitcast.24, s32[1,64]{1,0:T(1,128)S(1)} %bitcast.26, s32[1,64]{1,0:T(1,128)S(1)} %bitcast.28, bf16[2,64,128]{2,1,0:T(8,128)(2,1)S(1)} %collective-permute-done.9.prior_coefs_ref, ...), custom_call_target="tpu_custom_call", output_to_operand_aliasing={{0}: (7, {})} | custom-call | tf_op jit(solution)/shard_map/first/pallas_call | solution.py:390
  78.3 0.1 collective-permute-start.10
  78.4 1.2 %collective-permute-done.10 = f32[8,64]{1,0:T(8,128)S(1)} collective-permute-done((f32[8,64]{1,0:T(8,128)S(1)}, f32[8,64]{1,0:T(8,128)S(1)}, u32[]{:S(2)}, u32[]{:S(2)}) %collective-permute-start.10) | collective-permute-done | bytes 2080 | tf_op jit(solution)/shard_map/ppermute | solution.py:412
  79.5 1.1 %collective-permute-start.11 = (f32[8,64]{1,0:T(8,128)S(1)}, f32[8,64]{1,0:T(8,128)S(1)}, u32[]{:S(2)}, u32[]{:S(2)}) collective-permute-start(f32[8,64]{1,0:T(8,128)S(1)} %add.63), channel_id=1, source_target_pairs={{0,2},{1,3},{2,0},{3,1},{4,6},{5,7},{6,4},{7,5},{8,10},{9,11},{10,... | collective-permute-start | bytes 6152 | tf_op jit(solution)/shard_map/ppermute | solution.py:412
  80.7 2.5 %collective-permute-done.11 = f32[8,64]{1,0:T(8,128)S(1)} collective-permute-done((f32[8,64]{1,0:T(8,128)S(1)}, f32[8,64]{1,0:T(8,128)S(1)}, u32[]{:S(2)}, u32[]{:S(2)}) %collective-permute-start.11) | collective-permute-done | bytes 2080 | tf_op jit(solution)/shard_map/ppermute | solution.py:412
  83.1 2.0 %collective-permute-start.12 = (f32[8,64]{1,0:T(8,128)S(1)}, f32[8,64]{1,0:T(8,128)S(1)}, u32[]{:S(2)}, u32[]{:S(2)}) collective-permute-start(f32[8,64]{1,0:T(8,128)S(1)} %add.64), channel_id=1, source_target_pairs={{0,4},{1,5},{2,6},{3,7},{4,0},{5,1},{6,2},{7,3},{8,12},{9,13},{10,... | collective-permute-start | bytes 6152 | tf_op jit(solution)/shard_map/ppermute | solution.py:412
  85.2 1.6 %collective-permute-done.12 = f32[8,64]{1,0:T(8,128)S(1)} collective-permute-done((f32[8,64]{1,0:T(8,128)S(1)}, f32[8,64]{1,0:T(8,128)S(1)}, u32[]{:S(2)}, u32[]{:S(2)}) %collective-permute-start.12) | collective-permute-done | bytes 2080 | tf_op jit(solution)/shard_map/ppermute | solution.py:412
  86.8 3.1 %collective-permute-start.13 = (f32[8,64]{1,0:T(8,128)S(1)}, f32[8,64]{1,0:T(8,128)S(1)}, u32[]{:S(2)}, u32[]{:S(2)}) collective-permute-start(f32[8,64]{1,0:T(8,128)S(1)} %add.65), channel_id=1, source_target_pairs={{0,8},{1,9},{2,10},{3,11},{4,12},{5,13},{6,14},{7,15},{8,0},{9,1},... | collective-permute-start | bytes 6152 | tf_op jit(solution)/shard_map/ppermute | solution.py:412
  89.8 1.6 %collective-permute-done.13 = f32[8,64]{1,0:T(8,128)S(1)} collective-permute-done((f32[8,64]{1,0:T(8,128)S(1)}, f32[8,64]{1,0:T(8,128)S(1)}, u32[]{:S(2)}, u32[]{:S(2)}) %collective-permute-start.13) | collective-permute-done | bytes 2080 | tf_op jit(solution)/shard_map/ppermute | solution.py:412
  91.4 3.5 %collective-permute-start.14 = (f32[8,64]{1,0:T(8,128)S(1)}, f32[8,64]{1,0:T(8,128)S(1)}, u32[]{:S(2)}, u32[]{:S(2)}) collective-permute-start(f32[8,64]{1,0:T(8,128)S(1)} %add.66), channel_id=1, source_target_pairs={{0,24},{1,25},{2,26},{3,27},{4,28},{5,29},{6,30},{7,31},{8,16},{9,... | collective-permute-start | bytes 6152 | tf_op jit(solution)/shard_map/ppermute | solution.py:412
  94.9 2.2 %collective-permute-done.14 = f32[8,64]{1,0:T(8,128)S(1)} collective-permute-done((f32[8,64]{1,0:T(8,128)S(1)}, f32[8,64]{1,0:T(8,128)S(1)}, u32[]{:S(2)}, u32[]{:S(2)}) %collective-permute-start.14) | collective-permute-done | bytes 2080 | tf_op jit(solution)/shard_map/ppermute | solution.py:412
  97.1 0.6 add.67
  (16 shorter events, 0.2 us)
Async XLA Ops:
  1.6 12.9 %collective-permute-start = (bf16[2,16,4096]{2,1,0:T(8,128)(2,1)S(1)}, bf16[2,16,4096]{2,1,0:T(8,128)(2,1)S(1)}, u32[]{:S(2)}, u32[]{:S(2)}) collective-permute-start(bf16[2,16,4096]{2,1,0:T(8,128)(2,1)S(1)} %slice.6), channel_id=1, source_target_pairs={{0,32},{32,64},{64,96},{96,128},{128,160},{160,192},{192,224},{1,3... | collective-permute-start | bytes 786440 | tf_op jit(solution)/shard_map/ppermute | solution.py:428
  14.4 4.8 %collective-permute-start.1 = (f32[4,192,128]{2,1,0:T(8,128)S(1)}, f32[4,192,128]{2,1,0:T(8,128)S(1)}, u32[]{:S(2)}, u32[]{:S(2)}) collective-permute-start(f32[4,192,128]{2,1,0:T(8,128)S(1)} %get-tuple-element.21), channel_id=1, source_target_pairs={{0,1},{1,0},{2,3},{3,2},{4,5},{5,4},{6,7},{7,6},{8,9},{9,8},{10,11... | collective-permute-start | bytes 1179656 | tf_op jit(solution)/shard_map/ppermute | solution.py:412
  19.2 7.5 %collective-permute-start.2 = (f32[2,192,128]{2,1,0:T(8,128)S(1)}, f32[2,192,128]{2,1,0:T(8,128)S(1)}, u32[]{:S(2)}, u32[]{:S(2)}) collective-permute-start(f32[2,192,128]{2,1,0:T(8,128)S(1)} %bitcast_add_fusion), channel_id=1, source_target_pairs={{0,2},{1,3},{2,0},{3,1},{4,6},{5,7},{6,4},{7,5},{8,10},{9,11},{10,... | collective-permute-start | bytes 589832 | tf_op jit(solution)/shard_map/ppermute | solution.py:412
  20.3 14.9 %copy-start.3 = (bf16[128,16]{0,1:T(8,128)(2,1)S(1)}, bf16[128,16]{0,1:T(8,128)(2,1)}, u32[]{:S(2)}) copy-start(bf16[128,16]{0,1:T(8,128)(2,1)} %param.9) | copy-start | bytes 12292
  20.3 14.9 %copy-start.4 = (f32[128]{0:T(128)S(1)}, f32[128]{0:T(128)}, u32[]{:S(2)}) copy-start(f32[128]{0:T(128)} %param.10) | copy-start | bytes 1540
  26.8 5.0 %collective-permute-start.3 = (f32[192,128]{1,0:T(8,128)S(1)}, f32[192,128]{1,0:T(8,128)S(1)}, u32[]{:S(2)}, u32[]{:S(2)}) collective-permute-start(f32[192,128]{1,0:T(8,128)S(1)} %dynamic-slice_bitcast_fusion), channel_id=1, source_target_pairs={{0,4},{1,5},{2,6},{3,7},{4,0},{5,1},{6,2},{7,3},{8,12},{9,13},{10,... | collective-permute-start | bytes 294920 | tf_op jit(solution)/shard_map/ppermute | solution.py:412
  31.8 39.1 %copy-start = (s32[64]{0:T(128)S(1)}, s32[64]{0:T(128)}, u32[]{:S(2)}) copy-start(s32[64]{0:T(128)} %param.11) | copy-start | bytes 772
  31.8 39.1 %copy-start.1 = (s32[64]{0:T(128)S(1)}, s32[64]{0:T(128)}, u32[]{:S(2)}) copy-start(s32[64]{0:T(128)} %param.12) | copy-start | bytes 772
  31.8 39.1 %copy-start.2 = (s32[64]{0:T(128)S(1)}, s32[64]{0:T(128)}, u32[]{:S(2)}) copy-start(s32[64]{0:T(128)} %param.13) | copy-start | bytes 772
  31.8 7.6 %collective-permute-start.4 = (f32[192,128]{1,0:T(8,128)S(1)}, f32[192,128]{1,0:T(8,128)S(1)}, u32[]{:S(2)}, u32[]{:S(2)}) collective-permute-start(f32[192,128]{1,0:T(8,128)S(1)} %bitcast_add_fusion.2), channel_id=1, source_target_pairs={{0,8},{1,9},{2,10},{3,11},{4,12},{5,13},{6,14},{7,15},{8,0},{9,1},... | collective-permute-start | bytes 294920 | tf_op jit(solution)/shard_map/ppermute | solution.py:412
  39.4 7.1 %collective-permute-start.5 = (f32[192,128]{1,0:T(8,128)S(1)}, f32[192,128]{1,0:T(8,128)S(1)}, u32[]{:S(2)}, u32[]{:S(2)}) collective-permute-start(f32[192,128]{1,0:T(8,128)S(1)} %add.62.one_ref), channel_id=1, source_target_pairs={{0,24},{1,25},{2,26},{3,27},{4,28},{5,29},{6,30},{7,31},{8,16},{9,... | collective-permute-start | bytes 294920 | tf_op jit(solution)/shard_map/ppermute | solution.py:412
  57.4 4.3 %collective-permute-start.6 = (bf16[1,64,128]{2,1,0:T(8,128)(2,1)S(1)}, bf16[1,64,128]{2,1,0:T(8,128)(2,1)S(1)}, u32[]{:S(2)}, u32[]{:S(2)}) collective-permute-start(bf16[1,64,128]{2,1,0:T(8,128)(2,1)S(1)} %bitcast.22), channel_id=1, source_target_pairs={{0,4},{1,5},{2,6},{3,7},{4,0},{5,1},{6,2},{7,3},{8,12},{9,13},{10,... | collective-permute-start | bytes 49160 | tf_op jit(solution)/shard_map/ppermute | solution.py:412
  61.7 4.0 %collective-permute-start.7 = (bf16[2,64,128]{2,1,0:T(8,128)(2,1)S(1)}, bf16[2,64,128]{2,1,0:T(8,128)(2,1)S(1)}, u32[]{:S(2)}, u32[]{:S(2)}) collective-permute-start(bf16[2,64,128]{2,1,0:T(8,128)(2,1)S(1)} %pad_maximum_fusion.2), channel_id=1, source_target_pairs={{0,2},{1,3},{2,0},{3,1},{4,6},{5,7},{6,4},{7,5},{8,10},{9,11},{10,... | collective-permute-start | bytes 98312 | tf_op jit(solution)/shard_map/ppermute | solution.py:412
  65.7 1.3 %collective-permute-start.8 = (bf16[4,64,128]{2,1,0:T(8,128)(2,1)S(1)}, bf16[4,64,128]{2,1,0:T(8,128)(2,1)S(1)}, u32[]{:S(2)}, u32[]{:S(2)}) collective-permute-start(bf16[4,64,128]{2,1,0:T(8,128)(2,1)S(1)} %pad_maximum_fusion.1), channel_id=1, source_target_pairs={{0,1},{1,0},{2,3},{3,2},{4,5},{5,4},{6,7},{7,6},{8,9},{9,8},{10,11... | collective-permute-start | bytes 196616 | tf_op jit(solution)/shard_map/ppermute | solution.py:412
  67.1 9.2 %collective-permute-start.9 = (bf16[2,64,128]{2,1,0:T(8,128)(2,1)S(1)}, bf16[2,64,128]{2,1,0:T(8,128)(2,1)S(1)}, u32[]{:S(2)}, u32[]{:S(2)}) collective-permute-start(bf16[2,64,128]{2,1,0:T(8,128)(2,1)S(1)} %slice.8), channel_id=1, source_target_pairs={{0,32},{32,64},{64,96},{96,128},{128,160},{160,192},{192,224},{1,3... | collective-permute-start | bytes 98312 | tf_op jit(solution)/shard_map/ppermute | solution.py:428
  78.3 1.3 %collective-permute-start.10 = (f32[8,64]{1,0:T(8,128)S(1)}, f32[8,64]{1,0:T(8,128)S(1)}, u32[]{:S(2)}, u32[]{:S(2)}) collective-permute-start(f32[8,64]{1,0:T(8,128)S(1)} %get-tuple-element.31), channel_id=1, source_target_pairs={{0,1},{1,0},{2,3},{3,2},{4,5},{5,4},{6,7},{7,6},{8,9},{9,8},{10,11... | collective-permute-start | bytes 6152 | tf_op jit(solution)/shard_map/ppermute | solution.py:412
  79.5 3.6 %collective-permute-start.11 = (f32[8,64]{1,0:T(8,128)S(1)}, f32[8,64]{1,0:T(8,128)S(1)}, u32[]{:S(2)}, u32[]{:S(2)}) collective-permute-start(f32[8,64]{1,0:T(8,128)S(1)} %add.63), channel_id=1, source_target_pairs={{0,2},{1,3},{2,0},{3,1},{4,6},{5,7},{6,4},{7,5},{8,10},{9,11},{10,... | collective-permute-start | bytes 6152 | tf_op jit(solution)/shard_map/ppermute | solution.py:412
  83.1 3.6 %collective-permute-start.12 = (f32[8,64]{1,0:T(8,128)S(1)}, f32[8,64]{1,0:T(8,128)S(1)}, u32[]{:S(2)}, u32[]{:S(2)}) collective-permute-start(f32[8,64]{1,0:T(8,128)S(1)} %add.64), channel_id=1, source_target_pairs={{0,4},{1,5},{2,6},{3,7},{4,0},{5,1},{6,2},{7,3},{8,12},{9,13},{10,... | collective-permute-start | bytes 6152 | tf_op jit(solution)/shard_map/ppermute | solution.py:412
  86.8 4.7 %collective-permute-start.13 = (f32[8,64]{1,0:T(8,128)S(1)}, f32[8,64]{1,0:T(8,128)S(1)}, u32[]{:S(2)}, u32[]{:S(2)}) collective-permute-start(f32[8,64]{1,0:T(8,128)S(1)} %add.65), channel_id=1, source_target_pairs={{0,8},{1,9},{2,10},{3,11},{4,12},{5,13},{6,14},{7,15},{8,0},{9,1},... | collective-permute-start | bytes 6152 | tf_op jit(solution)/shard_map/ppermute | solution.py:412
  91.4 5.7 %collective-permute-start.14 = (f32[8,64]{1,0:T(8,128)S(1)}, f32[8,64]{1,0:T(8,128)S(1)}, u32[]{:S(2)}, u32[]{:S(2)}) collective-permute-start(f32[8,64]{1,0:T(8,128)S(1)} %add.66), channel_id=1, source_target_pairs={{0,24},{1,25},{2,26},{3,27},{4,28},{5,29},{6,30},{7,31},{8,16},{9,... | collective-permute-start | bytes 6152 | tf_op jit(solution)/shard_map/ppermute | solution.py:412

commit v4 on v3

--- a/solution.py
+++ b/solution.py
@@ -20,6 +20,7 @@
 ROUNDER = 12582912.0
 INV_TWO_PI = 0.15915494309189535
 CHUNK = 512
+BLOCK = 8
 
 
 def three_parts(x):
@@ -84,36 +85,36 @@
     )
     for copy in small:
         copy.start()
-    loads, saves = [], []
-    for i in range(dates):
-        t = first_ref[0] + i
-        loads.append(
-            (
-                pltpu.make_async_copy(factors_ref.at[t], factors_here.at[i], factor_sems.at[i]),
-                pltpu.make_async_copy(flows_ref.at[t], flows_here.at[i], flow_sems.at[i]),
-            )
-        )
-        saves.append(
-            pltpu.make_async_copy(features_here.at[i], features_ref.at[t], feature_sems.at[i])
-        )
-        for copy in loads[-1]:
+    ats = [first_ref[0] + i for i in range(dates)]
+    factor_loads = [
+        pltpu.make_async_copy(factors_ref.at[t], factors_here.at[i], factor_sems.at[i])
+        for i, t in enumerate(ats)
+    ]
+    flow_loads = [
+        pltpu.make_async_copy(flows_ref.at[t], flows_here.at[i], flow_sems.at[i])
+        for i, t in enumerate(ats)
+    ]
+    for pair in zip(factor_loads, flow_loads):
+        for copy in pair:
             copy.start()
     for copy in small:
         copy.wait()
     weights = turn_weights(freq_here, phase_here)
     items = [(i, pl.ds(at, CHUNK)) for i in range(dates) for at in range(0, paths, CHUNK)]
-    arrived = set()
+    arrived, joined, saves = set(), set(), []
 
     def turns_of(item):
         i, span = item
         if i not in arrived:
             arrived.add(i)
-            for copy in loads[i]:
-                copy.wait()
+            factor_loads[i].wait()
         return chunk_turns(weights, factors_here[i, :, span])
 
     def product_of(item, feats):
         i, span = item
+        if i not in joined:
+            joined.add(i)
+            flow_loads[i].wait()
         both = jnp.concatenate([feats, flows_here[i, :, span]], axis=0)
         return lax.dot_general(
             both, feats, (((1,), (1,)), ((), ())), preferred_element_type=jnp.float32
@@ -129,11 +130,18 @@
             sums = product if starts else sums + product
             if at == len(items) or items[at][0] != i:
                 sums_ref[i] = sums
-                saves[i].start()
         if at < len(items):
             i, span = items[at]
             feats = cosines(turns)
             features_here[i, :, span] = feats
+            saves.append(
+                pltpu.make_async_copy(
+                    features_here.at[i, :, span],
+                    features_ref.at[ats[i], :, span],
+                    feature_sems.at[at],
+                )
+            )
+            saves[-1].start()
             turns = later
     for copy in saves:
         copy.wait()
@@ -193,7 +201,7 @@
             pltpu.SemaphoreType.DMA((2,)),
             pltpu.SemaphoreType.DMA((dates,)),
             pltpu.SemaphoreType.DMA((dates,)),
-            pltpu.SemaphoreType.DMA((dates,)),
+            pltpu.SemaphoreType.DMA((dates * (paths // CHUNK),)),
         ],
         input_output_aliases=aliases,
         compiler_params=params(24),
@@ -212,14 +220,25 @@
     system = total[:k] + jnp.where(row_at == lane_at, ridge_weight, 0.0)
     m = jnp.concatenate([system, total[k:]], axis=0)
     lane = lax.broadcasted_iota(jnp.int32, (1, k), 1)
-    for j in range(k):
-        top = j // 8 * 8
-        row = m[j - (k + 64 - m.shape[0]) : j - (k + 64 - m.shape[0]) + 1, :]
-        pivot = 1.0 / row[:, j : j + 1]
-        scaled = jnp.where(lane == j, 1.0 - pivot, row * pivot)
-        if (j + 1) % 8 == 0:
-            m = m[8:, :]
-        m = m - m[:, j : j + 1] * scaled
+    for j in range(0, k, BLOCK):
+        pivots = [m[i : i + 1, :] for i in range(BLOCK)]
+        entries = [
+            [jnp.broadcast_to(row[:, j + i : j + i + 1], (1, k)) for i in range(BLOCK)]
+            for row in pivots
+        ]
+        rows = [row - jnp.where(lane == j + i, 1.0, 0.0) for i, row in enumerate(pivots)]
+        for p in range(BLOCK):
+            inverse = 1.0 / entries[p][p]
+            rows[p] = rows[p] * inverse
+            for q in range(p + 1, BLOCK):
+                entries[p][q] = entries[p][q] * inverse
+            for i in range(BLOCK):
+                if i != p:
+                    rows[i] = rows[i] - entries[i][p] * rows[p]
+                    for q in range(p + 1, BLOCK):
+                        entries[i][q] = entries[i][q] - entries[i][p] * entries[p][q]
+        m = m[BLOCK:]
+        m = m - sum(m[:, j + i : j + i + 1] * rows[i] for i in range(BLOCK))
     out_ref[...] = m.astype(jnp.bfloat16)
 
 
@@ -247,11 +266,13 @@
     offset = (column(threshold_ref) + column(transfer_ref)).astype(jnp.float32) / 100.0
     recent = jnp.where(column(lag_ref) == 1, 1.0, 0.0)
     times = CHUNK // 128
-    return jnp.concatenate([offset] * times, axis=1), jnp.concatenate([recent] * times, axis=1) > 0.5
+    return jnp.concatenate([offset] * times, axis=1), jnp.concatenate(
+        [recent.astype(jnp.bfloat16)] * times, axis=1
+    ) > 0.5
 
 
 def exposed_of(v, last, before, offset, recent):
-    lagged = jnp.where(recent, last.astype(jnp.float32), before.astype(jnp.float32))
+    lagged = jnp.where(recent, last, before).astype(jnp.float32)
     collateral = jnp.maximum(lagged - offset, 0.0)
     return jnp.maximum(v.astype(jnp.float32) - collateral, 0.0)
 
@@ -351,7 +372,9 @@
     ]
     for copy in copies:
         copy.start()
-    profile_ref[...] = profile_in_ref[...] + profile_of(totals, paths_all, profile_ref.shape[0])
+    profile = profile_in_ref[...] + profile_of(totals, paths_all, profile_in_ref.shape[0])
+    flat = jnp.concatenate([profile[t : t + 1] for t in range(profile.shape[0])], axis=1)
+    profile_ref[...] = jnp.broadcast_to(flat[None], profile_ref.shape)
     for copy in copies:
         copy.wait()
 
@@ -393,7 +416,7 @@
         out_specs=(IN_HBM, ON_CHIP),
         out_shape=(
             pltpu.HBM(exposure.shape, exposure.dtype),
-            jax.ShapeDtypeStruct(profile.shape, profile.dtype),
+            jax.ShapeDtypeStruct((lax.axis_size("path"), 1, profile.size), profile.dtype),
         ),
         scratch_shapes=[
             pltpu.VMEM(early.shape, jnp.bfloat16),
@@ -403,6 +426,23 @@
         compiler_params=params(12),
         name="first",
     )(*args)
+
+
+def total_kernel(parts_ref, total_ref):
+    flat = jnp.sum(parts_ref[...], axis=0)
+    dates, sets = total_ref.shape
+    for t in range(dates):
+        total_ref[t : t + 1, :] = flat[:, t * sets : (t + 1) * sets]
+
+
+def total_of(parts, shape):
+    return pl.pallas_call(
+        total_kernel,
+        in_specs=[ON_CHIP],
+        out_specs=ON_CHIP,
+        out_shape=jax.ShapeDtypeStruct(shape, parts.dtype),
+        name="total",
+    )(parts)
 
 
 CORE, ROW, NEAR, NEXT, FAR = 1, 2, 4, 8, 24
@@ -458,12 +498,10 @@
     prior_coefs = from_earlier(coefs[-LAG_MAX:])
     limits = tuple(a.reshape(1, -1) for a in (margin_lag, thresholds, transfer_min))
     exposure, early, profile = later_exposures(limits, coefs, features, paths_all)
-    exposure, profile = first_exposures(
+    exposure, parts = first_exposures(
         limits, prior_coefs, prior_features, early, profile, exposure, paths_all
     )
-    for step in (CORE, ROW, NEAR, NEXT, FAR):
-        profile = profile + swapped(profile, step)
-    return exposure, profile
+    return exposure, total_of(lax.all_to_all(parts, "path", 0, 0, tiled=True), profile.shape)
 
 
 def solution(mesh):

time: 98 us -> 90.9 us (0.928); the launches traced: 97.7 us -> 89.5 us
  blocking collectives: 0 us -> 16.2 us
  waiting for transfers between devices: 24.4 us -> 14.1 us
  starting transfers between devices: 33.1 us -> 24.7 us
  Pallas kernels: 37.5 us -> 32.6 us
    all_to_all x0 -> x1, blocking collectives: none -> 16.2 us  [local(): lax.all_to_all(parts, 'path', 0, 0, tiled=True)]
    ppermute x13 -> x8, waiting for transfers between devices: 24.4 us -> 14.1 us  [swapped(): lax.ppermute(value, 'path', [(i, i ^ step) for i in range(lax.axis_size('...]
    ppermute x13 -> x8, starting transfers between devices: 24.3 us -> 15.7 us  [swapped(): lax.ppermute(value, 'path', [(i, i ^ step) for i in range(lax.axis_size('...]
    pallas_call x1, Pallas kernels: 10.9 us -> 3.95 us  [solved(): pl.pallas_call(functools.partial(solve_kernel, paths_all), in_specs=[ON_C...]
    pallas_call x0 -> x1, Pallas kernels: none -> 1.56 us  [total_of(): pl.pallas_call(total_kernel, in_specs=[ON_CHIP], out_specs=ON_CHIP, out_s...]
  transfers between devices with their start and end apart: 15 -> 10, of which waited for: 12 -> 7; matrix products, arithmetic and copies ran while one was open for 0% -> 0% of each run, Pallas kernels for 25% -> 28%
where the time goes in v4:
time: 90.9 us; the launch traced here: 89.5 us
  Pallas kernels  32.6 us (36%)
  starting transfers between devices  24.7 us (27%)
  blocking collectives  16.2 us (18%)
  waiting for transfers between devices  14.1 us (16%)
  local copies, waits for them, and re-layouts  1.02 us (1%)
    pallas_call x3, Pallas kernels, sums_of(): pl.pallas_call(sums_kernel, in_specs=[SCALARS] + [IN_HBM] * (len(args) -...  17.4 us
    all_to_all x1, blocking collectives, local(): lax.all_to_all(parts, 'path', 0, 0, tiled=True)  16.2 us
    ppermute x8, starting transfers between devices, swapped(): lax.ppermute(value, 'path', [(i, i ^ step) for i in range(lax.axis_size('...  15.7 us
    ppermute x8, waiting for transfers between devices, swapped(): lax.ppermute(value, 'path', [(i, i ^ step) for i in range(lax.axis_size('...  14.1 us
    ppermute x2, starting transfers between devices, from_earlier(): return lax.ppermute(value, 'date', [(i, i + 1) for i in range(length - 1)])  8.99 us
    pallas_call x1, Pallas kernels, later_exposures(): pl.pallas_call(functools.partial(later_kernel, paths_all), in_specs=[ON_C...  5.41 us
    pallas_call x1, Pallas kernels, solved(): pl.pallas_call(functools.partial(solve_kernel, paths_all), in_specs=[ON_C...  3.95 us
    pallas_call x1, Pallas kernels, features_of(): pl.pallas_call(features_kernel, in_specs=[ON_CHIP, ON_CHIP, ON_CHIP], out...  2.25 us
  transfers between devices with their start and end apart: 10, of which 7 were waited for; matrix products, arithmetic and copies ran while one was open for 0% of the time, Pallas kernels for 28%

profile of v4, /device:TPU:2, one launch (start us, length us, event | category | flops | bytes accessed | tf_op | source)
XLA Modules:
  0.0 89.5 jit_solution(1474679851993260487)
XLA Ops:
  0.6 1.0 %slice.6 = bf16[2,16,4096]{2,1,0:T(8,128)(2,1)S(1)} slice(bf16[8,16,4096]{2,1,0:T(8,128)(2,1)} %factors_ref.5), slice={[6:8], [0:16], [0:4096]} | slice | bytes 524288 | tf_op jit(solution)/shard_map/slice | solution.py:478
  1.6 5.1 %collective-permute-start = (bf16[2,16,4096]{2,1,0:T(8,128)(2,1)S(1)}, bf16[2,16,4096]{2,1,0:T(8,128)(2,1)S(1)}, u32[]{:S(2)}, u32[]{:S(2)}) collective-permute-start(bf16[2,16,4096]{2,1,0:T(8,128)(2,1)S(1)} %slice.6), channel_id=1, source_target_pairs={{0,32},{32,64},{64,96},{96,128},{128,160},{160,192},{192,224},{1,3... | collective-permute-start | bytes 786440 | tf_op jit(solution)/shard_map/ppermute | solution.py:468
  6.7 8.1 %sums.3 = (bf16[8,128,4096]{2,1,0:T(8,128)(2,1)}, f32[4,192,128]{2,1,0:T(8,128)S(1)}) custom-call(s32[1]{0:T(128)} %bitcast.7.first_ref, bf16[16,128]{1,0:T(8,128)(2,1)} %bitcast.29, f32[1,128]{1,0:T(1,128)} %bitcast.33, bf16[8,16,4096]{2,1,0:T(8,128)(2,1)} %factors_ref.5, bf16[8,64,4096]{2,1,0:T(8,128)(2,1)} %flows_ref.5), custom_call_target="tpu_custom_call" | custom-call | flops 41943040000 | bytes 8388608 | tf_op jit(solution)/shard_map/sums/pallas_call | solution.py:187
  14.8 0.1 collective-permute-start.1
  14.9 0.0 collective-permute-done.factors_ref
  15.0 4.6 %sums.4 = (bf16[8,128,4096]{2,1,0:T(8,128)(2,1)}, f32[2,192,128]{2,1,0:T(8,128)S(1)}) custom-call(s32[1]{0:T(128)} %bitcast.6.first_ref, bf16[16,128]{1,0:T(8,128)(2,1)} %bitcast.30, f32[1,128]{1,0:T(1,128)} %bitcast.34, bf16[8,16,4096]{2,1,0:T(8,128)(2,1)} %factors_ref.5, bf16[8,64,4096]{2,1,0:T(8,128)(2,1)} %flows_ref.5, ...), custom_call_target="tpu_custom_call", output_to_operand_aliasing={{0}: (5, {})} | custom-call | flops 20971520000 | bytes 4194304 | tf_op jit(solution)/shard_map/sums/pallas_call | solution.py:187
  19.6 0.0 collective-permute-done.1
  19.7 0.9 %collective-permute-start.2 = (f32[2,192,128]{2,1,0:T(8,128)S(1)}, f32[2,192,128]{2,1,0:T(8,128)S(1)}, u32[]{:S(2)}, u32[]{:S(2)}) collective-permute-start(f32[2,192,128]{2,1,0:T(8,128)S(1)} %bitcast_add_fusion), channel_id=1, source_target_pairs={{0,2},{1,3},{2,0},{3,1},{4,6},{5,7},{6,4},{7,5},{8,10},{9,11},{10,... | collective-permute-start | bytes 589832 | tf_op jit(solution)/shard_map/ppermute | solution.py:452
  20.6 0.0 copy-start.3
  20.6 0.0 copy-start.4
  20.6 4.7 %sums.5 = (bf16[8,128,4096]{2,1,0:T(8,128)(2,1)}, f32[2,192,128]{2,1,0:T(8,128)S(1)}) custom-call(s32[1]{0:T(128)} %bitcast.3.first_ref, bf16[16,128]{1,0:T(8,128)(2,1)} %bitcast.31, f32[1,128]{1,0:T(1,128)} %bitcast.35, bf16[8,16,4096]{2,1,0:T(8,128)(2,1)} %factors_ref.5, bf16[8,64,4096]{2,1,0:T(8,128)(2,1)} %flows_ref.5, ...), custom_call_target="tpu_custom_call", output_to_operand_aliasing={{0}: (5, {})} | custom-call | flops 20971520000 | bytes 4194304 | tf_op jit(solution)/shard_map/sums/pallas_call | solution.py:187
  25.3 1.9 %collective-permute-done.2 = f32[2,192,128]{2,1,0:T(8,128)S(1)} collective-permute-done((f32[2,192,128]{2,1,0:T(8,128)S(1)}, f32[2,192,128]{2,1,0:T(8,128)S(1)}, u32[]{:S(2)}, u32[]{:S(2)}) %collective-permute-start.2) | collective-permute-done | bytes 196640 | tf_op jit(solution)/shard_map/ppermute | solution.py:452
  27.3 2.0 %collective-permute-start.3 = (f32[192,128]{1,0:T(8,128)S(1)}, f32[192,128]{1,0:T(8,128)S(1)}, u32[]{:S(2)}, u32[]{:S(2)}) collective-permute-start(f32[192,128]{1,0:T(8,128)S(1)} %dynamic-slice_bitcast_fusion), channel_id=1, source_target_pairs={{0,4},{1,5},{2,6},{3,7},{4,0},{5,1},{6,2},{7,3},{8,12},{9,13},{10,... | collective-permute-start | bytes 294920 | tf_op jit(solution)/shard_map/ppermute | solution.py:452
  29.3 2.7 %collective-permute-done.3 = f32[192,128]{1,0:T(8,128)S(1)} collective-permute-done((f32[192,128]{1,0:T(8,128)S(1)}, f32[192,128]{1,0:T(8,128)S(1)}, u32[]{:S(2)}, u32[]{:S(2)}) %collective-permute-start.3) | collective-permute-done | bytes 98336 | tf_op jit(solution)/shard_map/ppermute | solution.py:452
  32.0 0.0 copy-start
  32.0 0.0 copy-start.1
  32.0 0.0 copy-start.2
  32.0 3.4 %collective-permute-start.4 = (f32[192,128]{1,0:T(8,128)S(1)}, f32[192,128]{1,0:T(8,128)S(1)}, u32[]{:S(2)}, u32[]{:S(2)}) collective-permute-start(f32[192,128]{1,0:T(8,128)S(1)} %bitcast_add_fusion.2), channel_id=1, source_target_pairs={{0,8},{1,9},{2,10},{3,11},{4,12},{5,13},{6,14},{7,15},{8,0},{9,1},... | collective-permute-start | bytes 294920 | tf_op jit(solution)/shard_map/ppermute | solution.py:452
  35.4 0.0 copy-done.3
  35.4 0.0 copy-done.4
  35.4 2.3 %features.1.prior_features_ref = bf16[2,128,4096]{2,1,0:T(8,128)(2,1)S(1)} custom-call(bf16[16,128]{1,0:T(8,128)(2,1)S(1)} %bitcast.32, f32[1,128]{1,0:T(1,128)S(1)} %bitcast.36, bf16[2,16,4096]{2,1,0:T(8,128)(2,1)S(1)} %collective-permute-done.factors_ref), custom_call_target="tpu_custom_call" | custom-call | flops 2097152000 | bytes 2097152 | tf_op jit(solution)/shard_map/features/pallas_call | solution.py:166
  37.7 0.6 collective-permute-done.4
  38.3 5.9 %collective-permute-start.5 = (f32[192,128]{1,0:T(8,128)S(1)}, f32[192,128]{1,0:T(8,128)S(1)}, u32[]{:S(2)}, u32[]{:S(2)}) collective-permute-start(f32[192,128]{1,0:T(8,128)S(1)} %add.47.one_ref), channel_id=1, source_target_pairs={{0,24},{1,25},{2,26},{3,27},{4,28},{5,29},{6,30},{7,31},{8,16},{9,... | collective-permute-start | bytes 294920 | tf_op jit(solution)/shard_map/ppermute | solution.py:452
  44.1 2.7 %collective-permute-done.5.two_ref = f32[192,128]{1,0:T(8,128)S(1)} collective-permute-done((f32[192,128]{1,0:T(8,128)S(1)}, f32[192,128]{1,0:T(8,128)S(1)}, u32[]{:S(2)}, u32[]{:S(2)}) %collective-permute-start.5) | collective-permute-done | bytes 98336 | tf_op jit(solution)/shard_map/ppermute | solution.py:452
  46.8 3.9 %solve.1 = bf16[64,128]{1,0:T(8,128)(2,1)S(1)} custom-call(f32[192,128]{1,0:T(8,128)S(1)} %add.47.one_ref, f32[192,128]{1,0:T(8,128)S(1)} %collective-permute-done.5.two_ref), custom_call_target="tpu_custom_call" | custom-call | tf_op jit(solution)/shard_map/solve/pallas_call | solution.py:248
  50.7 2.5 %collective-permute-start.6 = (bf16[1,64,128]{2,1,0:T(8,128)(2,1)S(1)}, bf16[1,64,128]{2,1,0:T(8,128)(2,1)S(1)}, u32[]{:S(2)}, u32[]{:S(2)}) collective-permute-start(bf16[1,64,128]{2,1,0:T(8,128)(2,1)S(1)} %bitcast.22), channel_id=1, source_target_pairs={{0,4},{1,5},{2,6},{3,7},{4,0},{5,1},{6,2},{7,3},{8,12},{9,13},{10,... | collective-permute-start | bytes 49160 | tf_op jit(solution)/shard_map/ppermute | solution.py:452
  53.3 1.7 %collective-permute-done.6 = bf16[1,64,128]{2,1,0:T(8,128)(2,1)S(1)} collective-permute-done((bf16[1,64,128]{2,1,0:T(8,128)(2,1)S(1)}, bf16[1,64,128]{2,1,0:T(8,128)(2,1)S(1)}, u32[]{:S(2)}, u32[]{:S(2)}) %collective-permute-start.6) | collective-permute-done | bytes 16416 | tf_op jit(solution)/shard_map/ppermute | solution.py:452
  55.0 0.8 collective-permute-start.7
  55.8 3.2 %collective-permute-done.7 = bf16[2,64,128]{2,1,0:T(8,128)(2,1)S(1)} collective-permute-done((bf16[2,64,128]{2,1,0:T(8,128)(2,1)S(1)}, bf16[2,64,128]{2,1,0:T(8,128)(2,1)S(1)}, u32[]{:S(2)}, u32[]{:S(2)}) %collective-permute-start.7) | collective-permute-done | bytes 32800 | tf_op jit(solution)/shard_map/ppermute | solution.py:452
  59.1 0.1 collective-permute-start.8
  59.2 1.2 %collective-permute-done.8 = bf16[4,64,128]{2,1,0:T(8,128)(2,1)S(1)} collective-permute-done((bf16[4,64,128]{2,1,0:T(8,128)(2,1)S(1)}, bf16[4,64,128]{2,1,0:T(8,128)(2,1)S(1)}, u32[]{:S(2)}, u32[]{:S(2)}) %collective-permute-start.8) | collective-permute-done | bytes 65568 | tf_op jit(solution)/shard_map/ppermute | solution.py:452
  60.5 3.9 %collective-permute-start.9 = (bf16[2,64,128]{2,1,0:T(8,128)(2,1)S(1)}, bf16[2,64,128]{2,1,0:T(8,128)(2,1)S(1)}, u32[]{:S(2)}, u32[]{:S(2)}) collective-permute-start(bf16[2,64,128]{2,1,0:T(8,128)(2,1)S(1)} %slice.8), channel_id=1, source_target_pairs={{0,32},{32,64},{64,96},{96,128},{128,160},{160,192},{192,224},{1,3... | collective-permute-start | bytes 98312 | tf_op jit(solution)/shard_map/ppermute | solution.py:468
  64.3 0.0 copy-done
  64.4 0.0 copy-done.1
  64.4 0.0 copy-done.2
  64.4 5.4 %later.1 = (bf16[8,64,4096]{2,1,0:T(8,128)(2,1)}, bf16[2,64,4096]{2,1,0:T(8,128)(2,1)S(1)}, f32[8,64]{1,0:T(8,128)S(1)}) custom-call(s32[1,64]{1,0:T(1,128)S(1)} %bitcast.23, s32[1,64]{1,0:T(1,128)S(1)} %bitcast.25, s32[1,64]{1,0:T(1,128)S(1)} %bitcast.27, bf16[8,64,128]{2,1,0:T(8,128)(2,1)S(1)} %pad_maximum_fusion.coefs_ref, ...), custom_call_target="tpu_custom_call" | custom-call | flops 53687091200 | bytes 12582912 | tf_op jit(solution)/shard_map/later/pallas_call | solution.py:385
  69.8 0.0 collective-permute-done.9.prior_coefs_ref
  69.8 2.0 %first.1 = (bf16[8,64,4096]{2,1,0:T(8,128)(2,1)}, f32[32,1,512]{2,1,0:T(1,128)S(1)}) custom-call(s32[1,64]{1,0:T(1,128)S(1)} %bitcast.24, s32[1,64]{1,0:T(1,128)S(1)} %bitcast.26, s32[1,64]{1,0:T(1,128)S(1)} %bitcast.28, bf16[2,64,128]{2,1,0:T(8,128)(2,1)S(1)} %collective-permute-done.9.prior_coefs_ref, ...), custom_call_target="tpu_custom_call", output_to_operand_aliasing={{0}: (7, {})} | custom-call | tf_op jit(solution)/shard_map/first/pallas_call | solution.py:413
  71.8 16.2 %all_to_all.5.parts_ref = f32[32,1,512]{2,1,0:T(1,128)} all-to-all(f32[32,1,512]{2,1,0:T(1,128)S(1)} %get-tuple-element.31), channel_id=1, replica_groups=mesh['date'=8,'path'=32] {'path'}, dimensions={0} | all-to-all | bytes 131072 | tf_op jit(solution)/shard_map/all_to_all | solution.py:504
  87.9 1.6 %total.1 = f32[8,64]{1,0:T(8,128)} custom-call(f32[32,1,512]{2,1,0:T(1,128)} %all_to_all.5.parts_ref), custom_call_target="tpu_custom_call" | custom-call | tf_op jit(solution)/shard_map/total/pallas_call | solution.py:439
  (12 shorter events, 0.2 us)
Async XLA Ops:
  1.6 13.3 %collective-permute-start = (bf16[2,16,4096]{2,1,0:T(8,128)(2,1)S(1)}, bf16[2,16,4096]{2,1,0:T(8,128)(2,1)S(1)}, u32[]{:S(2)}, u32[]{:S(2)}) collective-permute-start(bf16[2,16,4096]{2,1,0:T(8,128)(2,1)S(1)} %slice.6), channel_id=1, source_target_pairs={{0,32},{32,64},{64,96},{96,128},{128,160},{160,192},{192,224},{1,3... | collective-permute-start | bytes 786440 | tf_op jit(solution)/shard_map/ppermute | solution.py:468
  14.8 4.8 %collective-permute-start.1 = (f32[4,192,128]{2,1,0:T(8,128)S(1)}, f32[4,192,128]{2,1,0:T(8,128)S(1)}, u32[]{:S(2)}, u32[]{:S(2)}) collective-permute-start(f32[4,192,128]{2,1,0:T(8,128)S(1)} %get-tuple-element.21), channel_id=1, source_target_pairs={{0,1},{1,0},{2,3},{3,2},{4,5},{5,4},{6,7},{7,6},{8,9},{9,8},{10,11... | collective-permute-start | bytes 1179656 | tf_op jit(solution)/shard_map/ppermute | solution.py:452
  19.7 7.6 %collective-permute-start.2 = (f32[2,192,128]{2,1,0:T(8,128)S(1)}, f32[2,192,128]{2,1,0:T(8,128)S(1)}, u32[]{:S(2)}, u32[]{:S(2)}) collective-permute-start(f32[2,192,128]{2,1,0:T(8,128)S(1)} %bitcast_add_fusion), channel_id=1, source_target_pairs={{0,2},{1,3},{2,0},{3,1},{4,6},{5,7},{6,4},{7,5},{8,10},{9,11},{10,... | collective-permute-start | bytes 589832 | tf_op jit(solution)/shard_map/ppermute | solution.py:452
  20.6 14.8 %copy-start.3 = (bf16[128,16]{0,1:T(8,128)(2,1)S(1)}, bf16[128,16]{0,1:T(8,128)(2,1)}, u32[]{:S(2)}) copy-start(bf16[128,16]{0,1:T(8,128)(2,1)} %param.9) | copy-start | bytes 12292
  20.6 14.8 %copy-start.4 = (f32[128]{0:T(128)S(1)}, f32[128]{0:T(128)}, u32[]{:S(2)}) copy-start(f32[128]{0:T(128)} %param.10) | copy-start | bytes 1540
  27.3 4.7 %collective-permute-start.3 = (f32[192,128]{1,0:T(8,128)S(1)}, f32[192,128]{1,0:T(8,128)S(1)}, u32[]{:S(2)}, u32[]{:S(2)}) collective-permute-start(f32[192,128]{1,0:T(8,128)S(1)} %dynamic-slice_bitcast_fusion), channel_id=1, source_target_pairs={{0,4},{1,5},{2,6},{3,7},{4,0},{5,1},{6,2},{7,3},{8,12},{9,13},{10,... | collective-permute-start | bytes 294920 | tf_op jit(solution)/shard_map/ppermute | solution.py:452
  32.0 32.4 %copy-start = (s32[64]{0:T(128)S(1)}, s32[64]{0:T(128)}, u32[]{:S(2)}) copy-start(s32[64]{0:T(128)} %param.11) | copy-start | bytes 772
  32.0 32.3 %copy-start.1 = (s32[64]{0:T(128)S(1)}, s32[64]{0:T(128)}, u32[]{:S(2)}) copy-start(s32[64]{0:T(128)} %param.12) | copy-start | bytes 772
  32.0 32.3 %copy-start.2 = (s32[64]{0:T(128)S(1)}, s32[64]{0:T(128)}, u32[]{:S(2)}) copy-start(s32[64]{0:T(128)} %param.13) | copy-start | bytes 772
  32.0 6.2 %collective-permute-start.4 = (f32[192,128]{1,0:T(8,128)S(1)}, f32[192,128]{1,0:T(8,128)S(1)}, u32[]{:S(2)}, u32[]{:S(2)}) collective-permute-start(f32[192,128]{1,0:T(8,128)S(1)} %bitcast_add_fusion.2), channel_id=1, source_target_pairs={{0,8},{1,9},{2,10},{3,11},{4,12},{5,13},{6,14},{7,15},{8,0},{9,1},... | collective-permute-start | bytes 294920 | tf_op jit(solution)/shard_map/ppermute | solution.py:452
  38.3 8.5 %collective-permute-start.5 = (f32[192,128]{1,0:T(8,128)S(1)}, f32[192,128]{1,0:T(8,128)S(1)}, u32[]{:S(2)}, u32[]{:S(2)}) collective-permute-start(f32[192,128]{1,0:T(8,128)S(1)} %add.47.one_ref), channel_id=1, source_target_pairs={{0,24},{1,25},{2,26},{3,27},{4,28},{5,29},{6,30},{7,31},{8,16},{9,... | collective-permute-start | bytes 294920 | tf_op jit(solution)/shard_map/ppermute | solution.py:452
  50.7 4.3 %collective-permute-start.6 = (bf16[1,64,128]{2,1,0:T(8,128)(2,1)S(1)}, bf16[1,64,128]{2,1,0:T(8,128)(2,1)S(1)}, u32[]{:S(2)}, u32[]{:S(2)}) collective-permute-start(bf16[1,64,128]{2,1,0:T(8,128)(2,1)S(1)} %bitcast.22), channel_id=1, source_target_pairs={{0,4},{1,5},{2,6},{3,7},{4,0},{5,1},{6,2},{7,3},{8,12},{9,13},{10,... | collective-permute-start | bytes 49160 | tf_op jit(solution)/shard_map/ppermute | solution.py:452
  55.0 4.0 %collective-permute-start.7 = (bf16[2,64,128]{2,1,0:T(8,128)(2,1)S(1)}, bf16[2,64,128]{2,1,0:T(8,128)(2,1)S(1)}, u32[]{:S(2)}, u32[]{:S(2)}) collective-permute-start(bf16[2,64,128]{2,1,0:T(8,128)(2,1)S(1)} %pad_maximum_fusion.2), channel_id=1, source_target_pairs={{0,2},{1,3},{2,0},{3,1},{4,6},{5,7},{6,4},{7,5},{8,10},{9,11},{10,... | collective-permute-start | bytes 98312 | tf_op jit(solution)/shard_map/ppermute | solution.py:452
  59.1 1.3 %collective-permute-start.8 = (bf16[4,64,128]{2,1,0:T(8,128)(2,1)S(1)}, bf16[4,64,128]{2,1,0:T(8,128)(2,1)S(1)}, u32[]{:S(2)}, u32[]{:S(2)}) collective-permute-start(bf16[4,64,128]{2,1,0:T(8,128)(2,1)S(1)} %pad_maximum_fusion.1), channel_id=1, source_target_pairs={{0,1},{1,0},{2,3},{3,2},{4,5},{5,4},{6,7},{7,6},{8,9},{9,8},{10,11... | collective-permute-start | bytes 196616 | tf_op jit(solution)/shard_map/ppermute | solution.py:452
  60.5 9.3 %collective-permute-start.9 = (bf16[2,64,128]{2,1,0:T(8,128)(2,1)S(1)}, bf16[2,64,128]{2,1,0:T(8,128)(2,1)S(1)}, u32[]{:S(2)}, u32[]{:S(2)}) collective-permute-start(bf16[2,64,128]{2,1,0:T(8,128)(2,1)S(1)} %slice.8), channel_id=1, source_target_pairs={{0,32},{32,64},{64,96},{96,128},{128,160},{160,192},{192,224},{1,3... | collective-permute-start | bytes 98312 | tf_op jit(solution)/shard_map/ppermute | solution.py:468

commit v5 on v4

--- a/solution.py
+++ b/solution.py
@@ -56,35 +56,29 @@
     return total.astype(jnp.bfloat16)
 
 
-def features_kernel(freq_ref, phase_ref, factors_ref, features_ref):
-    weights = turn_weights(freq_ref, phase_ref)
+def features_kernel(weights_ref, factors_ref, features_ref):
     for i in range(factors_ref.shape[0]):
         for at in range(0, factors_ref.shape[2], CHUNK):
             span = pl.ds(at, CHUNK)
-            features_ref[i, :, span] = cosines(chunk_turns(weights, factors_ref[i, :, span]))
-
-
-def sums_kernel(first_ref, freq_ref, phase_ref, factors_ref, flows_ref, *refs):
-    (
-        features_ref,
-        sums_ref,
-        freq_here,
-        phase_here,
-        factors_here,
-        flows_here,
-        features_here,
-        weight_sems,
-        factor_sems,
-        flow_sems,
-        feature_sems,
-    ) = refs[-11:]
-    dates, _, paths = factors_here.shape
-    small = (
-        pltpu.make_async_copy(freq_ref, freq_here, weight_sems.at[0]),
-        pltpu.make_async_copy(phase_ref, phase_here, weight_sems.at[1]),
-    )
-    for copy in small:
-        copy.start()
+            features_ref[i, :, span] = cosines(
+                chunk_turns(weights_ref[...], factors_ref[i, :, span])
+            )
+
+
+def sums_kernel(first_ref, *refs):
+    *given, factors_ref, flows_ref = refs[: -6 if len(refs) == 9 else -10]
+    if len(given) == 1:
+        features_ref, sums_ref, factors_here, flows_here, factor_sems, flow_sems = refs[-6:]
+    else:
+        features_ref, sums_ref, weights_out_ref, freq_here, phase_here = refs[-10:-5]
+        factors_here, flows_here, factor_sems, flow_sems, weight_sems = refs[-5:]
+        small = [
+            pltpu.make_async_copy(source, here, weight_sems.at[i])
+            for i, (source, here) in enumerate(zip(given, (freq_here, phase_here)))
+        ]
+        for copy in small:
+            copy.start()
+    dates, _, paths = features_ref.shape
     ats = [first_ref[0] + i for i in range(dates)]
     factor_loads = [
         pltpu.make_async_copy(factors_ref.at[t], factors_here.at[i], factor_sems.at[i])
@@ -97,11 +91,15 @@
     for pair in zip(factor_loads, flow_loads):
         for copy in pair:
             copy.start()
-    for copy in small:
-        copy.wait()
-    weights = turn_weights(freq_here, phase_here)
+    if len(given) == 1:
+        weights = given[0][...]
+    else:
+        for copy in small:
+            copy.wait()
+        weights = turn_weights(freq_here, phase_here)
+        weights_out_ref[...] = weights
     items = [(i, pl.ds(at, CHUNK)) for i in range(dates) for at in range(0, paths, CHUNK)]
-    arrived, joined, saves = set(), set(), []
+    arrived, joined = set(), set()
 
     def turns_of(item):
         i, span = item
@@ -133,18 +131,8 @@
         if at < len(items):
             i, span = items[at]
             feats = cosines(turns)
-            features_here[i, :, span] = feats
-            saves.append(
-                pltpu.make_async_copy(
-                    features_here.at[i, :, span],
-                    features_ref.at[ats[i], :, span],
-                    feature_sems.at[at],
-                )
-            )
-            saves[-1].start()
+            features_ref[i, :, span] = feats
             turns = later
-    for copy in saves:
-        copy.wait()
 
 
 ON_CHIP = pl.BlockSpec(memory_space=pltpu.VMEM)
@@ -160,12 +148,12 @@
     return pltpu.CompilerParams(vmem_limit_bytes=mebibytes << 20)
 
 
-def features_of(frequency, phases, factors):
+def features_of(weights, factors):
     dates, r, paths = factors.shape
-    k = frequency.shape[1]
+    k = weights.shape[0]
     return pl.pallas_call(
         features_kernel,
-        in_specs=[ON_CHIP, ON_CHIP, ON_CHIP],
+        in_specs=[ON_CHIP, ON_CHIP],
         out_specs=ON_CHIP,
         out_shape=jax.ShapeDtypeStruct((dates, k, paths), jnp.bfloat16),
         compiler_params=params(8),
@@ -173,43 +161,43 @@
             flops=2000 * dates * k * paths, bytes_accessed=2 * dates * k * paths, transcendentals=0
         ),
         name="features",
-    )(frequency, phases, factors)
-
-
-def sums_of(first, dates, frequency, phases, factors, flows, features=None):
-    dates_all, r, paths = factors.shape
-    k, sets = frequency.shape[1], flows.shape[1]
-    args = [first.reshape(1), *map(in_hbm, (frequency, phases, factors, flows))]
-    aliases = {}
-    if features is not None:
-        aliases[len(args)] = 0
-        args.append(in_hbm(features))
+    )(weights, factors)
+
+
+def sums_of(first, dates, given, factors, flows):
+    _, r, paths = factors.shape
+    k, sets = given[0].shape[len(given) - 1], flows.shape[1]
+    outs = [
+        jax.ShapeDtypeStruct((dates, k, paths), jnp.bfloat16),
+        jax.ShapeDtypeStruct((dates, k + sets, k), jnp.float32),
+    ]
+    scratch = [
+        pltpu.VMEM((dates, r, paths), jnp.bfloat16),
+        pltpu.VMEM((dates, sets, paths), jnp.bfloat16),
+        pltpu.SemaphoreType.DMA((dates,)),
+        pltpu.SemaphoreType.DMA((dates,)),
+    ]
+    specs = [ON_CHIP]
+    if len(given) == 2:
+        outs.append(jax.ShapeDtypeStruct((k, 4 * r), jnp.bfloat16))
+        scratch = [pltpu.VMEM(a.shape, a.dtype) for a in given] + scratch
+        scratch.append(pltpu.SemaphoreType.DMA((2,)))
+        specs = [IN_HBM, IN_HBM]
+        given = map(in_hbm, given)
     return pl.pallas_call(
         sums_kernel,
-        in_specs=[SCALARS] + [IN_HBM] * (len(args) - 1),
-        out_specs=(IN_HBM, ON_CHIP),
-        out_shape=(
-            pltpu.HBM((dates_all, k, paths), jnp.bfloat16),
-            jax.ShapeDtypeStruct((dates, k + sets, k), jnp.float32),
-        ),
-        scratch_shapes=[
-            pltpu.VMEM(frequency.shape, frequency.dtype),
-            pltpu.VMEM(phases.shape, phases.dtype),
-            pltpu.VMEM((dates, r, paths), jnp.bfloat16),
-            pltpu.VMEM((dates, sets, paths), jnp.bfloat16),
-            pltpu.VMEM((dates, k, paths), jnp.bfloat16),
-            pltpu.SemaphoreType.DMA((2,)),
-            pltpu.SemaphoreType.DMA((dates,)),
-            pltpu.SemaphoreType.DMA((dates,)),
-            pltpu.SemaphoreType.DMA((dates * (paths // CHUNK),)),
-        ],
-        input_output_aliases=aliases,
-        compiler_params=params(24),
+        in_specs=[SCALARS, *specs, IN_HBM, IN_HBM],
+        out_specs=(ON_CHIP,) * len(outs),
+        out_shape=tuple(outs),
+        scratch_shapes=scratch,
+        compiler_params=params(14),
         cost_estimate=pl.CostEstimate(
-            flops=20000 * dates * k * paths, bytes_accessed=4 * dates * k * paths, transcendentals=0
+            flops=20000 * dates * k * paths,
+            bytes_accessed=4 * dates * k * paths,
+            transcendentals=0,
         ),
         name="sums",
-    )(*args)
+    )(first.reshape(1), *given, in_hbm(factors), in_hbm(flows))
 
 
 def solve_kernel(paths_all, one_ref, two_ref, out_ref):
@@ -293,37 +281,25 @@
 
 def later_kernel(
     paths_all,
+    parts,
+    firsts_ref,
     lag_ref,
     threshold_ref,
     transfer_ref,
     coefs_ref,
-    features_ref,
-    exposure_ref,
-    early_ref,
-    profile_ref,
-    features_here,
-    values_ref,
-    staged_ref,
-    feature_sems,
-    sems,
+    *refs,
 ):
+    exposure_ref, early_ref, profile_ref, values_ref, staged_ref, sems = refs[parts:]
     dates, sets, paths = values_ref.shape
     spans = [pl.ds(at, CHUNK) for at in range(0, paths, CHUNK)]
-    loads = [
-        pltpu.make_async_copy(features_ref.at[t], features_here.at[t], feature_sems.at[t])
-        for t in range(dates)
-    ]
-    for copy in loads:
-        copy.start()
+    for part, features_ref in enumerate(refs[:parts]):
+        for i in range(features_ref.shape[0]):
+            t = firsts_ref[part] + i
+            for span in spans:
+                values_ref[t, :, span] = value_of(coefs_ref[t], features_ref[i, :, span])
     offset, recent = limits_of(lag_ref, threshold_ref, transfer_ref)
     totals, copies = {}, []
-    for t in range(dates):
-        loads[t].wait()
-        for span in spans:
-            values_ref[t, :, span] = value_of(coefs_ref[t], features_here[t, :, span])
-        if t < LAG_MAX:
-            early_ref[t] = values_ref[t]
-            continue
+    for t in range(LAG_MAX, dates):
         totals[t] = jnp.zeros((sets, 128), jnp.float32)
         for span in spans:
             exposed = exposed_of(
@@ -334,6 +310,7 @@
         at = t - LAG_MAX
         copies.append(pltpu.make_async_copy(staged_ref.at[at], exposure_ref.at[t], sems.at[at]))
         copies[-1].start()
+    early_ref[...] = values_ref[:LAG_MAX]
     profile_ref[...] = profile_of(totals, paths_all, dates)
     for copy in copies:
         copy.wait()
@@ -379,12 +356,12 @@
         copy.wait()
 
 
-def later_exposures(limits, coefs, features, paths_all):
-    dates, k, paths = features.shape
-    sets = coefs.shape[1]
-    return pl.pallas_call(
-        functools.partial(later_kernel, paths_all),
-        in_specs=[ON_CHIP] * (len(limits) + 1) + [IN_HBM],
+def later_exposures(firsts, limits, coefs, parts, paths_all):
+    dates, sets, k = coefs.shape
+    paths = parts[0].shape[2]
+    return pl.pallas_call(
+        functools.partial(later_kernel, paths_all, len(parts)),
+        in_specs=[SCALARS] + [ON_CHIP] * (len(limits) + 1 + len(parts)),
         out_specs=(IN_HBM, ON_CHIP, ON_CHIP),
         out_shape=(
             pltpu.HBM((dates, sets, paths), jnp.bfloat16),
@@ -392,20 +369,18 @@
             jax.ShapeDtypeStruct((dates, sets), jnp.float32),
         ),
         scratch_shapes=[
-            pltpu.VMEM((dates, k, paths), jnp.bfloat16),
             pltpu.VMEM((dates, sets, paths), jnp.bfloat16),
             pltpu.VMEM((dates - LAG_MAX, sets, paths), jnp.bfloat16),
-            pltpu.SemaphoreType.DMA((dates,)),
             pltpu.SemaphoreType.DMA((dates - LAG_MAX,)),
         ],
-        compiler_params=params(32),
+        compiler_params=params(20),
         cost_estimate=pl.CostEstimate(
             flops=200 * dates * k * sets * paths,
             bytes_accessed=2 * dates * (k + sets) * paths,
             transcendentals=0,
         ),
         name="later",
-    )(*limits, coefs, in_hbm(features))
+    )(firsts, *limits, coefs, *parts)
 
 
 def first_exposures(limits, prior_coefs, prior_features, early, profile, exposure, paths_all):
@@ -452,15 +427,15 @@
     return lax.ppermute(value, "path", [(i, i ^ step) for i in range(lax.axis_size("path"))])
 
 
-def picked(value, at):
-    return lax.dynamic_index_in_dim(value, at, 0, keepdims=False)
-
-
-def doubled(value, step, bit):
+def picked(value, low):
+    return jnp.where(low, value[0], value[1])
+
+
+def doubled(value, step, low):
     other = swapped(value, step)
-    low = jnp.where(bit == 0, value, other)
-    high = jnp.where(bit == 0, other, value)
-    return jnp.concatenate([low, high], axis=0)
+    first = jnp.where(low, value, other)
+    second = jnp.where(low, other, value)
+    return jnp.concatenate([first, second], axis=0)
 
 
 def from_earlier(value):
@@ -470,34 +445,37 @@
 
 def local(factors, cashflows, frequency, phases, margin_lag, thresholds, transfer_min):
     paths_all = factors.shape[2] * lax.axis_size("path")
-    me = lax.axis_index("path")
-    core, row, near = me & 1, (me >> 1) & 1, (me >> 2) & 1
+    me = lax.axis_index("path").astype(jnp.uint32)
+    core, row, near = (((me >> bit) & 1).astype(jnp.int32) for bit in range(3))
     half = factors.shape[0] // 2
     quarter = half // 2
     firsts = (half * (1 - core), half * core + quarter * (1 - row), half * core + quarter * row)
+    scalars = (*firsts, jnp.stack(firsts), core == 0, row == 0, near == 0)
+    first_a, first_b, first_c, firsts, core_low, row_low, near_low = lax.optimization_barrier(
+        scalars
+    )
     prior_factors = from_earlier(factors[-LAG_MAX:])
-    phases = phases.reshape(1, -1)
-    frequency = frequency.T
-    features, sums_a = sums_of(firsts[0], half, frequency, phases, factors, cashflows)
+    given = (frequency.T, phases.reshape(1, -1))
+    part_a, sums_a, weights = sums_of(first_a, half, given, factors, cashflows)
     from_core = swapped(sums_a, CORE).reshape(2, quarter, *sums_a.shape[1:])
-    first_b, prior_factors = lax.optimization_barrier((firsts[1], prior_factors))
-    features, sums_b = sums_of(
-        first_b, quarter, frequency, phases, factors, cashflows, features
-    )
-    from_row = swapped(sums_b + picked(from_core, 1 - row), ROW)
-    features, sums_c = sums_of(firsts[2], quarter, frequency, phases, factors, cashflows, features)
-    kept = sums_c + picked(from_core, row) + from_row
-    kept = picked(kept, near) + swapped(picked(kept, 1 - near), NEAR)
+    first_b, prior_factors = lax.optimization_barrier((first_b, prior_factors))
+    part_b, sums_b = sums_of(first_b, quarter, (weights,), factors, cashflows)
+    from_row = swapped(sums_b + picked(from_core[::-1], row_low), ROW)
+    part_c, sums_c = sums_of(first_c, quarter, (weights,), factors, cashflows)
+    kept = sums_c + picked(from_core, row_low) + from_row
+    kept = picked(kept, near_low) + swapped(picked(kept[::-1], near_low), NEAR)
     kept = kept + swapped(kept, NEXT)
-    prior_features = features_of(frequency, phases, prior_factors)
+    prior_features = features_of(weights, prior_factors)
     kept, prior_features = lax.optimization_barrier((kept, prior_features))
     coefs = solved(kept, swapped(kept, FAR), paths_all)
-    coefs = doubled(coefs[None], NEAR, near)
-    coefs = doubled(coefs, ROW, row)
-    coefs = doubled(coefs, CORE, core)
+    coefs = doubled(coefs[None], NEAR, near_low)
+    coefs = doubled(coefs, ROW, row_low)
+    coefs = doubled(coefs, CORE, core_low)
     prior_coefs = from_earlier(coefs[-LAG_MAX:])
     limits = tuple(a.reshape(1, -1) for a in (margin_lag, thresholds, transfer_min))
-    exposure, early, profile = later_exposures(limits, coefs, features, paths_all)
+    exposure, early, profile = later_exposures(
+        firsts, limits, coefs, (part_a, part_b, part_c), paths_all
+    )
     exposure, parts = first_exposures(
         limits, prior_coefs, prior_features, early, profile, exposure, paths_all
     )

time: 90.9 us -> 88.1 us (0.969)
  Pallas kernels: 32.6 us -> 28.7 us
  starting transfers between devices: 24.7 us -> 25.7 us
    pallas_call x5, Pallas kernels: 25.1 us -> 21.2 us  [the longest x3 14.3 us: sums_of(): pl.pallas_call(sums_kernel, in_specs=[SCALARS, *specs, IN_HBM, IN_HBM], o...]
    ppermute x8, starting transfers between devices: 15.7 us -> 16.8 us  [swapped(): lax.ppermute(value, 'path', [(i, i ^ step) for i in range(lax.axis_size('...]
  transfers between devices with their start and end apart: 10 -> 10, of which waited for: 7 -> 8; matrix products, arithmetic and copies ran while one was open for 0% -> 0% of each run, Pallas kernels for 28% -> 24%
where the time goes in v5:
time: 88.1 us; the launch traced here: 86.7 us
  Pallas kernels  28.7 us (33%)
  starting transfers between devices  25.7 us (29%)
  blocking collectives  16.2 us (18%)
  waiting for transfers between devices  14 us (16%)
  local copies, waits for them, and re-layouts  0.99 us (1%)
    ppermute x8, starting transfers between devices, swapped(): lax.ppermute(value, 'path', [(i, i ^ step) for i in range(lax.axis_size('...  16.8 us
    all_to_all x1, blocking collectives, local(): lax.all_to_all(parts, 'path', 0, 0, tiled=True)  16.2 us
    pallas_call x3, Pallas kernels, sums_of(): pl.pallas_call(sums_kernel, in_specs=[SCALARS, *specs, IN_HBM, IN_HBM], o...  14.3 us
    ppermute x8, waiting for transfers between devices, swapped(): lax.ppermute(value, 'path', [(i, i ^ step) for i in range(lax.axis_size('...  13.9 us
    ppermute x2, starting transfers between devices, from_earlier(): return lax.ppermute(value, 'date', [(i, i + 1) for i in range(length - 1)])  8.93 us
    pallas_call x1, Pallas kernels, later_exposures(): pl.pallas_call(functools.partial(later_kernel, paths_all, len(parts)), in...  4.71 us
    pallas_call x1, Pallas kernels, solved(): pl.pallas_call(functools.partial(solve_kernel, paths_all), in_specs=[ON_C...  3.95 us
    pallas_call x1, Pallas kernels, features_of(): pl.pallas_call(features_kernel, in_specs=[ON_CHIP, ON_CHIP], out_specs=ON...  2.16 us
  transfers between devices with their start and end apart: 10, of which 8 were waited for; matrix products, arithmetic and copies ran while one was open for 0% of the time, Pallas kernels for 24%

profile of v5, /device:TPU:2, one launch (start us, length us, event | category | flops | bytes accessed | tf_op | source)
XLA Modules:
  0.0 86.7 jit_solution(16731152644221228865)
XLA Ops:
  0.6 1.0 %slice.32 = bf16[2,16,4096]{2,1,0:T(8,128)(2,1)S(1)} slice(bf16[8,16,4096]{2,1,0:T(8,128)(2,1)} %refs_1_.3), slice={[6:8], [0:16], [0:4096]} | slice | bytes 524288 | tf_op jit(solution)/shard_map/slice | solution.py:457
  1.6 5.1 %collective-permute-start.1 = (bf16[2,16,4096]{2,1,0:T(8,128)(2,1)S(1)}, bf16[2,16,4096]{2,1,0:T(8,128)(2,1)S(1)}, u32[]{:S(2)}, u32[]{:S(2)}) collective-permute-start(bf16[2,16,4096]{2,1,0:T(8,128)(2,1)S(1)} %slice.32), channel_id=1, source_target_pairs={{0,32},{32,64},{64,96},{96,128},{128,160},{160,192},{192,224},{1,3... | collective-permute-start | bytes 786440 | tf_op jit(solution)/shard_map/ppermute | solution.py:443
  6.7 0.1 pad_add_fusion.firsts_ref
  6.8 6.9 %sums.3 = (bf16[4,128,4096]{2,1,0:T(8,128)(2,1)S(1)}, f32[4,192,128]{2,1,0:T(8,128)S(1)}, bf16[128,64]{1,0:T(8,128)(2,1)S(1)}) custom-call(s32[1]{0:T(128)} %bitcast.7.first_ref, bf16[16,128]{1,0:T(8,128)(2,1)} %bitcast.25, f32[1,128]{1,0:T(1,128)} %bitcast.26, bf16[8,16,4096]{2,1,0:T(8,128)(2,1)} %refs_1_.3, bf16[8,64,4096]{2,1,0:T(8,128)(2,1)} %refs_2_.5), custom_call_target="tpu_custom_call" | custom-call | flops 41943040000 | bytes 8388608 | tf_op jit(solution)/shard_map/sums/pallas_call | solution.py:187
  13.7 0.1 collective-permute-start
  13.8 0.2 collective-permute-done.1.factors_ref
  13.9 3.7 %sums.5 = (bf16[2,128,4096]{2,1,0:T(8,128)(2,1)S(1)}, f32[2,192,128]{2,1,0:T(8,128)S(1)}) custom-call(s32[1]{0:T(128)} %bitcast.10.first_ref, bf16[128,64]{1,0:T(8,128)(2,1)S(1)} %get-tuple-element.30.refs_0_.weights_ref, bf16[8,16,4096]{2,1,0:T(8,128)(2,1)} %refs_1_.3, bf16[8,64,4096]{2,1,0:T(8,128)(2,1)} %refs_2_.5), custom_call_target="tpu_custom_call" | custom-call | flops 20971520000 | bytes 4194304 | tf_op jit(solution)/shard_map/sums/pallas_call | solution.py:187
  17.7 0.0 collective-permute-done
  17.7 1.7 %collective-permute-start.2 = (f32[2,192,128]{2,1,0:T(8,128)S(1)}, f32[2,192,128]{2,1,0:T(8,128)S(1)}, u32[]{:S(2)}, u32[]{:S(2)}) collective-permute-start(f32[2,192,128]{2,1,0:T(8,128)S(1)} %select_add_fusion), channel_id=1, source_target_pairs={{0,2},{1,3},{2,0},{3,1},{4,6},{5,7},{6,4},{7,5},{8,10},{9,11},{10,... | collective-permute-start | bytes 589832 | tf_op jit(solution)/shard_map/ppermute | solution.py:427
  19.4 3.7 %sums.4 = (bf16[2,128,4096]{2,1,0:T(8,128)(2,1)S(1)}, f32[2,192,128]{2,1,0:T(8,128)S(1)}) custom-call(s32[1]{0:T(128)} %bitcast.6.first_ref, bf16[128,64]{1,0:T(8,128)(2,1)S(1)} %get-tuple-element.30.refs_0_.weights_ref, bf16[8,16,4096]{2,1,0:T(8,128)(2,1)} %refs_1_.3, bf16[8,64,4096]{2,1,0:T(8,128)(2,1)} %refs_2_.5), custom_call_target="tpu_custom_call" | custom-call | flops 20971520000 | bytes 4194304 | tf_op jit(solution)/shard_map/sums/pallas_call | solution.py:187
  23.2 1.8 %collective-permute-done.2 = f32[2,192,128]{2,1,0:T(8,128)S(1)} collective-permute-done((f32[2,192,128]{2,1,0:T(8,128)S(1)}, f32[2,192,128]{2,1,0:T(8,128)S(1)}, u32[]{:S(2)}, u32[]{:S(2)}) %collective-permute-start.2) | collective-permute-done | bytes 196640 | tf_op jit(solution)/shard_map/ppermute | solution.py:427
  25.0 2.0 %collective-permute-start.3 = (f32[192,128]{1,0:T(8,128)S(1)}, f32[192,128]{1,0:T(8,128)S(1)}, u32[]{:S(2)}, u32[]{:S(2)}) collective-permute-start(f32[192,128]{1,0:T(8,128)S(1)} %select_bitcast_fusion), channel_id=1, source_target_pairs={{0,4},{1,5},{2,6},{3,7},{4,0},{5,1},{6,2},{7,3},{8,12},{9,13},{10,... | collective-permute-start | bytes 294920 | tf_op jit(solution)/shard_map/ppermute | solution.py:427
  27.0 2.7 %collective-permute-done.3 = f32[192,128]{1,0:T(8,128)S(1)} collective-permute-done((f32[192,128]{1,0:T(8,128)S(1)}, f32[192,128]{1,0:T(8,128)S(1)}, u32[]{:S(2)}, u32[]{:S(2)}) %collective-permute-start.3) | collective-permute-done | bytes 98336 | tf_op jit(solution)/shard_map/ppermute | solution.py:427
  29.8 0.0 copy-start
  29.8 0.0 copy-start.1
  29.8 0.0 copy-start.2
  29.8 3.5 %collective-permute-start.4 = (f32[192,128]{1,0:T(8,128)S(1)}, f32[192,128]{1,0:T(8,128)S(1)}, u32[]{:S(2)}, u32[]{:S(2)}) collective-permute-start(f32[192,128]{1,0:T(8,128)S(1)} %bitcast_add_fusion), channel_id=1, source_target_pairs={{0,8},{1,9},{2,10},{3,11},{4,12},{5,13},{6,14},{7,15},{8,0},{9,1},... | collective-permute-start | bytes 294920 | tf_op jit(solution)/shard_map/ppermute | solution.py:427
  33.3 2.2 %features.1.prior_features_ref = bf16[2,128,4096]{2,1,0:T(8,128)(2,1)S(1)} custom-call(bf16[128,64]{1,0:T(8,128)(2,1)S(1)} %get-tuple-element.30.refs_0_.weights_ref, bf16[2,16,4096]{2,1,0:T(8,128)(2,1)S(1)} %collective-permute-done.1.factors_ref), custom_call_target="tpu_custom_call" | custom-call | flops 2097152000 | bytes 2097152 | tf_op jit(solution)/shard_map/features/pallas_call | solution.py:154
  35.5 0.5 collective-permute-done.4
  36.0 6.1 %collective-permute-start.5 = (f32[192,128]{1,0:T(8,128)S(1)}, f32[192,128]{1,0:T(8,128)S(1)}, u32[]{:S(2)}, u32[]{:S(2)}) collective-permute-start(f32[192,128]{1,0:T(8,128)S(1)} %add.27.one_ref), channel_id=1, source_target_pairs={{0,24},{1,25},{2,26},{3,27},{4,28},{5,29},{6,30},{7,31},{8,16},{9,... | collective-permute-start | bytes 294920 | tf_op jit(solution)/shard_map/ppermute | solution.py:427
  42.1 2.7 %collective-permute-done.5.two_ref = f32[192,128]{1,0:T(8,128)S(1)} collective-permute-done((f32[192,128]{1,0:T(8,128)S(1)}, f32[192,128]{1,0:T(8,128)S(1)}, u32[]{:S(2)}, u32[]{:S(2)}) %collective-permute-start.5) | collective-permute-done | bytes 98336 | tf_op jit(solution)/shard_map/ppermute | solution.py:427
  44.7 3.9 %solve.1 = bf16[64,128]{1,0:T(8,128)(2,1)S(1)} custom-call(f32[192,128]{1,0:T(8,128)S(1)} %add.27.one_ref, f32[192,128]{1,0:T(8,128)S(1)} %collective-permute-done.5.two_ref), custom_call_target="tpu_custom_call" | custom-call | tf_op jit(solution)/shard_map/solve/pallas_call | solution.py:236
  48.7 2.5 %collective-permute-start.6 = (bf16[1,64,128]{2,1,0:T(8,128)(2,1)S(1)}, bf16[1,64,128]{2,1,0:T(8,128)(2,1)S(1)}, u32[]{:S(2)}, u32[]{:S(2)}) collective-permute-start(bf16[1,64,128]{2,1,0:T(8,128)(2,1)S(1)} %bitcast.18), channel_id=1, source_target_pairs={{0,4},{1,5},{2,6},{3,7},{4,0},{5,1},{6,2},{7,3},{8,12},{9,13},{10,... | collective-permute-start | bytes 49160 | tf_op jit(solution)/shard_map/ppermute | solution.py:427
  51.2 1.7 %collective-permute-done.6 = bf16[1,64,128]{2,1,0:T(8,128)(2,1)S(1)} collective-permute-done((bf16[1,64,128]{2,1,0:T(8,128)(2,1)S(1)}, bf16[1,64,128]{2,1,0:T(8,128)(2,1)S(1)}, u32[]{:S(2)}, u32[]{:S(2)}) %collective-permute-start.6) | collective-permute-done | bytes 16416 | tf_op jit(solution)/shard_map/ppermute | solution.py:427
  53.0 0.8 collective-permute-start.7
  53.7 3.2 %collective-permute-done.7 = bf16[2,64,128]{2,1,0:T(8,128)(2,1)S(1)} collective-permute-done((bf16[2,64,128]{2,1,0:T(8,128)(2,1)S(1)}, bf16[2,64,128]{2,1,0:T(8,128)(2,1)S(1)}, u32[]{:S(2)}, u32[]{:S(2)}) %collective-permute-start.7) | collective-permute-done | bytes 32800 | tf_op jit(solution)/shard_map/ppermute | solution.py:427
  57.0 0.1 collective-permute-start.8
  57.1 1.2 %collective-permute-done.8 = bf16[4,64,128]{2,1,0:T(8,128)(2,1)S(1)} collective-permute-done((bf16[4,64,128]{2,1,0:T(8,128)(2,1)S(1)}, bf16[4,64,128]{2,1,0:T(8,128)(2,1)S(1)}, u32[]{:S(2)}, u32[]{:S(2)}) %collective-permute-start.8) | collective-permute-done | bytes 65568 | tf_op jit(solution)/shard_map/ppermute | solution.py:427
  58.4 3.8 %collective-permute-start.9 = (bf16[2,64,128]{2,1,0:T(8,128)(2,1)S(1)}, bf16[2,64,128]{2,1,0:T(8,128)(2,1)S(1)}, u32[]{:S(2)}, u32[]{:S(2)}) collective-permute-start(bf16[2,64,128]{2,1,0:T(8,128)(2,1)S(1)} %slice.40), channel_id=1, source_target_pairs={{0,32},{32,64},{64,96},{96,128},{128,160},{160,192},{192,224},{1,3... | collective-permute-start | bytes 98312 | tf_op jit(solution)/shard_map/ppermute | solution.py:443
  62.2 0.0 copy-done
  62.2 0.0 copy-done.1
  62.2 0.0 copy-done.2
  62.3 4.7 %later.1 = (bf16[8,64,4096]{2,1,0:T(8,128)(2,1)}, bf16[2,64,4096]{2,1,0:T(8,128)(2,1)S(1)}, f32[8,64]{1,0:T(8,128)S(1)}) custom-call(s32[3]{0:T(128)S(1)} %pad_add_fusion.firsts_ref, s32[1,64]{1,0:T(1,128)S(1)} %bitcast.19, s32[1,64]{1,0:T(1,128)S(1)} %bitcast.21, s32[1,64]{1,0:T(1,128)S(1)} %bitcast.23, bf16[8,64,128]{2,1,0:T(8,128)(2,1)S(1)} %pad_maximum_fusion.coefs_ref, ...), custom_call_target="tpu_custom_call" | custom-call | flops 53687091200 | bytes 12582912 | tf_op jit(solution)/shard_map/later/pallas_call | solution.py:362
  67.0 0.0 collective-permute-done.9.prior_coefs_ref
  67.0 2.0 %first.1 = (bf16[8,64,4096]{2,1,0:T(8,128)(2,1)}, f32[32,1,512]{2,1,0:T(1,128)S(1)}) custom-call(s32[1,64]{1,0:T(1,128)S(1)} %bitcast.20, s32[1,64]{1,0:T(1,128)S(1)} %bitcast.22, s32[1,64]{1,0:T(1,128)S(1)} %bitcast.24, bf16[2,64,128]{2,1,0:T(8,128)(2,1)S(1)} %collective-permute-done.9.prior_coefs_ref, ...), custom_call_target="tpu_custom_call", output_to_operand_aliasing={{0}: (7, {})} | custom-call | tf_op jit(solution)/shard_map/first/pallas_call | solution.py:388
  68.9 16.2 %all_to_all.5.parts_ref = f32[32,1,512]{2,1,0:T(1,128)} all-to-all(f32[32,1,512]{2,1,0:T(1,128)S(1)} %get-tuple-element.47), channel_id=1, replica_groups=mesh['date'=8,'path'=32] {'path'}, dimensions={0} | all-to-all | bytes 131072 | tf_op jit(solution)/shard_map/all_to_all | solution.py:482
  85.2 1.6 %total.1 = f32[8,64]{1,0:T(8,128)} custom-call(f32[32,1,512]{2,1,0:T(1,128)} %all_to_all.5.parts_ref), custom_call_target="tpu_custom_call" | custom-call | tf_op jit(solution)/shard_map/total/pallas_call | solution.py:414
  (12 shorter events, 0.2 us)
Async XLA Ops:
  1.6 12.3 %collective-permute-start.1 = (bf16[2,16,4096]{2,1,0:T(8,128)(2,1)S(1)}, bf16[2,16,4096]{2,1,0:T(8,128)(2,1)S(1)}, u32[]{:S(2)}, u32[]{:S(2)}) collective-permute-start(bf16[2,16,4096]{2,1,0:T(8,128)(2,1)S(1)} %slice.32), channel_id=1, source_target_pairs={{0,32},{32,64},{64,96},{96,128},{128,160},{160,192},{192,224},{1,3... | collective-permute-start | bytes 786440 | tf_op jit(solution)/shard_map/ppermute | solution.py:443
  13.7 4.0 %collective-permute-start = (f32[4,192,128]{2,1,0:T(8,128)S(1)}, f32[4,192,128]{2,1,0:T(8,128)S(1)}, u32[]{:S(2)}, u32[]{:S(2)}) collective-permute-start(f32[4,192,128]{2,1,0:T(8,128)S(1)} %get-tuple-element.32), channel_id=1, source_target_pairs={{0,1},{1,0},{2,3},{3,2},{4,5},{5,4},{6,7},{7,6},{8,9},{9,8},{10,11... | collective-permute-start | bytes 1179656 | tf_op jit(solution)/shard_map/ppermute | solution.py:427
  17.7 7.2 %collective-permute-start.2 = (f32[2,192,128]{2,1,0:T(8,128)S(1)}, f32[2,192,128]{2,1,0:T(8,128)S(1)}, u32[]{:S(2)}, u32[]{:S(2)}) collective-permute-start(f32[2,192,128]{2,1,0:T(8,128)S(1)} %select_add_fusion), channel_id=1, source_target_pairs={{0,2},{1,3},{2,0},{3,1},{4,6},{5,7},{6,4},{7,5},{8,10},{9,11},{10,... | collective-permute-start | bytes 589832 | tf_op jit(solution)/shard_map/ppermute | solution.py:427
  25.0 4.7 %collective-permute-start.3 = (f32[192,128]{1,0:T(8,128)S(1)}, f32[192,128]{1,0:T(8,128)S(1)}, u32[]{:S(2)}, u32[]{:S(2)}) collective-permute-start(f32[192,128]{1,0:T(8,128)S(1)} %select_bitcast_fusion), channel_id=1, source_target_pairs={{0,4},{1,5},{2,6},{3,7},{4,0},{5,1},{6,2},{7,3},{8,12},{9,13},{10,... | collective-permute-start | bytes 294920 | tf_op jit(solution)/shard_map/ppermute | solution.py:427
  29.8 32.5 %copy-start = (s32[64]{0:T(128)S(1)}, s32[64]{0:T(128)}, u32[]{:S(2)}) copy-start(s32[64]{0:T(128)} %param.11) | copy-start | bytes 772
  29.8 32.5 %copy-start.1 = (s32[64]{0:T(128)S(1)}, s32[64]{0:T(128)}, u32[]{:S(2)}) copy-start(s32[64]{0:T(128)} %param.12) | copy-start | bytes 772
  29.8 32.5 %copy-start.2 = (s32[64]{0:T(128)S(1)}, s32[64]{0:T(128)}, u32[]{:S(2)}) copy-start(s32[64]{0:T(128)} %param.13) | copy-start | bytes 772
  29.8 6.2 %collective-permute-start.4 = (f32[192,128]{1,0:T(8,128)S(1)}, f32[192,128]{1,0:T(8,128)S(1)}, u32[]{:S(2)}, u32[]{:S(2)}) collective-permute-start(f32[192,128]{1,0:T(8,128)S(1)} %bitcast_add_fusion), channel_id=1, source_target_pairs={{0,8},{1,9},{2,10},{3,11},{4,12},{5,13},{6,14},{7,15},{8,0},{9,1},... | collective-permute-start | bytes 294920 | tf_op jit(solution)/shard_map/ppermute | solution.py:427
  36.0 8.7 %collective-permute-start.5 = (f32[192,128]{1,0:T(8,128)S(1)}, f32[192,128]{1,0:T(8,128)S(1)}, u32[]{:S(2)}, u32[]{:S(2)}) collective-permute-start(f32[192,128]{1,0:T(8,128)S(1)} %add.27.one_ref), channel_id=1, source_target_pairs={{0,24},{1,25},{2,26},{3,27},{4,28},{5,29},{6,30},{7,31},{8,16},{9,... | collective-permute-start | bytes 294920 | tf_op jit(solution)/shard_map/ppermute | solution.py:427
  48.7 4.3 %collective-permute-start.6 = (bf16[1,64,128]{2,1,0:T(8,128)(2,1)S(1)}, bf16[1,64,128]{2,1,0:T(8,128)(2,1)S(1)}, u32[]{:S(2)}, u32[]{:S(2)}) collective-permute-start(bf16[1,64,128]{2,1,0:T(8,128)(2,1)S(1)} %bitcast.18), channel_id=1, source_target_pairs={{0,4},{1,5},{2,6},{3,7},{4,0},{5,1},{6,2},{7,3},{8,12},{9,13},{10,... | collective-permute-start | bytes 49160 | tf_op jit(solution)/shard_map/ppermute | solution.py:427
  53.0 4.0 %collective-permute-start.7 = (bf16[2,64,128]{2,1,0:T(8,128)(2,1)S(1)}, bf16[2,64,128]{2,1,0:T(8,128)(2,1)S(1)}, u32[]{:S(2)}, u32[]{:S(2)}) collective-permute-start(bf16[2,64,128]{2,1,0:T(8,128)(2,1)S(1)} %pad_maximum_fusion.2), channel_id=1, source_target_pairs={{0,2},{1,3},{2,0},{3,1},{4,6},{5,7},{6,4},{7,5},{8,10},{9,11},{10,... | collective-permute-start | bytes 98312 | tf_op jit(solution)/shard_map/ppermute | solution.py:427
  57.0 1.3 %collective-permute-start.8 = (bf16[4,64,128]{2,1,0:T(8,128)(2,1)S(1)}, bf16[4,64,128]{2,1,0:T(8,128)(2,1)S(1)}, u32[]{:S(2)}, u32[]{:S(2)}) collective-permute-start(bf16[4,64,128]{2,1,0:T(8,128)(2,1)S(1)} %pad_maximum_fusion.1), channel_id=1, source_target_pairs={{0,1},{1,0},{2,3},{3,2},{4,5},{5,4},{6,7},{7,6},{8,9},{9,8},{10,11... | collective-permute-start | bytes 196616 | tf_op jit(solution)/shard_map/ppermute | solution.py:427
  58.4 8.6 %collective-permute-start.9 = (bf16[2,64,128]{2,1,0:T(8,128)(2,1)S(1)}, bf16[2,64,128]{2,1,0:T(8,128)(2,1)S(1)}, u32[]{:S(2)}, u32[]{:S(2)}) collective-permute-start(bf16[2,64,128]{2,1,0:T(8,128)(2,1)S(1)} %slice.40), channel_id=1, source_target_pairs={{0,32},{32,64},{64,96},{96,128},{128,160},{160,192},{192,224},{1,3... | collective-permute-start | bytes 98312 | tf_op jit(solution)/shard_map/ppermute | solution.py:443

commit v6 on v5

--- a/solution.py
+++ b/solution.py
@@ -20,6 +20,7 @@
 ROUNDER = 12582912.0
 INV_TWO_PI = 0.15915494309189535
 CHUNK = 512
+PIECES = 2
 BLOCK = 8
 
 
@@ -279,29 +280,42 @@
     return sums.T[:dates]
 
 
+def add_values(first_ref, coefs_ref, features_ref, values_ref):
+    for i in range(features_ref.shape[0]):
+        t = first_ref[0] + i
+        for at in range(0, values_ref.shape[2], CHUNK):
+            span = pl.ds(at, CHUNK)
+            values_ref[t, :, span] = value_of(coefs_ref[i], features_ref[i, :, span])
+
+
+def values_kernel(first_ref, coefs_ref, features_ref, *refs):
+    add_values(first_ref, coefs_ref, features_ref, refs[-1])
+
+
 def later_kernel(
     paths_all,
-    parts,
-    firsts_ref,
+    first_ref,
     lag_ref,
     threshold_ref,
     transfer_ref,
     coefs_ref,
-    *refs,
+    features_ref,
+    given_values_ref,
+    exposure_ref,
+    values_ref,
+    profile_ref,
+    staged_ref,
+    sems,
 ):
-    exposure_ref, early_ref, profile_ref, values_ref, staged_ref, sems = refs[parts:]
+    del given_values_ref
+    add_values(first_ref, coefs_ref, features_ref, values_ref)
     dates, sets, paths = values_ref.shape
-    spans = [pl.ds(at, CHUNK) for at in range(0, paths, CHUNK)]
-    for part, features_ref in enumerate(refs[:parts]):
-        for i in range(features_ref.shape[0]):
-            t = firsts_ref[part] + i
-            for span in spans:
-                values_ref[t, :, span] = value_of(coefs_ref[t], features_ref[i, :, span])
     offset, recent = limits_of(lag_ref, threshold_ref, transfer_ref)
     totals, copies = {}, []
     for t in range(LAG_MAX, dates):
         totals[t] = jnp.zeros((sets, 128), jnp.float32)
-        for span in spans:
+        for at in range(0, paths, CHUNK):
+            span = pl.ds(at, CHUNK)
             exposed = exposed_of(
                 *(values_ref[t - back, :, span] for back in range(LAG_MAX + 1)), offset, recent
             )
@@ -310,7 +324,6 @@
         at = t - LAG_MAX
         copies.append(pltpu.make_async_copy(staged_ref.at[at], exposure_ref.at[t], sems.at[at]))
         copies[-1].start()
-    early_ref[...] = values_ref[:LAG_MAX]
     profile_ref[...] = profile_of(totals, paths_all, dates)
     for copy in copies:
         copy.wait()
@@ -323,7 +336,7 @@
     transfer_ref,
     prior_coefs_ref,
     prior_features_ref,
-    early_ref,
+    values_ref,
     profile_in_ref,
     exposure_in_ref,
     exposure_ref,
@@ -332,23 +345,28 @@
     sems,
 ):
     del exposure_in_ref
-    sets, paths = early_ref.shape[1:]
+    sets, paths = values_ref.shape[1:]
     offset, recent = limits_of(lag_ref, threshold_ref, transfer_ref)
     totals = {t: jnp.zeros((sets, 128), jnp.float32) for t in range(LAG_MAX)}
+    copies, piece = [], paths // PIECES
     for at in range(0, paths, CHUNK):
         span = pl.ds(at, CHUNK)
         v = [value_of(prior_coefs_ref[i], prior_features_ref[i, :, span]) for i in range(LAG_MAX)]
         for t in range(LAG_MAX):
-            v.append(early_ref[t, :, span])
+            v.append(values_ref[t, :, span])
             exposed = exposed_of(v[-1], v[-2], v[-3], offset, recent)
             staged_ref[t, :, span] = exposed.astype(jnp.bfloat16)
             totals[t] += by_lane(exposed)
-    copies = [
-        pltpu.make_async_copy(staged_ref.at[t], exposure_ref.at[t], sems.at[t])
-        for t in range(LAG_MAX)
-    ]
-    for copy in copies:
-        copy.start()
+        if (at + CHUNK) % piece == 0:
+            there = pl.ds(at + CHUNK - piece, piece)
+            copies.append(
+                pltpu.make_async_copy(
+                    staged_ref.at[:, :, there],
+                    exposure_ref.at[pl.ds(0, LAG_MAX), :, there],
+                    sems.at[len(copies)],
+                )
+            )
+            copies[-1].start()
     profile = profile_in_ref[...] + profile_of(totals, paths_all, profile_in_ref.shape[0])
     flat = jnp.concatenate([profile[t : t + 1] for t in range(profile.shape[0])], axis=1)
     profile_ref[...] = jnp.broadcast_to(flat[None], profile_ref.shape)
@@ -356,35 +374,55 @@
         copy.wait()
 
 
-def later_exposures(firsts, limits, coefs, parts, paths_all):
-    dates, sets, k = coefs.shape
-    paths = parts[0].shape[2]
-    return pl.pallas_call(
-        functools.partial(later_kernel, paths_all, len(parts)),
-        in_specs=[SCALARS] + [ON_CHIP] * (len(limits) + 1 + len(parts)),
+def values_of(first, coefs, features, dates, values=None):
+    here, sets, k = coefs.shape
+    paths = features.shape[2]
+    given = () if values is None else (values,)
+    return pl.pallas_call(
+        values_kernel,
+        in_specs=[SCALARS] + [ON_CHIP] * (2 + len(given)),
+        out_specs=ON_CHIP,
+        out_shape=jax.ShapeDtypeStruct((dates, sets, paths), jnp.bfloat16),
+        input_output_aliases={3: 0} if given else {},
+        compiler_params=params(4),
+        cost_estimate=pl.CostEstimate(
+            flops=200 * here * k * sets * paths,
+            bytes_accessed=2 * here * (k + sets) * paths,
+            transcendentals=0,
+        ),
+        name="values",
+    )(first.reshape(1), coefs, features, *given)
+
+
+def later_exposures(first, limits, coefs, features, values, paths_all):
+    dates, sets, paths = values.shape
+    args = (first.reshape(1), *limits, coefs, features, values)
+    return pl.pallas_call(
+        functools.partial(later_kernel, paths_all),
+        in_specs=[SCALARS] + [ON_CHIP] * (len(args) - 1),
         out_specs=(IN_HBM, ON_CHIP, ON_CHIP),
         out_shape=(
-            pltpu.HBM((dates, sets, paths), jnp.bfloat16),
-            jax.ShapeDtypeStruct((LAG_MAX, sets, paths), jnp.bfloat16),
+            pltpu.HBM(values.shape, values.dtype),
+            jax.ShapeDtypeStruct(values.shape, values.dtype),
             jax.ShapeDtypeStruct((dates, sets), jnp.float32),
         ),
         scratch_shapes=[
-            pltpu.VMEM((dates, sets, paths), jnp.bfloat16),
             pltpu.VMEM((dates - LAG_MAX, sets, paths), jnp.bfloat16),
             pltpu.SemaphoreType.DMA((dates - LAG_MAX,)),
         ],
-        compiler_params=params(20),
+        input_output_aliases={len(args) - 1: 1},
+        compiler_params=params(12),
         cost_estimate=pl.CostEstimate(
-            flops=200 * dates * k * sets * paths,
-            bytes_accessed=2 * dates * (k + sets) * paths,
+            flops=200 * dates * 128 * sets * paths,
+            bytes_accessed=4 * dates * sets * paths,
             transcendentals=0,
         ),
         name="later",
-    )(firsts, *limits, coefs, *parts)
-
-
-def first_exposures(limits, prior_coefs, prior_features, early, profile, exposure, paths_all):
-    args = (*limits, prior_coefs, prior_features, early, profile, exposure)
+    )(*args)
+
+
+def first_exposures(limits, prior_coefs, prior_features, values, profile, exposure, paths_all):
+    args = (*limits, prior_coefs, prior_features, values, profile, exposure)
     return pl.pallas_call(
         functools.partial(first_kernel, paths_all),
         in_specs=[ON_CHIP] * (len(args) - 1) + [IN_HBM],
@@ -394,11 +432,11 @@
             jax.ShapeDtypeStruct((lax.axis_size("path"), 1, profile.size), profile.dtype),
         ),
         scratch_shapes=[
-            pltpu.VMEM(early.shape, jnp.bfloat16),
-            pltpu.SemaphoreType.DMA((LAG_MAX,)),
+            pltpu.VMEM((LAG_MAX, *values.shape[1:]), jnp.bfloat16),
+            pltpu.SemaphoreType.DMA((PIECES,)),
         ],
         input_output_aliases={len(args) - 1: 0},
-        compiler_params=params(12),
+        compiler_params=params(8),
         name="first",
     )(*args)
 
@@ -417,7 +455,7 @@
         out_specs=ON_CHIP,
         out_shape=jax.ShapeDtypeStruct(shape, parts.dtype),
         name="total",
-    )(parts)
+    )(pltpu.with_memory_space_constraint(parts, pltpu.VMEM))
 
 
 CORE, ROW, NEAR, NEXT, FAR = 1, 2, 4, 8, 24
@@ -431,10 +469,9 @@
     return jnp.where(low, value[0], value[1])
 
 
-def doubled(value, step, low):
-    other = swapped(value, step)
-    first = jnp.where(low, value, other)
-    second = jnp.where(low, other, value)
+def ordered(mine, other, low):
+    first = jnp.where(low, mine, other)
+    second = jnp.where(low, other, mine)
     return jnp.concatenate([first, second], axis=0)
 
 
@@ -450,9 +487,8 @@
     half = factors.shape[0] // 2
     quarter = half // 2
     firsts = (half * (1 - core), half * core + quarter * (1 - row), half * core + quarter * row)
-    scalars = (*firsts, jnp.stack(firsts), core == 0, row == 0, near == 0)
-    first_a, first_b, first_c, firsts, core_low, row_low, near_low = lax.optimization_barrier(
-        scalars
+    first_a, first_b, first_c, core_low, row_low, near_low = lax.optimization_barrier(
+        (*firsts, core == 0, row == 0, near == 0)
     )
     prior_factors = from_earlier(factors[-LAG_MAX:])
     given = (frequency.T, phases.reshape(1, -1))
@@ -468,16 +504,21 @@
     prior_features = features_of(weights, prior_factors)
     kept, prior_features = lax.optimization_barrier((kept, prior_features))
     coefs = solved(kept, swapped(kept, FAR), paths_all)
-    coefs = doubled(coefs[None], NEAR, near_low)
-    coefs = doubled(coefs, ROW, row_low)
-    coefs = doubled(coefs, CORE, core_low)
-    prior_coefs = from_earlier(coefs[-LAG_MAX:])
+    dates = factors.shape[0]
+    coefs_c = ordered(coefs[None], swapped(coefs[None], NEAR), near_low)
+    coefs_b = swapped(coefs_c, ROW)
+    values = values_of(first_c, coefs_c, part_c, dates)
+    coefs_here = ordered(coefs_c, coefs_b, row_low)
+    coefs_a = swapped(coefs_here, CORE)
+    values = values_of(first_b, coefs_b, part_b, dates, values)
+    last_coefs = jnp.where(core_low, coefs_a[-LAG_MAX:], coefs_here[-LAG_MAX:])
+    prior_coefs = from_earlier(last_coefs)
     limits = tuple(a.reshape(1, -1) for a in (margin_lag, thresholds, transfer_min))
-    exposure, early, profile = later_exposures(
-        firsts, limits, coefs, (part_a, part_b, part_c), paths_all
+    exposure, values, profile = later_exposures(
+        first_a, limits, coefs_a, part_a, values, paths_all
     )
     exposure, parts = first_exposures(
-        limits, prior_coefs, prior_features, early, profile, exposure, paths_all
+        limits, prior_coefs, prior_features, values, profile, exposure, paths_all
     )
     return exposure, total_of(lax.all_to_all(parts, "path", 0, 0, tiled=True), profile.shape)
 

time: 88.1 us -> 85.7 us (0.973)
  Pallas kernels: 28.7 us -> 27.5 us
    ppermute x8, waiting for transfers between devices: 13.9 us -> 12.8 us  [swapped(): lax.ppermute(value, 'path', [(i, i ^ step) for i in range(lax.axis_size('...]
    pallas_call x1 -> x3, Pallas kernels: 4.71 us -> 4.49 us  [the longest x1 3.63 us: later_exposures(): pl.pallas_call(functools.partial(later_kernel, paths_all), in_specs=[SCAL...]
  transfers between devices with their start and end apart: 10 -> 10, of which waited for: 8 -> 9; matrix products, arithmetic and copies ran while one was open for 0% -> 0% of each run, Pallas kernels for 24% -> 25%
where the time goes in v6:
time: 85.7 us; the launch traced here: 84.6 us
  Pallas kernels  27.5 us (32%)
  starting transfers between devices  25.7 us (30%)
  blocking collectives  15.6 us (18%)
  waiting for transfers between devices  13.8 us (16%)
  local copies, waits for them, and re-layouts  0.99 us (1%)
    ppermute x8, starting transfers between devices, swapped(): lax.ppermute(value, 'path', [(i, i ^ step) for i in range(lax.axis_size('...  16.8 us
    all_to_all x1, blocking collectives, local(): lax.all_to_all(parts, 'path', 0, 0, tiled=True)  15.6 us
    pallas_call x3, Pallas kernels, sums_of(): pl.pallas_call(sums_kernel, in_specs=[SCALARS, *specs, IN_HBM, IN_HBM], o...  14.3 us
    ppermute x8, waiting for transfers between devices, swapped(): lax.ppermute(value, 'path', [(i, i ^ step) for i in range(lax.axis_size('...  12.8 us
    ppermute x2, starting transfers between devices, from_earlier(): return lax.ppermute(value, 'date', [(i, i + 1) for i in range(length - 1)])  8.93 us
    pallas_call x1, Pallas kernels, solved(): pl.pallas_call(functools.partial(solve_kernel, paths_all), in_specs=[ON_C...  3.95 us
    pallas_call x1, Pallas kernels, later_exposures(): pl.pallas_call(functools.partial(later_kernel, paths_all), in_specs=[SCAL...  3.63 us
    pallas_call x1, Pallas kernels, features_of(): pl.pallas_call(features_kernel, in_specs=[ON_CHIP, ON_CHIP], out_specs=ON...  2.17 us
  transfers between devices with their start and end apart: 10, of which 9 were waited for; matrix products, arithmetic and copies ran while one was open for 0% of the time, Pallas kernels for 25%

profile of v6, /device:TPU:2, one launch (start us, length us, event | category | flops | bytes accessed | tf_op | source)
XLA Modules:
  0.0 84.6 jit_solution(5147844953623352786)
XLA Ops:
  0.6 1.0 %slice.32 = bf16[2,16,4096]{2,1,0:T(8,128)(2,1)S(1)} slice(bf16[8,16,4096]{2,1,0:T(8,128)(2,1)} %refs_1_.3), slice={[6:8], [0:16], [0:4096]} | slice | bytes 524288 | tf_op jit(solution)/shard_map/slice | solution.py:493
  1.6 5.1 %collective-permute-start.1 = (bf16[2,16,4096]{2,1,0:T(8,128)(2,1)S(1)}, bf16[2,16,4096]{2,1,0:T(8,128)(2,1)S(1)}, u32[]{:S(2)}, u32[]{:S(2)}) collective-permute-start(bf16[2,16,4096]{2,1,0:T(8,128)(2,1)S(1)} %slice.32), channel_id=1, source_target_pairs={{0,32},{32,64},{64,96},{96,128},{128,160},{160,192},{192,224},{1,3... | collective-permute-start | bytes 786440 | tf_op jit(solution)/shard_map/ppermute | solution.py:480
  6.7 6.9 %sums.3 = (bf16[4,128,4096]{2,1,0:T(8,128)(2,1)S(1)}, f32[4,192,128]{2,1,0:T(8,128)S(1)}, bf16[128,64]{1,0:T(8,128)(2,1)S(1)}) custom-call(s32[1]{0:T(128)} %bitcast.4.first_ref, bf16[16,128]{1,0:T(8,128)(2,1)} %bitcast.22, f32[1,128]{1,0:T(1,128)} %bitcast.23, bf16[8,16,4096]{2,1,0:T(8,128)(2,1)} %refs_1_.3, bf16[8,64,4096]{2,1,0:T(8,128)(2,1)} %refs_2_.5), custom_call_target="tpu_custom_call" | custom-call | flops 41943040000 | bytes 8388608 | tf_op jit(solution)/shard_map/sums/pallas_call | solution.py:188
  13.6 0.1 collective-permute-start
  13.7 0.2 collective-permute-done.1.factors_ref
  13.9 3.7 %sums.5 = (bf16[2,128,4096]{2,1,0:T(8,128)(2,1)S(1)}, f32[2,192,128]{2,1,0:T(8,128)S(1)}) custom-call(s32[1]{0:T(128)} %bitcast.7.first_ref, bf16[128,64]{1,0:T(8,128)(2,1)S(1)} %get-tuple-element.29.refs_0_.weights_ref, bf16[8,16,4096]{2,1,0:T(8,128)(2,1)} %refs_1_.3, bf16[8,64,4096]{2,1,0:T(8,128)(2,1)} %refs_2_.5), custom_call_target="tpu_custom_call" | custom-call | flops 20971520000 | bytes 4194304 | tf_op jit(solution)/shard_map/sums/pallas_call | solution.py:188
  17.7 0.0 collective-permute-done
  17.7 1.7 %collective-permute-start.2 = (f32[2,192,128]{2,1,0:T(8,128)S(1)}, f32[2,192,128]{2,1,0:T(8,128)S(1)}, u32[]{:S(2)}, u32[]{:S(2)}) collective-permute-start(f32[2,192,128]{2,1,0:T(8,128)S(1)} %select_add_fusion), channel_id=1, source_target_pairs={{0,2},{1,3},{2,0},{3,1},{4,6},{5,7},{6,4},{7,5},{8,10},{9,11},{10,... | collective-permute-start | bytes 589832 | tf_op jit(solution)/shard_map/ppermute | solution.py:465
  19.4 3.7 %sums.4 = (bf16[2,128,4096]{2,1,0:T(8,128)(2,1)S(1)}, f32[2,192,128]{2,1,0:T(8,128)S(1)}) custom-call(s32[1]{0:T(128)} %bitcast.3.first_ref, bf16[128,64]{1,0:T(8,128)(2,1)S(1)} %get-tuple-element.29.refs_0_.weights_ref, bf16[8,16,4096]{2,1,0:T(8,128)(2,1)} %refs_1_.3, bf16[8,64,4096]{2,1,0:T(8,128)(2,1)} %refs_2_.5), custom_call_target="tpu_custom_call" | custom-call | flops 20971520000 | bytes 4194304 | tf_op jit(solution)/shard_map/sums/pallas_call | solution.py:188
  23.2 1.7 %collective-permute-done.2 = f32[2,192,128]{2,1,0:T(8,128)S(1)} collective-permute-done((f32[2,192,128]{2,1,0:T(8,128)S(1)}, f32[2,192,128]{2,1,0:T(8,128)S(1)}, u32[]{:S(2)}, u32[]{:S(2)}) %collective-permute-start.2) | collective-permute-done | bytes 196640 | tf_op jit(solution)/shard_map/ppermute | solution.py:465
  25.0 2.0 %collective-permute-start.3 = (f32[192,128]{1,0:T(8,128)S(1)}, f32[192,128]{1,0:T(8,128)S(1)}, u32[]{:S(2)}, u32[]{:S(2)}) collective-permute-start(f32[192,128]{1,0:T(8,128)S(1)} %select_bitcast_fusion), channel_id=1, source_target_pairs={{0,4},{1,5},{2,6},{3,7},{4,0},{5,1},{6,2},{7,3},{8,12},{9,13},{10,... | collective-permute-start | bytes 294920 | tf_op jit(solution)/shard_map/ppermute | solution.py:465
  27.0 2.7 %collective-permute-done.3 = f32[192,128]{1,0:T(8,128)S(1)} collective-permute-done((f32[192,128]{1,0:T(8,128)S(1)}, f32[192,128]{1,0:T(8,128)S(1)}, u32[]{:S(2)}, u32[]{:S(2)}) %collective-permute-start.3) | collective-permute-done | bytes 98336 | tf_op jit(solution)/shard_map/ppermute | solution.py:465
  29.7 3.5 %collective-permute-start.4 = (f32[192,128]{1,0:T(8,128)S(1)}, f32[192,128]{1,0:T(8,128)S(1)}, u32[]{:S(2)}, u32[]{:S(2)}) collective-permute-start(f32[192,128]{1,0:T(8,128)S(1)} %bitcast_add_fusion), channel_id=1, source_target_pairs={{0,8},{1,9},{2,10},{3,11},{4,12},{5,13},{6,14},{7,15},{8,0},{9,1},... | collective-permute-start | bytes 294920 | tf_op jit(solution)/shard_map/ppermute | solution.py:465
  33.2 2.2 %features.1.prior_features_ref = bf16[2,128,4096]{2,1,0:T(8,128)(2,1)S(1)} custom-call(bf16[128,64]{1,0:T(8,128)(2,1)S(1)} %get-tuple-element.29.refs_0_.weights_ref, bf16[2,16,4096]{2,1,0:T(8,128)(2,1)S(1)} %collective-permute-done.1.factors_ref), custom_call_target="tpu_custom_call" | custom-call | flops 2097152000 | bytes 2097152 | tf_op jit(solution)/shard_map/features/pallas_call | solution.py:155
  35.4 0.4 collective-permute-done.4
  35.8 6.1 %collective-permute-start.5 = (f32[192,128]{1,0:T(8,128)S(1)}, f32[192,128]{1,0:T(8,128)S(1)}, u32[]{:S(2)}, u32[]{:S(2)}) collective-permute-start(f32[192,128]{1,0:T(8,128)S(1)} %add.27.one_ref), channel_id=1, source_target_pairs={{0,24},{1,25},{2,26},{3,27},{4,28},{5,29},{6,30},{7,31},{8,16},{9,... | collective-permute-start | bytes 294920 | tf_op jit(solution)/shard_map/ppermute | solution.py:465
  42.0 2.7 %collective-permute-done.5.two_ref = f32[192,128]{1,0:T(8,128)S(1)} collective-permute-done((f32[192,128]{1,0:T(8,128)S(1)}, f32[192,128]{1,0:T(8,128)S(1)}, u32[]{:S(2)}, u32[]{:S(2)}) %collective-permute-start.5) | collective-permute-done | bytes 98336 | tf_op jit(solution)/shard_map/ppermute | solution.py:465
  44.6 3.9 %solve.1 = bf16[64,128]{1,0:T(8,128)(2,1)S(1)} custom-call(f32[192,128]{1,0:T(8,128)S(1)} %add.27.one_ref, f32[192,128]{1,0:T(8,128)S(1)} %collective-permute-done.5.two_ref), custom_call_target="tpu_custom_call" | custom-call | tf_op jit(solution)/shard_map/solve/pallas_call | solution.py:237
  48.6 2.5 %collective-permute-start.6 = (bf16[1,64,128]{2,1,0:T(8,128)(2,1)S(1)}, bf16[1,64,128]{2,1,0:T(8,128)(2,1)S(1)}, u32[]{:S(2)}, u32[]{:S(2)}) collective-permute-start(bf16[1,64,128]{2,1,0:T(8,128)(2,1)S(1)} %bitcast.15), channel_id=1, source_target_pairs={{0,4},{1,5},{2,6},{3,7},{4,0},{5,1},{6,2},{7,3},{8,12},{9,13},{10,... | collective-permute-start | bytes 49160 | tf_op jit(solution)/shard_map/ppermute | solution.py:465
  51.1 1.7 %collective-permute-done.6 = bf16[1,64,128]{2,1,0:T(8,128)(2,1)S(1)} collective-permute-done((bf16[1,64,128]{2,1,0:T(8,128)(2,1)S(1)}, bf16[1,64,128]{2,1,0:T(8,128)(2,1)S(1)}, u32[]{:S(2)}, u32[]{:S(2)}) %collective-permute-start.6) | collective-permute-done | bytes 16416 | tf_op jit(solution)/shard_map/ppermute | solution.py:465
  52.9 0.8 collective-permute-start.7
  53.6 0.4 values.2.refs_0_
  54.1 2.8 %collective-permute-done.7.coefs_ref = bf16[2,64,128]{2,1,0:T(8,128)(2,1)S(1)} collective-permute-done((bf16[2,64,128]{2,1,0:T(8,128)(2,1)S(1)}, bf16[2,64,128]{2,1,0:T(8,128)(2,1)S(1)}, u32[]{:S(2)}, u32[]{:S(2)}) %collective-permute-start.7) | collective-permute-done | bytes 32800 | tf_op jit(solution)/shard_map/ppermute | solution.py:465
  56.9 0.1 collective-permute-start.8
  57.0 0.0 copy-start
  57.0 0.0 copy-start.1
  57.0 0.0 copy-start.2
  57.0 0.4 values.3.given_values_ref
  57.5 0.8 collective-permute-done.8.coefs_ref
  58.2 3.8 %collective-permute-start.9 = (bf16[2,64,128]{2,1,0:T(8,128)(2,1)S(1)}, bf16[2,64,128]{2,1,0:T(8,128)(2,1)S(1)}, u32[]{:S(2)}, u32[]{:S(2)}) collective-permute-start(bf16[2,64,128]{2,1,0:T(8,128)(2,1)S(1)} %slice_select_fusion), channel_id=1, source_target_pairs={{0,32},{32,64},{64,96},{96,128},{128,160},{160,192},{192,224},{1,3... | collective-permute-start | bytes 98312 | tf_op jit(solution)/shard_map/ppermute | solution.py:480
  62.1 0.0 copy-done
  62.1 0.0 copy-done.1
  62.1 0.0 copy-done.2
  62.1 3.6 %later.1 = (bf16[8,64,4096]{2,1,0:T(8,128)(2,1)}, bf16[8,64,4096]{2,1,0:T(8,128)(2,1)S(1)}, f32[8,64]{1,0:T(8,128)S(1)}) custom-call(s32[1]{0:T(128)} %bitcast.4.first_ref, s32[1,64]{1,0:T(1,128)S(1)} %bitcast.16, s32[1,64]{1,0:T(1,128)S(1)} %bitcast.18, s32[1,64]{1,0:T(1,128)S(1)} %bitcast.20, ...), custom_call_target="tpu_custom_call", output_to_operand_aliasing={{1}: (6, {})} | custom-call | flops 53687091200 | bytes 8388608 | tf_op jit(solution)/shard_map/later/pallas_call | solution.py:400
  65.7 0.7 collective-permute-done.9.prior_coefs_ref
  66.4 1.8 %first.1 = (bf16[8,64,4096]{2,1,0:T(8,128)(2,1)}, f32[32,1,512]{2,1,0:T(1,128)S(1)}) custom-call(s32[1,64]{1,0:T(1,128)S(1)} %bitcast.17, s32[1,64]{1,0:T(1,128)S(1)} %bitcast.19, s32[1,64]{1,0:T(1,128)S(1)} %bitcast.21, bf16[2,64,128]{2,1,0:T(8,128)(2,1)S(1)} %collective-permute-done.9.prior_coefs_ref, ...), custom_call_target="tpu_custom_call", output_to_operand_aliasing={{0}: (7, {})} | custom-call | tf_op jit(solution)/shard_map/first/pallas_call | solution.py:426
  68.2 15.6 %all_to_all.5.parts_ref = f32[32,1,512]{2,1,0:T(1,128)S(1)} all-to-all(f32[32,1,512]{2,1,0:T(1,128)S(1)} %get-tuple-element.45), channel_id=1, replica_groups=mesh['date'=8,'path'=32] {'path'}, dimensions={0} | all-to-all | bytes 131072 | tf_op jit(solution)/shard_map/all_to_all | solution.py:523
  83.8 0.7 total.1
  (10 shorter events, 0.2 us)
Async XLA Ops:
  1.6 12.3 %collective-permute-start.1 = (bf16[2,16,4096]{2,1,0:T(8,128)(2,1)S(1)}, bf16[2,16,4096]{2,1,0:T(8,128)(2,1)S(1)}, u32[]{:S(2)}, u32[]{:S(2)}) collective-permute-start(bf16[2,16,4096]{2,1,0:T(8,128)(2,1)S(1)} %slice.32), channel_id=1, source_target_pairs={{0,32},{32,64},{64,96},{96,128},{128,160},{160,192},{192,224},{1,3... | collective-permute-start | bytes 786440 | tf_op jit(solution)/shard_map/ppermute | solution.py:480
  13.6 4.1 %collective-permute-start = (f32[4,192,128]{2,1,0:T(8,128)S(1)}, f32[4,192,128]{2,1,0:T(8,128)S(1)}, u32[]{:S(2)}, u32[]{:S(2)}) collective-permute-start(f32[4,192,128]{2,1,0:T(8,128)S(1)} %get-tuple-element.31), channel_id=1, source_target_pairs={{0,1},{1,0},{2,3},{3,2},{4,5},{5,4},{6,7},{7,6},{8,9},{9,8},{10,11... | collective-permute-start | bytes 1179656 | tf_op jit(solution)/shard_map/ppermute | solution.py:465
  17.7 7.1 %collective-permute-start.2 = (f32[2,192,128]{2,1,0:T(8,128)S(1)}, f32[2,192,128]{2,1,0:T(8,128)S(1)}, u32[]{:S(2)}, u32[]{:S(2)}) collective-permute-start(f32[2,192,128]{2,1,0:T(8,128)S(1)} %select_add_fusion), channel_id=1, source_target_pairs={{0,2},{1,3},{2,0},{3,1},{4,6},{5,7},{6,4},{7,5},{8,10},{9,11},{10,... | collective-permute-start | bytes 589832 | tf_op jit(solution)/shard_map/ppermute | solution.py:465
  25.0 4.7 %collective-permute-start.3 = (f32[192,128]{1,0:T(8,128)S(1)}, f32[192,128]{1,0:T(8,128)S(1)}, u32[]{:S(2)}, u32[]{:S(2)}) collective-permute-start(f32[192,128]{1,0:T(8,128)S(1)} %select_bitcast_fusion), channel_id=1, source_target_pairs={{0,4},{1,5},{2,6},{3,7},{4,0},{5,1},{6,2},{7,3},{8,12},{9,13},{10,... | collective-permute-start | bytes 294920 | tf_op jit(solution)/shard_map/ppermute | solution.py:465
  29.7 6.1 %collective-permute-start.4 = (f32[192,128]{1,0:T(8,128)S(1)}, f32[192,128]{1,0:T(8,128)S(1)}, u32[]{:S(2)}, u32[]{:S(2)}) collective-permute-start(f32[192,128]{1,0:T(8,128)S(1)} %bitcast_add_fusion), channel_id=1, source_target_pairs={{0,8},{1,9},{2,10},{3,11},{4,12},{5,13},{6,14},{7,15},{8,0},{9,1},... | collective-permute-start | bytes 294920 | tf_op jit(solution)/shard_map/ppermute | solution.py:465
  35.8 8.8 %collective-permute-start.5 = (f32[192,128]{1,0:T(8,128)S(1)}, f32[192,128]{1,0:T(8,128)S(1)}, u32[]{:S(2)}, u32[]{:S(2)}) collective-permute-start(f32[192,128]{1,0:T(8,128)S(1)} %add.27.one_ref), channel_id=1, source_target_pairs={{0,24},{1,25},{2,26},{3,27},{4,28},{5,29},{6,30},{7,31},{8,16},{9,... | collective-permute-start | bytes 294920 | tf_op jit(solution)/shard_map/ppermute | solution.py:465
  48.6 4.3 %collective-permute-start.6 = (bf16[1,64,128]{2,1,0:T(8,128)(2,1)S(1)}, bf16[1,64,128]{2,1,0:T(8,128)(2,1)S(1)}, u32[]{:S(2)}, u32[]{:S(2)}) collective-permute-start(bf16[1,64,128]{2,1,0:T(8,128)(2,1)S(1)} %bitcast.15), channel_id=1, source_target_pairs={{0,4},{1,5},{2,6},{3,7},{4,0},{5,1},{6,2},{7,3},{8,12},{9,13},{10,... | collective-permute-start | bytes 49160 | tf_op jit(solution)/shard_map/ppermute | solution.py:465
  52.9 4.0 %collective-permute-start.7 = (bf16[2,64,128]{2,1,0:T(8,128)(2,1)S(1)}, bf16[2,64,128]{2,1,0:T(8,128)(2,1)S(1)}, u32[]{:S(2)}, u32[]{:S(2)}) collective-permute-start(bf16[2,64,128]{2,1,0:T(8,128)(2,1)S(1)} %pad_maximum_fusion.1.coefs_ref), channel_id=1, source_target_pairs={{0,2},{1,3},{2,0},{3,1},{4,6},{5,7},{6,4},{7,5},{8,10},{9,11},{10,... | collective-permute-start | bytes 98312 | tf_op jit(solution)/shard_map/ppermute | solution.py:465
  56.9 1.3 %collective-permute-start.8 = (bf16[4,64,128]{2,1,0:T(8,128)(2,1)S(1)}, bf16[4,64,128]{2,1,0:T(8,128)(2,1)S(1)}, u32[]{:S(2)}, u32[]{:S(2)}) collective-permute-start(bf16[4,64,128]{2,1,0:T(8,128)(2,1)S(1)} %pad_maximum_fusion), channel_id=1, source_target_pairs={{0,1},{1,0},{2,3},{3,2},{4,5},{5,4},{6,7},{7,6},{8,9},{9,8},{10,11... | collective-permute-start | bytes 196616 | tf_op jit(solution)/shard_map/ppermute | solution.py:465
  57.0 5.1 %copy-start = (s32[64]{0:T(128)S(1)}, s32[64]{0:T(128)}, u32[]{:S(2)}) copy-start(s32[64]{0:T(128)} %param.11) | copy-start | bytes 772
  57.0 5.1 %copy-start.1 = (s32[64]{0:T(128)S(1)}, s32[64]{0:T(128)}, u32[]{:S(2)}) copy-start(s32[64]{0:T(128)} %param.12) | copy-start | bytes 772
  57.0 5.1 %copy-start.2 = (s32[64]{0:T(128)S(1)}, s32[64]{0:T(128)}, u32[]{:S(2)}) copy-start(s32[64]{0:T(128)} %param.13) | copy-start | bytes 772
  58.2 8.2 %collective-permute-start.9 = (bf16[2,64,128]{2,1,0:T(8,128)(2,1)S(1)}, bf16[2,64,128]{2,1,0:T(8,128)(2,1)S(1)}, u32[]{:S(2)}, u32[]{:S(2)}) collective-permute-start(bf16[2,64,128]{2,1,0:T(8,128)(2,1)S(1)} %slice_select_fusion), channel_id=1, source_target_pairs={{0,32},{32,64},{64,96},{96,128},{128,160},{160,192},{192,224},{1,3... | collective-permute-start | bytes 98312 | tf_op jit(solution)/shard_map/ppermute | solution.py:480

commit v7 on v6

--- a/solution.py
+++ b/solution.py
@@ -64,6 +64,25 @@
             features_ref[i, :, span] = cosines(
                 chunk_turns(weights_ref[...], factors_ref[i, :, span])
             )
+
+
+def packed(sums):
+    k = sums.shape[1]
+    half, quarter = k // 2, k // 4
+    lane = lax.broadcasted_iota(jnp.int32, (quarter, k), 1)
+    folded = jnp.where(lane < half, sums[:quarter], pltpu.roll(sums[quarter:half], half, 1))
+    return jnp.concatenate([sums[k:], sums[half:k], folded], axis=0)
+
+
+def unpacked(rows):
+    k = rows.shape[1]
+    half, quarter = k // 2, k // 4
+    sets = rows.shape[0] - half - quarter
+    low, folded = rows[sets : sets + half], rows[sets + half :]
+    left = jnp.concatenate([folded, pltpu.roll(folded, half, 1)], axis=0)
+    across = jnp.concatenate([left, low], axis=0).T[:half]
+    lane = lax.broadcasted_iota(jnp.int32, (half, k), 1)
+    return jnp.concatenate([jnp.where(lane < half, left, across), low], axis=0), rows[:sets]
 
 
 def sums_kernel(first_ref, *refs):
@@ -128,7 +147,7 @@
             starts = at == 1 or items[at - 2][0] != i
             sums = product if starts else sums + product
             if at == len(items) or items[at][0] != i:
-                sums_ref[i] = sums
+                sums_ref[i] = packed(sums)
         if at < len(items):
             i, span = items[at]
             feats = cosines(turns)
@@ -170,7 +189,7 @@
     k, sets = given[0].shape[len(given) - 1], flows.shape[1]
     outs = [
         jax.ShapeDtypeStruct((dates, k, paths), jnp.bfloat16),
-        jax.ShapeDtypeStruct((dates, k + sets, k), jnp.float32),
+        jax.ShapeDtypeStruct((dates, sets + k // 2 + k // 4, k), jnp.float32),
     ]
     scratch = [
         pltpu.VMEM((dates, r, paths), jnp.bfloat16),
@@ -203,29 +222,32 @@
 
 def solve_kernel(paths_all, one_ref, two_ref, out_ref):
     k = one_ref.shape[1]
-    total = (one_ref[...] + two_ref[...]) / paths_all
+    system, right = unpacked((one_ref[...] + two_ref[...]) / paths_all)
     row_at = lax.broadcasted_iota(jnp.int32, (k, k), 0)
     lane_at = lax.broadcasted_iota(jnp.int32, (k, k), 1)
-    system = total[:k] + jnp.where(row_at == lane_at, ridge_weight, 0.0)
-    m = jnp.concatenate([system, total[k:]], axis=0)
+    system = system + jnp.where(row_at == lane_at, ridge_weight, 0.0)
+    m = jnp.concatenate([system, right], axis=0)
     lane = lax.broadcasted_iota(jnp.int32, (1, k), 1)
     for j in range(0, k, BLOCK):
         pivots = [m[i : i + 1, :] for i in range(BLOCK)]
-        entries = [
-            [jnp.broadcast_to(row[:, j + i : j + i + 1], (1, k)) for i in range(BLOCK)]
-            for row in pivots
-        ]
+        entries = {
+            (i, q): jnp.broadcast_to(pivots[i][:, j + q : j + q + 1], (1, k))
+            for i in range(BLOCK)
+            for q in range(i, BLOCK)
+        }
         rows = [row - jnp.where(lane == j + i, 1.0, 0.0) for i, row in enumerate(pivots)]
         for p in range(BLOCK):
-            inverse = 1.0 / entries[p][p]
+            inverse = 1.0 / entries[p, p]
             rows[p] = rows[p] * inverse
-            for q in range(p + 1, BLOCK):
-                entries[p][q] = entries[p][q] * inverse
+            scaled = {q: entries[p, q] * inverse for q in range(p + 1, BLOCK)}
             for i in range(BLOCK):
                 if i != p:
-                    rows[i] = rows[i] - entries[i][p] * rows[p]
-                    for q in range(p + 1, BLOCK):
-                        entries[i][q] = entries[i][q] - entries[i][p] * entries[p][q]
+                    factor = entries[min(i, p), max(i, p)]
+                    rows[i] = rows[i] - factor * rows[p]
+                    for q in range(max(i, p + 1), BLOCK):
+                        entries[i, q] = entries[i, q] - factor * scaled[q]
+            for q, entry in scaled.items():
+                entries[p, q] = entry
         m = m[BLOCK:]
         m = m - sum(m[:, j + i : j + i + 1] * rows[i] for i in range(BLOCK))
     out_ref[...] = m.astype(jnp.bfloat16)
@@ -233,7 +255,7 @@
 
 def solved(one, two, paths_all):
     k = one.shape[1]
-    sets = one.shape[0] - k
+    sets = one.shape[0] - k // 2 - k // 4
     return pl.pallas_call(
         functools.partial(solve_kernel, paths_all),
         in_specs=[ON_CHIP, ON_CHIP],

time: 85.7 us -> 84.1 us (0.981)
  waiting for transfers between devices: 13.8 us -> 12.5 us
    ppermute x8, waiting for transfers between devices: 12.8 us -> 11.5 us  [swapped(): lax.ppermute(value, 'path', [(i, i ^ step) for i in range(lax.axis_size('...]
where the time goes in v7:
time: 84.1 us; the launch traced here: 82.9 us
  Pallas kernels  27.2 us (32%)
  starting transfers between devices  25.6 us (30%)
  blocking collectives  15.6 us (19%)
  waiting for transfers between devices  12.5 us (15%)
  local copies, waits for them, and re-layouts  0.99 us (1%)
  between operations  0.85 us (1%)
    ppermute x8, starting transfers between devices, swapped(): lax.ppermute(value, 'path', [(i, i ^ step) for i in range(lax.axis_size('...  16.7 us
    all_to_all x1, blocking collectives, local(): lax.all_to_all(parts, 'path', 0, 0, tiled=True)  15.6 us
    pallas_call x3, Pallas kernels, sums_of(): pl.pallas_call(sums_kernel, in_specs=[SCALARS, *specs, IN_HBM, IN_HBM], o...  14.3 us
    ppermute x8, waiting for transfers between devices, swapped(): lax.ppermute(value, 'path', [(i, i ^ step) for i in range(lax.axis_size('...  11.5 us
    ppermute x2, starting transfers between devices, from_earlier(): return lax.ppermute(value, 'date', [(i, i + 1) for i in range(length - 1)])  8.94 us
    pallas_call x1, Pallas kernels, solved(): pl.pallas_call(functools.partial(solve_kernel, paths_all), in_specs=[ON_C...  3.81 us
    pallas_call x1, Pallas kernels, later_exposures(): pl.pallas_call(functools.partial(later_kernel, paths_all), in_specs=[SCAL...  3.63 us
    pallas_call x1, Pallas kernels, features_of(): pl.pallas_call(features_kernel, in_specs=[ON_CHIP, ON_CHIP], out_specs=ON...  2.17 us
  transfers between devices with their start and end apart: 10, of which 9 were waited for; matrix products, arithmetic and copies ran while one was open for 0% of the time, Pallas kernels for 25%

profile of v7, /device:TPU:2, one launch (start us, length us, event | category | flops | bytes accessed | tf_op | source)
XLA Modules:
  0.0 82.9 jit_solution(1714966525713864813)
XLA Ops:
  0.6 1.0 %slice.32 = bf16[2,16,4096]{2,1,0:T(8,128)(2,1)S(1)} slice(bf16[8,16,4096]{2,1,0:T(8,128)(2,1)} %refs_1_.3), slice={[6:8], [0:16], [0:4096]} | slice | bytes 524288 | tf_op jit(solution)/shard_map/slice | solution.py:515
  1.6 5.1 %collective-permute-start.1 = (bf16[2,16,4096]{2,1,0:T(8,128)(2,1)S(1)}, bf16[2,16,4096]{2,1,0:T(8,128)(2,1)S(1)}, u32[]{:S(2)}, u32[]{:S(2)}) collective-permute-start(bf16[2,16,4096]{2,1,0:T(8,128)(2,1)S(1)} %slice.32), channel_id=1, source_target_pairs={{0,32},{32,64},{64,96},{96,128},{128,160},{160,192},{192,224},{1,3... | collective-permute-start | bytes 786440 | tf_op jit(solution)/shard_map/ppermute | solution.py:502
  6.7 6.8 %sums.3 = (bf16[4,128,4096]{2,1,0:T(8,128)(2,1)S(1)}, f32[4,160,128]{2,1,0:T(8,128)S(1)}, bf16[128,64]{1,0:T(8,128)(2,1)S(1)}) custom-call(s32[1]{0:T(128)} %bitcast.4.first_ref, bf16[16,128]{1,0:T(8,128)(2,1)} %bitcast.22, f32[1,128]{1,0:T(1,128)} %bitcast.23, bf16[8,16,4096]{2,1,0:T(8,128)(2,1)} %refs_1_.3, bf16[8,64,4096]{2,1,0:T(8,128)(2,1)} %refs_2_.5), custom_call_target="tpu_custom_call" | custom-call | flops 41943040000 | bytes 8388608 | tf_op jit(solution)/shard_map/sums/pallas_call | solution.py:207
  13.5 0.1 collective-permute-start
  13.6 0.3 collective-permute-done.1.factors_ref
  13.9 3.7 %sums.5 = (bf16[2,128,4096]{2,1,0:T(8,128)(2,1)S(1)}, f32[2,160,128]{2,1,0:T(8,128)S(1)}) custom-call(s32[1]{0:T(128)} %bitcast.7.first_ref, bf16[128,64]{1,0:T(8,128)(2,1)S(1)} %get-tuple-element.29.refs_0_.weights_ref, bf16[8,16,4096]{2,1,0:T(8,128)(2,1)} %refs_1_.3, bf16[8,64,4096]{2,1,0:T(8,128)(2,1)} %refs_2_.5), custom_call_target="tpu_custom_call" | custom-call | flops 20971520000 | bytes 4194304 | tf_op jit(solution)/shard_map/sums/pallas_call | solution.py:207
  17.7 0.0 collective-permute-done
  17.7 1.7 %collective-permute-start.2 = (f32[2,160,128]{2,1,0:T(8,128)S(1)}, f32[2,160,128]{2,1,0:T(8,128)S(1)}, u32[]{:S(2)}, u32[]{:S(2)}) collective-permute-start(f32[2,160,128]{2,1,0:T(8,128)S(1)} %select_add_fusion), channel_id=1, source_target_pairs={{0,2},{1,3},{2,0},{3,1},{4,6},{5,7},{6,4},{7,5},{8,10},{9,11},{10,... | collective-permute-start | bytes 491528 | tf_op jit(solution)/shard_map/ppermute | solution.py:487
  19.4 3.7 %sums.4 = (bf16[2,128,4096]{2,1,0:T(8,128)(2,1)S(1)}, f32[2,160,128]{2,1,0:T(8,128)S(1)}) custom-call(s32[1]{0:T(128)} %bitcast.3.first_ref, bf16[128,64]{1,0:T(8,128)(2,1)S(1)} %get-tuple-element.29.refs_0_.weights_ref, bf16[8,16,4096]{2,1,0:T(8,128)(2,1)} %refs_1_.3, bf16[8,64,4096]{2,1,0:T(8,128)(2,1)} %refs_2_.5), custom_call_target="tpu_custom_call" | custom-call | flops 20971520000 | bytes 4194304 | tf_op jit(solution)/shard_map/sums/pallas_call | solution.py:207
  23.1 1.0 %collective-permute-done.2 = f32[2,160,128]{2,1,0:T(8,128)S(1)} collective-permute-done((f32[2,160,128]{2,1,0:T(8,128)S(1)}, f32[2,160,128]{2,1,0:T(8,128)S(1)}, u32[]{:S(2)}, u32[]{:S(2)}) %collective-permute-start.2) | collective-permute-done | bytes 163872 | tf_op jit(solution)/shard_map/ppermute | solution.py:487
  24.2 2.0 %collective-permute-start.3 = (f32[160,128]{1,0:T(8,128)S(1)}, f32[160,128]{1,0:T(8,128)S(1)}, u32[]{:S(2)}, u32[]{:S(2)}) collective-permute-start(f32[160,128]{1,0:T(8,128)S(1)} %select_bitcast_fusion), channel_id=1, source_target_pairs={{0,4},{1,5},{2,6},{3,7},{4,0},{5,1},{6,2},{7,3},{8,12},{9,13},{10,... | collective-permute-start | bytes 245768 | tf_op jit(solution)/shard_map/ppermute | solution.py:487
  26.2 2.5 %collective-permute-done.3 = f32[160,128]{1,0:T(8,128)S(1)} collective-permute-done((f32[160,128]{1,0:T(8,128)S(1)}, f32[160,128]{1,0:T(8,128)S(1)}, u32[]{:S(2)}, u32[]{:S(2)}) %collective-permute-start.3) | collective-permute-done | bytes 81952 | tf_op jit(solution)/shard_map/ppermute | solution.py:487
  28.7 3.5 %collective-permute-start.4 = (f32[160,128]{1,0:T(8,128)S(1)}, f32[160,128]{1,0:T(8,128)S(1)}, u32[]{:S(2)}, u32[]{:S(2)}) collective-permute-start(f32[160,128]{1,0:T(8,128)S(1)} %bitcast_add_fusion), channel_id=1, source_target_pairs={{0,8},{1,9},{2,10},{3,11},{4,12},{5,13},{6,14},{7,15},{8,0},{9,1},... | collective-permute-start | bytes 245768 | tf_op jit(solution)/shard_map/ppermute | solution.py:487
  32.3 2.2 %features.1.prior_features_ref = bf16[2,128,4096]{2,1,0:T(8,128)(2,1)S(1)} custom-call(bf16[128,64]{1,0:T(8,128)(2,1)S(1)} %get-tuple-element.29.refs_0_.weights_ref, bf16[2,16,4096]{2,1,0:T(8,128)(2,1)S(1)} %collective-permute-done.1.factors_ref), custom_call_target="tpu_custom_call" | custom-call | flops 2097152000 | bytes 2097152 | tf_op jit(solution)/shard_map/features/pallas_call | solution.py:174
  34.4 0.2 collective-permute-done.4
  34.7 6.1 %collective-permute-start.5 = (f32[160,128]{1,0:T(8,128)S(1)}, f32[160,128]{1,0:T(8,128)S(1)}, u32[]{:S(2)}, u32[]{:S(2)}) collective-permute-start(f32[160,128]{1,0:T(8,128)S(1)} %add.27.one_ref), channel_id=1, source_target_pairs={{0,24},{1,25},{2,26},{3,27},{4,28},{5,29},{6,30},{7,31},{8,16},{9,... | collective-permute-start | bytes 245768 | tf_op jit(solution)/shard_map/ppermute | solution.py:487
  40.8 2.5 %collective-permute-done.5.two_ref = f32[160,128]{1,0:T(8,128)S(1)} collective-permute-done((f32[160,128]{1,0:T(8,128)S(1)}, f32[160,128]{1,0:T(8,128)S(1)}, u32[]{:S(2)}, u32[]{:S(2)}) %collective-permute-start.5) | collective-permute-done | bytes 81952 | tf_op jit(solution)/shard_map/ppermute | solution.py:487
  43.3 3.8 %solve.1 = bf16[64,128]{1,0:T(8,128)(2,1)S(1)} custom-call(f32[160,128]{1,0:T(8,128)S(1)} %add.27.one_ref, f32[160,128]{1,0:T(8,128)S(1)} %collective-permute-done.5.two_ref), custom_call_target="tpu_custom_call" | custom-call | tf_op jit(solution)/shard_map/solve/pallas_call | solution.py:259
  47.1 2.4 %collective-permute-start.6 = (bf16[1,64,128]{2,1,0:T(8,128)(2,1)S(1)}, bf16[1,64,128]{2,1,0:T(8,128)(2,1)S(1)}, u32[]{:S(2)}, u32[]{:S(2)}) collective-permute-start(bf16[1,64,128]{2,1,0:T(8,128)(2,1)S(1)} %bitcast.15), channel_id=1, source_target_pairs={{0,4},{1,5},{2,6},{3,7},{4,0},{5,1},{6,2},{7,3},{8,12},{9,13},{10,... | collective-permute-start | bytes 49160 | tf_op jit(solution)/shard_map/ppermute | solution.py:487
  49.5 1.7 %collective-permute-done.6 = bf16[1,64,128]{2,1,0:T(8,128)(2,1)S(1)} collective-permute-done((bf16[1,64,128]{2,1,0:T(8,128)(2,1)S(1)}, bf16[1,64,128]{2,1,0:T(8,128)(2,1)S(1)}, u32[]{:S(2)}, u32[]{:S(2)}) %collective-permute-start.6) | collective-permute-done | bytes 16416 | tf_op jit(solution)/shard_map/ppermute | solution.py:487
  51.2 0.8 collective-permute-start.7
  52.0 0.4 values.2.refs_0_
  52.4 2.8 %collective-permute-done.7.coefs_ref = bf16[2,64,128]{2,1,0:T(8,128)(2,1)S(1)} collective-permute-done((bf16[2,64,128]{2,1,0:T(8,128)(2,1)S(1)}, bf16[2,64,128]{2,1,0:T(8,128)(2,1)S(1)}, u32[]{:S(2)}, u32[]{:S(2)}) %collective-permute-start.7) | collective-permute-done | bytes 32800 | tf_op jit(solution)/shard_map/ppermute | solution.py:487
  55.3 0.1 collective-permute-start.8
  55.4 0.0 copy-start
  55.4 0.0 copy-start.1
  55.4 0.0 copy-start.2
  55.4 0.4 values.3.given_values_ref
  55.8 0.8 collective-permute-done.8.coefs_ref
  56.6 3.8 %collective-permute-start.9 = (bf16[2,64,128]{2,1,0:T(8,128)(2,1)S(1)}, bf16[2,64,128]{2,1,0:T(8,128)(2,1)S(1)}, u32[]{:S(2)}, u32[]{:S(2)}) collective-permute-start(bf16[2,64,128]{2,1,0:T(8,128)(2,1)S(1)} %slice_select_fusion), channel_id=1, source_target_pairs={{0,32},{32,64},{64,96},{96,128},{128,160},{160,192},{192,224},{1,3... | collective-permute-start | bytes 98312 | tf_op jit(solution)/shard_map/ppermute | solution.py:502
  60.5 0.0 copy-done
  60.5 0.0 copy-done.1
  60.5 0.0 copy-done.2
  60.5 3.6 %later.1 = (bf16[8,64,4096]{2,1,0:T(8,128)(2,1)}, bf16[8,64,4096]{2,1,0:T(8,128)(2,1)S(1)}, f32[8,64]{1,0:T(8,128)S(1)}) custom-call(s32[1]{0:T(128)} %bitcast.4.first_ref, s32[1,64]{1,0:T(1,128)S(1)} %bitcast.16, s32[1,64]{1,0:T(1,128)S(1)} %bitcast.18, s32[1,64]{1,0:T(1,128)S(1)} %bitcast.20, ...), custom_call_target="tpu_custom_call", output_to_operand_aliasing={{1}: (6, {})} | custom-call | flops 53687091200 | bytes 8388608 | tf_op jit(solution)/shard_map/later/pallas_call | solution.py:422
  64.1 0.7 collective-permute-done.9.prior_coefs_ref
  64.8 1.8 %first.1 = (bf16[8,64,4096]{2,1,0:T(8,128)(2,1)}, f32[32,1,512]{2,1,0:T(1,128)S(1)}) custom-call(s32[1,64]{1,0:T(1,128)S(1)} %bitcast.17, s32[1,64]{1,0:T(1,128)S(1)} %bitcast.19, s32[1,64]{1,0:T(1,128)S(1)} %bitcast.21, bf16[2,64,128]{2,1,0:T(8,128)(2,1)S(1)} %collective-permute-done.9.prior_coefs_ref, ...), custom_call_target="tpu_custom_call", output_to_operand_aliasing={{0}: (7, {})} | custom-call | tf_op jit(solution)/shard_map/first/pallas_call | solution.py:448
  66.6 15.6 %all_to_all.5.parts_ref = f32[32,1,512]{2,1,0:T(1,128)S(1)} all-to-all(f32[32,1,512]{2,1,0:T(1,128)S(1)} %get-tuple-element.45), channel_id=1, replica_groups=mesh['date'=8,'path'=32] {'path'}, dimensions={0} | all-to-all | bytes 131072 | tf_op jit(solution)/shard_map/all_to_all | solution.py:545
  82.2 0.7 total.1
  (10 shorter events, 0.1 us)
Async XLA Ops:
  1.6 12.3 %collective-permute-start.1 = (bf16[2,16,4096]{2,1,0:T(8,128)(2,1)S(1)}, bf16[2,16,4096]{2,1,0:T(8,128)(2,1)S(1)}, u32[]{:S(2)}, u32[]{:S(2)}) collective-permute-start(bf16[2,16,4096]{2,1,0:T(8,128)(2,1)S(1)} %slice.32), channel_id=1, source_target_pairs={{0,32},{32,64},{64,96},{96,128},{128,160},{160,192},{192,224},{1,3... | collective-permute-start | bytes 786440 | tf_op jit(solution)/shard_map/ppermute | solution.py:502
  13.5 4.2 %collective-permute-start = (f32[4,160,128]{2,1,0:T(8,128)S(1)}, f32[4,160,128]{2,1,0:T(8,128)S(1)}, u32[]{:S(2)}, u32[]{:S(2)}) collective-permute-start(f32[4,160,128]{2,1,0:T(8,128)S(1)} %get-tuple-element.31), channel_id=1, source_target_pairs={{0,1},{1,0},{2,3},{3,2},{4,5},{5,4},{6,7},{7,6},{8,9},{9,8},{10,11... | collective-permute-start | bytes 983048 | tf_op jit(solution)/shard_map/ppermute | solution.py:487
  17.7 6.4 %collective-permute-start.2 = (f32[2,160,128]{2,1,0:T(8,128)S(1)}, f32[2,160,128]{2,1,0:T(8,128)S(1)}, u32[]{:S(2)}, u32[]{:S(2)}) collective-permute-start(f32[2,160,128]{2,1,0:T(8,128)S(1)} %select_add_fusion), channel_id=1, source_target_pairs={{0,2},{1,3},{2,0},{3,1},{4,6},{5,7},{6,4},{7,5},{8,10},{9,11},{10,... | collective-permute-start | bytes 491528 | tf_op jit(solution)/shard_map/ppermute | solution.py:487
  24.2 4.5 %collective-permute-start.3 = (f32[160,128]{1,0:T(8,128)S(1)}, f32[160,128]{1,0:T(8,128)S(1)}, u32[]{:S(2)}, u32[]{:S(2)}) collective-permute-start(f32[160,128]{1,0:T(8,128)S(1)} %select_bitcast_fusion), channel_id=1, source_target_pairs={{0,4},{1,5},{2,6},{3,7},{4,0},{5,1},{6,2},{7,3},{8,12},{9,13},{10,... | collective-permute-start | bytes 245768 | tf_op jit(solution)/shard_map/ppermute | solution.py:487
  28.7 6.0 %collective-permute-start.4 = (f32[160,128]{1,0:T(8,128)S(1)}, f32[160,128]{1,0:T(8,128)S(1)}, u32[]{:S(2)}, u32[]{:S(2)}) collective-permute-start(f32[160,128]{1,0:T(8,128)S(1)} %bitcast_add_fusion), channel_id=1, source_target_pairs={{0,8},{1,9},{2,10},{3,11},{4,12},{5,13},{6,14},{7,15},{8,0},{9,1},... | collective-permute-start | bytes 245768 | tf_op jit(solution)/shard_map/ppermute | solution.py:487
  34.7 8.6 %collective-permute-start.5 = (f32[160,128]{1,0:T(8,128)S(1)}, f32[160,128]{1,0:T(8,128)S(1)}, u32[]{:S(2)}, u32[]{:S(2)}) collective-permute-start(f32[160,128]{1,0:T(8,128)S(1)} %add.27.one_ref), channel_id=1, source_target_pairs={{0,24},{1,25},{2,26},{3,27},{4,28},{5,29},{6,30},{7,31},{8,16},{9,... | collective-permute-start | bytes 245768 | tf_op jit(solution)/shard_map/ppermute | solution.py:487
  47.1 4.1 %collective-permute-start.6 = (bf16[1,64,128]{2,1,0:T(8,128)(2,1)S(1)}, bf16[1,64,128]{2,1,0:T(8,128)(2,1)S(1)}, u32[]{:S(2)}, u32[]{:S(2)}) collective-permute-start(bf16[1,64,128]{2,1,0:T(8,128)(2,1)S(1)} %bitcast.15), channel_id=1, source_target_pairs={{0,4},{1,5},{2,6},{3,7},{4,0},{5,1},{6,2},{7,3},{8,12},{9,13},{10,... | collective-permute-start | bytes 49160 | tf_op jit(solution)/shard_map/ppermute | solution.py:487
  51.2 4.0 %collective-permute-start.7 = (bf16[2,64,128]{2,1,0:T(8,128)(2,1)S(1)}, bf16[2,64,128]{2,1,0:T(8,128)(2,1)S(1)}, u32[]{:S(2)}, u32[]{:S(2)}) collective-permute-start(bf16[2,64,128]{2,1,0:T(8,128)(2,1)S(1)} %pad_maximum_fusion.1.coefs_ref), channel_id=1, source_target_pairs={{0,2},{1,3},{2,0},{3,1},{4,6},{5,7},{6,4},{7,5},{8,10},{9,11},{10,... | collective-permute-start | bytes 98312 | tf_op jit(solution)/shard_map/ppermute | solution.py:487
  55.3 1.3 %collective-permute-start.8 = (bf16[4,64,128]{2,1,0:T(8,128)(2,1)S(1)}, bf16[4,64,128]{2,1,0:T(8,128)(2,1)S(1)}, u32[]{:S(2)}, u32[]{:S(2)}) collective-permute-start(bf16[4,64,128]{2,1,0:T(8,128)(2,1)S(1)} %pad_maximum_fusion), channel_id=1, source_target_pairs={{0,1},{1,0},{2,3},{3,2},{4,5},{5,4},{6,7},{7,6},{8,9},{9,8},{10,11... | collective-permute-start | bytes 196616 | tf_op jit(solution)/shard_map/ppermute | solution.py:487
  55.4 5.1 %copy-start = (s32[64]{0:T(128)S(1)}, s32[64]{0:T(128)}, u32[]{:S(2)}) copy-start(s32[64]{0:T(128)} %param.11) | copy-start | bytes 772
  55.4 5.1 %copy-start.1 = (s32[64]{0:T(128)S(1)}, s32[64]{0:T(128)}, u32[]{:S(2)}) copy-start(s32[64]{0:T(128)} %param.12) | copy-start | bytes 772
  55.4 5.1 %copy-start.2 = (s32[64]{0:T(128)S(1)}, s32[64]{0:T(128)}, u32[]{:S(2)}) copy-start(s32[64]{0:T(128)} %param.13) | copy-start | bytes 772
  56.6 8.2 %collective-permute-start.9 = (bf16[2,64,128]{2,1,0:T(8,128)(2,1)S(1)}, bf16[2,64,128]{2,1,0:T(8,128)(2,1)S(1)}, u32[]{:S(2)}, u32[]{:S(2)}) collective-permute-start(bf16[2,64,128]{2,1,0:T(8,128)(2,1)S(1)} %slice_select_fusion), channel_id=1, source_target_pairs={{0,32},{32,64},{64,96},{96,128},{128,160},{160,192},{192,224},{1,3... | collective-permute-start | bytes 98312 | tf_op jit(solution)/shard_map/ppermute | solution.py:502

commit v8 on v7

--- a/solution.py
+++ b/solution.py
@@ -20,7 +20,7 @@
 ROUNDER = 12582912.0
 INV_TWO_PI = 0.15915494309189535
 CHUNK = 512
-PIECES = 2
+PIECES = 4
 BLOCK = 8
 
 
@@ -524,8 +524,8 @@
     kept = picked(kept, near_low) + swapped(picked(kept[::-1], near_low), NEAR)
     kept = kept + swapped(kept, NEXT)
     prior_features = features_of(weights, prior_factors)
-    kept, prior_features = lax.optimization_barrier((kept, prior_features))
-    coefs = solved(kept, swapped(kept, FAR), paths_all)
+    from_far, prior_features = lax.optimization_barrier((swapped(kept, FAR), prior_features))
+    coefs = solved(kept, from_far, paths_all)
     dates = factors.shape[0]
     coefs_c = ordered(coefs[None], swapped(coefs[None], NEAR), near_low)
     coefs_b = swapped(coefs_c, ROW)

time: 84.1 us -> 84 us (level)
  no operation moved by 1% of the time
where the time goes in v8:
time: 84 us; the launch traced here: 82.8 us
  Pallas kernels  27.2 us (32%)
  starting transfers between devices  25.6 us (30%)
  blocking collectives  15.6 us (19%)
  waiting for transfers between devices  12.5 us (15%)
  local copies, waits for them, and re-layouts  0.99 us (1%)
  between operations  0.85 us (1%)
    ppermute x8, starting transfers between devices, swapped(): lax.ppermute(value, 'path', [(i, i ^ step) for i in range(lax.axis_size('...  16.7 us
    all_to_all x1, blocking collectives, local(): lax.all_to_all(parts, 'path', 0, 0, tiled=True)  15.6 us
    pallas_call x3, Pallas kernels, sums_of(): pl.pallas_call(sums_kernel, in_specs=[SCALARS, *specs, IN_HBM, IN_HBM], o...  14.3 us
    ppermute x8, waiting for transfers between devices, swapped(): lax.ppermute(value, 'path', [(i, i ^ step) for i in range(lax.axis_size('...  11.5 us
    ppermute x2, starting transfers between devices, from_earlier(): return lax.ppermute(value, 'date', [(i, i + 1) for i in range(length - 1)])  8.94 us
    pallas_call x1, Pallas kernels, solved(): pl.pallas_call(functools.partial(solve_kernel, paths_all), in_specs=[ON_C...  3.81 us
    pallas_call x1, Pallas kernels, later_exposures(): pl.pallas_call(functools.partial(later_kernel, paths_all), in_specs=[SCAL...  3.63 us
    pallas_call x1, Pallas kernels, features_of(): pl.pallas_call(features_kernel, in_specs=[ON_CHIP, ON_CHIP], out_specs=ON...  2.16 us
  transfers between devices with their start and end apart: 10, of which 9 were waited for; matrix products, arithmetic and copies ran while one was open for 0% of the time, Pallas kernels for 25%

profile of v8, /device:TPU:2, one launch (start us, length us, event | category | flops | bytes accessed | tf_op | source)
XLA Modules:
  0.0 82.8 jit_solution(1995166979512556401)
XLA Ops:
  0.6 1.0 %slice.32 = bf16[2,16,4096]{2,1,0:T(8,128)(2,1)S(1)} slice(bf16[8,16,4096]{2,1,0:T(8,128)(2,1)} %refs_1_.3), slice={[6:8], [0:16], [0:4096]} | slice | bytes 524288 | tf_op jit(solution)/shard_map/slice | solution.py:515
  1.6 5.1 %collective-permute-start.1 = (bf16[2,16,4096]{2,1,0:T(8,128)(2,1)S(1)}, bf16[2,16,4096]{2,1,0:T(8,128)(2,1)S(1)}, u32[]{:S(2)}, u32[]{:S(2)}) collective-permute-start(bf16[2,16,4096]{2,1,0:T(8,128)(2,1)S(1)} %slice.32), channel_id=1, source_target_pairs={{0,32},{32,64},{64,96},{96,128},{128,160},{160,192},{192,224},{1,3... | collective-permute-start | bytes 786440 | tf_op jit(solution)/shard_map/ppermute | solution.py:502
  6.7 6.8 %sums.3 = (bf16[4,128,4096]{2,1,0:T(8,128)(2,1)S(1)}, f32[4,160,128]{2,1,0:T(8,128)S(1)}, bf16[128,64]{1,0:T(8,128)(2,1)S(1)}) custom-call(s32[1]{0:T(128)} %bitcast.4.first_ref, bf16[16,128]{1,0:T(8,128)(2,1)} %bitcast.22, f32[1,128]{1,0:T(1,128)} %bitcast.23, bf16[8,16,4096]{2,1,0:T(8,128)(2,1)} %refs_1_.3, bf16[8,64,4096]{2,1,0:T(8,128)(2,1)} %refs_2_.5), custom_call_target="tpu_custom_call" | custom-call | flops 41943040000 | bytes 8388608 | tf_op jit(solution)/shard_map/sums/pallas_call | solution.py:207
  13.5 0.1 collective-permute-start
  13.6 0.3 collective-permute-done.1.factors_ref
  13.9 3.7 %sums.5 = (bf16[2,128,4096]{2,1,0:T(8,128)(2,1)S(1)}, f32[2,160,128]{2,1,0:T(8,128)S(1)}) custom-call(s32[1]{0:T(128)} %bitcast.7.first_ref, bf16[128,64]{1,0:T(8,128)(2,1)S(1)} %get-tuple-element.29.refs_0_.weights_ref, bf16[8,16,4096]{2,1,0:T(8,128)(2,1)} %refs_1_.3, bf16[8,64,4096]{2,1,0:T(8,128)(2,1)} %refs_2_.5), custom_call_target="tpu_custom_call" | custom-call | flops 20971520000 | bytes 4194304 | tf_op jit(solution)/shard_map/sums/pallas_call | solution.py:207
  17.7 0.0 collective-permute-done
  17.7 1.7 %collective-permute-start.2 = (f32[2,160,128]{2,1,0:T(8,128)S(1)}, f32[2,160,128]{2,1,0:T(8,128)S(1)}, u32[]{:S(2)}, u32[]{:S(2)}) collective-permute-start(f32[2,160,128]{2,1,0:T(8,128)S(1)} %select_add_fusion), channel_id=1, source_target_pairs={{0,2},{1,3},{2,0},{3,1},{4,6},{5,7},{6,4},{7,5},{8,10},{9,11},{10,... | collective-permute-start | bytes 491528 | tf_op jit(solution)/shard_map/ppermute | solution.py:487
  19.4 3.7 %sums.4 = (bf16[2,128,4096]{2,1,0:T(8,128)(2,1)S(1)}, f32[2,160,128]{2,1,0:T(8,128)S(1)}) custom-call(s32[1]{0:T(128)} %bitcast.3.first_ref, bf16[128,64]{1,0:T(8,128)(2,1)S(1)} %get-tuple-element.29.refs_0_.weights_ref, bf16[8,16,4096]{2,1,0:T(8,128)(2,1)} %refs_1_.3, bf16[8,64,4096]{2,1,0:T(8,128)(2,1)} %refs_2_.5), custom_call_target="tpu_custom_call" | custom-call | flops 20971520000 | bytes 4194304 | tf_op jit(solution)/shard_map/sums/pallas_call | solution.py:207
  23.1 1.0 %collective-permute-done.2 = f32[2,160,128]{2,1,0:T(8,128)S(1)} collective-permute-done((f32[2,160,128]{2,1,0:T(8,128)S(1)}, f32[2,160,128]{2,1,0:T(8,128)S(1)}, u32[]{:S(2)}, u32[]{:S(2)}) %collective-permute-start.2) | collective-permute-done | bytes 163872 | tf_op jit(solution)/shard_map/ppermute | solution.py:487
  24.2 2.0 %collective-permute-start.3 = (f32[160,128]{1,0:T(8,128)S(1)}, f32[160,128]{1,0:T(8,128)S(1)}, u32[]{:S(2)}, u32[]{:S(2)}) collective-permute-start(f32[160,128]{1,0:T(8,128)S(1)} %select_bitcast_fusion), channel_id=1, source_target_pairs={{0,4},{1,5},{2,6},{3,7},{4,0},{5,1},{6,2},{7,3},{8,12},{9,13},{10,... | collective-permute-start | bytes 245768 | tf_op jit(solution)/shard_map/ppermute | solution.py:487
  26.2 2.5 %collective-permute-done.3 = f32[160,128]{1,0:T(8,128)S(1)} collective-permute-done((f32[160,128]{1,0:T(8,128)S(1)}, f32[160,128]{1,0:T(8,128)S(1)}, u32[]{:S(2)}, u32[]{:S(2)}) %collective-permute-start.3) | collective-permute-done | bytes 81952 | tf_op jit(solution)/shard_map/ppermute | solution.py:487
  28.7 3.5 %collective-permute-start.4 = (f32[160,128]{1,0:T(8,128)S(1)}, f32[160,128]{1,0:T(8,128)S(1)}, u32[]{:S(2)}, u32[]{:S(2)}) collective-permute-start(f32[160,128]{1,0:T(8,128)S(1)} %bitcast_add_fusion), channel_id=1, source_target_pairs={{0,8},{1,9},{2,10},{3,11},{4,12},{5,13},{6,14},{7,15},{8,0},{9,1},... | collective-permute-start | bytes 245768 | tf_op jit(solution)/shard_map/ppermute | solution.py:487
  32.3 2.4 %collective-permute-done.4 = f32[160,128]{1,0:T(8,128)S(1)} collective-permute-done((f32[160,128]{1,0:T(8,128)S(1)}, f32[160,128]{1,0:T(8,128)S(1)}, u32[]{:S(2)}, u32[]{:S(2)}) %collective-permute-start.4) | collective-permute-done | bytes 81952 | tf_op jit(solution)/shard_map/ppermute | solution.py:487
  34.7 6.1 %collective-permute-start.5 = (f32[160,128]{1,0:T(8,128)S(1)}, f32[160,128]{1,0:T(8,128)S(1)}, u32[]{:S(2)}, u32[]{:S(2)}) collective-permute-start(f32[160,128]{1,0:T(8,128)S(1)} %add.27.one_ref), channel_id=1, source_target_pairs={{0,24},{1,25},{2,26},{3,27},{4,28},{5,29},{6,30},{7,31},{8,16},{9,... | collective-permute-start | bytes 245768 | tf_op jit(solution)/shard_map/ppermute | solution.py:487
  40.8 2.2 %features.1.prior_features_ref = bf16[2,128,4096]{2,1,0:T(8,128)(2,1)S(1)} custom-call(bf16[128,64]{1,0:T(8,128)(2,1)S(1)} %get-tuple-element.29.refs_0_.weights_ref, bf16[2,16,4096]{2,1,0:T(8,128)(2,1)S(1)} %collective-permute-done.1.factors_ref), custom_call_target="tpu_custom_call" | custom-call | flops 2097152000 | bytes 2097152 | tf_op jit(solution)/shard_map/features/pallas_call | solution.py:174
  43.0 0.3 collective-permute-done.5.two_ref
  43.3 3.8 %solve.1 = bf16[64,128]{1,0:T(8,128)(2,1)S(1)} custom-call(f32[160,128]{1,0:T(8,128)S(1)} %add.27.one_ref, f32[160,128]{1,0:T(8,128)S(1)} %collective-permute-done.5.two_ref), custom_call_target="tpu_custom_call" | custom-call | tf_op jit(solution)/shard_map/solve/pallas_call | solution.py:259
  47.1 2.4 %collective-permute-start.6 = (bf16[1,64,128]{2,1,0:T(8,128)(2,1)S(1)}, bf16[1,64,128]{2,1,0:T(8,128)(2,1)S(1)}, u32[]{:S(2)}, u32[]{:S(2)}) collective-permute-start(bf16[1,64,128]{2,1,0:T(8,128)(2,1)S(1)} %bitcast.15), channel_id=1, source_target_pairs={{0,4},{1,5},{2,6},{3,7},{4,0},{5,1},{6,2},{7,3},{8,12},{9,13},{10,... | collective-permute-start | bytes 49160 | tf_op jit(solution)/shard_map/ppermute | solution.py:487
  49.5 1.7 %collective-permute-done.6 = bf16[1,64,128]{2,1,0:T(8,128)(2,1)S(1)} collective-permute-done((bf16[1,64,128]{2,1,0:T(8,128)(2,1)S(1)}, bf16[1,64,128]{2,1,0:T(8,128)(2,1)S(1)}, u32[]{:S(2)}, u32[]{:S(2)}) %collective-permute-start.6) | collective-permute-done | bytes 16416 | tf_op jit(solution)/shard_map/ppermute | solution.py:487
  51.2 0.8 collective-permute-start.7
  52.0 0.4 values.2.refs_0_
  52.4 2.8 %collective-permute-done.7.coefs_ref = bf16[2,64,128]{2,1,0:T(8,128)(2,1)S(1)} collective-permute-done((bf16[2,64,128]{2,1,0:T(8,128)(2,1)S(1)}, bf16[2,64,128]{2,1,0:T(8,128)(2,1)S(1)}, u32[]{:S(2)}, u32[]{:S(2)}) %collective-permute-start.7) | collective-permute-done | bytes 32800 | tf_op jit(solution)/shard_map/ppermute | solution.py:487
  55.3 0.1 collective-permute-start.8
  55.4 0.0 copy-start
  55.4 0.0 copy-start.1
  55.4 0.0 copy-start.2
  55.4 0.4 values.3.given_values_ref
  55.8 0.8 collective-permute-done.8.coefs_ref
  56.6 3.8 %collective-permute-start.9 = (bf16[2,64,128]{2,1,0:T(8,128)(2,1)S(1)}, bf16[2,64,128]{2,1,0:T(8,128)(2,1)S(1)}, u32[]{:S(2)}, u32[]{:S(2)}) collective-permute-start(bf16[2,64,128]{2,1,0:T(8,128)(2,1)S(1)} %slice_select_fusion), channel_id=1, source_target_pairs={{0,32},{32,64},{64,96},{96,128},{128,160},{160,192},{192,224},{1,3... | collective-permute-start | bytes 98312 | tf_op jit(solution)/shard_map/ppermute | solution.py:502
  60.5 0.0 copy-done
  60.5 0.0 copy-done.1
  60.5 0.0 copy-done.2
  60.5 3.6 %later.1 = (bf16[8,64,4096]{2,1,0:T(8,128)(2,1)}, bf16[8,64,4096]{2,1,0:T(8,128)(2,1)S(1)}, f32[8,64]{1,0:T(8,128)S(1)}) custom-call(s32[1]{0:T(128)} %bitcast.4.first_ref, s32[1,64]{1,0:T(1,128)S(1)} %bitcast.16, s32[1,64]{1,0:T(1,128)S(1)} %bitcast.18, s32[1,64]{1,0:T(1,128)S(1)} %bitcast.20, ...), custom_call_target="tpu_custom_call", output_to_operand_aliasing={{1}: (6, {})} | custom-call | flops 53687091200 | bytes 8388608 | tf_op jit(solution)/shard_map/later/pallas_call | solution.py:422
  64.1 0.7 collective-permute-done.9.prior_coefs_ref
  64.8 1.7 %first.1 = (bf16[8,64,4096]{2,1,0:T(8,128)(2,1)}, f32[32,1,512]{2,1,0:T(1,128)S(1)}) custom-call(s32[1,64]{1,0:T(1,128)S(1)} %bitcast.17, s32[1,64]{1,0:T(1,128)S(1)} %bitcast.19, s32[1,64]{1,0:T(1,128)S(1)} %bitcast.21, bf16[2,64,128]{2,1,0:T(8,128)(2,1)S(1)} %collective-permute-done.9.prior_coefs_ref, ...), custom_call_target="tpu_custom_call", output_to_operand_aliasing={{0}: (7, {})} | custom-call | tf_op jit(solution)/shard_map/first/pallas_call | solution.py:448
  66.5 15.6 %all_to_all.5.parts_ref = f32[32,1,512]{2,1,0:T(1,128)S(1)} all-to-all(f32[32,1,512]{2,1,0:T(1,128)S(1)} %get-tuple-element.45), channel_id=1, replica_groups=mesh['date'=8,'path'=32] {'path'}, dimensions={0} | all-to-all | bytes 131072 | tf_op jit(solution)/shard_map/all_to_all | solution.py:545
  82.1 0.7 total.1
  (10 shorter events, 0.1 us)
Async XLA Ops:
  1.6 12.3 %collective-permute-start.1 = (bf16[2,16,4096]{2,1,0:T(8,128)(2,1)S(1)}, bf16[2,16,4096]{2,1,0:T(8,128)(2,1)S(1)}, u32[]{:S(2)}, u32[]{:S(2)}) collective-permute-start(bf16[2,16,4096]{2,1,0:T(8,128)(2,1)S(1)} %slice.32), channel_id=1, source_target_pairs={{0,32},{32,64},{64,96},{96,128},{128,160},{160,192},{192,224},{1,3... | collective-permute-start | bytes 786440 | tf_op jit(solution)/shard_map/ppermute | solution.py:502
  13.5 4.2 %collective-permute-start = (f32[4,160,128]{2,1,0:T(8,128)S(1)}, f32[4,160,128]{2,1,0:T(8,128)S(1)}, u32[]{:S(2)}, u32[]{:S(2)}) collective-permute-start(f32[4,160,128]{2,1,0:T(8,128)S(1)} %get-tuple-element.31), channel_id=1, source_target_pairs={{0,1},{1,0},{2,3},{3,2},{4,5},{5,4},{6,7},{7,6},{8,9},{9,8},{10,11... | collective-permute-start | bytes 983048 | tf_op jit(solution)/shard_map/ppermute | solution.py:487
  17.7 6.4 %collective-permute-start.2 = (f32[2,160,128]{2,1,0:T(8,128)S(1)}, f32[2,160,128]{2,1,0:T(8,128)S(1)}, u32[]{:S(2)}, u32[]{:S(2)}) collective-permute-start(f32[2,160,128]{2,1,0:T(8,128)S(1)} %select_add_fusion), channel_id=1, source_target_pairs={{0,2},{1,3},{2,0},{3,1},{4,6},{5,7},{6,4},{7,5},{8,10},{9,11},{10,... | collective-permute-start | bytes 491528 | tf_op jit(solution)/shard_map/ppermute | solution.py:487
  24.2 4.5 %collective-permute-start.3 = (f32[160,128]{1,0:T(8,128)S(1)}, f32[160,128]{1,0:T(8,128)S(1)}, u32[]{:S(2)}, u32[]{:S(2)}) collective-permute-start(f32[160,128]{1,0:T(8,128)S(1)} %select_bitcast_fusion), channel_id=1, source_target_pairs={{0,4},{1,5},{2,6},{3,7},{4,0},{5,1},{6,2},{7,3},{8,12},{9,13},{10,... | collective-permute-start | bytes 245768 | tf_op jit(solution)/shard_map/ppermute | solution.py:487
  28.7 6.0 %collective-permute-start.4 = (f32[160,128]{1,0:T(8,128)S(1)}, f32[160,128]{1,0:T(8,128)S(1)}, u32[]{:S(2)}, u32[]{:S(2)}) collective-permute-start(f32[160,128]{1,0:T(8,128)S(1)} %bitcast_add_fusion), channel_id=1, source_target_pairs={{0,8},{1,9},{2,10},{3,11},{4,12},{5,13},{6,14},{7,15},{8,0},{9,1},... | collective-permute-start | bytes 245768 | tf_op jit(solution)/shard_map/ppermute | solution.py:487
  34.7 8.6 %collective-permute-start.5 = (f32[160,128]{1,0:T(8,128)S(1)}, f32[160,128]{1,0:T(8,128)S(1)}, u32[]{:S(2)}, u32[]{:S(2)}) collective-permute-start(f32[160,128]{1,0:T(8,128)S(1)} %add.27.one_ref), channel_id=1, source_target_pairs={{0,24},{1,25},{2,26},{3,27},{4,28},{5,29},{6,30},{7,31},{8,16},{9,... | collective-permute-start | bytes 245768 | tf_op jit(solution)/shard_map/ppermute | solution.py:487
  47.1 4.1 %collective-permute-start.6 = (bf16[1,64,128]{2,1,0:T(8,128)(2,1)S(1)}, bf16[1,64,128]{2,1,0:T(8,128)(2,1)S(1)}, u32[]{:S(2)}, u32[]{:S(2)}) collective-permute-start(bf16[1,64,128]{2,1,0:T(8,128)(2,1)S(1)} %bitcast.15), channel_id=1, source_target_pairs={{0,4},{1,5},{2,6},{3,7},{4,0},{5,1},{6,2},{7,3},{8,12},{9,13},{10,... | collective-permute-start | bytes 49160 | tf_op jit(solution)/shard_map/ppermute | solution.py:487
  51.2 4.0 %collective-permute-start.7 = (bf16[2,64,128]{2,1,0:T(8,128)(2,1)S(1)}, bf16[2,64,128]{2,1,0:T(8,128)(2,1)S(1)}, u32[]{:S(2)}, u32[]{:S(2)}) collective-permute-start(bf16[2,64,128]{2,1,0:T(8,128)(2,1)S(1)} %pad_maximum_fusion.1.coefs_ref), channel_id=1, source_target_pairs={{0,2},{1,3},{2,0},{3,1},{4,6},{5,7},{6,4},{7,5},{8,10},{9,11},{10,... | collective-permute-start | bytes 98312 | tf_op jit(solution)/shard_map/ppermute | solution.py:487
  55.3 1.3 %collective-permute-start.8 = (bf16[4,64,128]{2,1,0:T(8,128)(2,1)S(1)}, bf16[4,64,128]{2,1,0:T(8,128)(2,1)S(1)}, u32[]{:S(2)}, u32[]{:S(2)}) collective-permute-start(bf16[4,64,128]{2,1,0:T(8,128)(2,1)S(1)} %pad_maximum_fusion), channel_id=1, source_target_pairs={{0,1},{1,0},{2,3},{3,2},{4,5},{5,4},{6,7},{7,6},{8,9},{9,8},{10,11... | collective-permute-start | bytes 196616 | tf_op jit(solution)/shard_map/ppermute | solution.py:487
  55.4 5.1 %copy-start = (s32[64]{0:T(128)S(1)}, s32[64]{0:T(128)}, u32[]{:S(2)}) copy-start(s32[64]{0:T(128)} %param.11) | copy-start | bytes 772
  55.4 5.1 %copy-start.1 = (s32[64]{0:T(128)S(1)}, s32[64]{0:T(128)}, u32[]{:S(2)}) copy-start(s32[64]{0:T(128)} %param.12) | copy-start | bytes 772
  55.4 5.1 %copy-start.2 = (s32[64]{0:T(128)S(1)}, s32[64]{0:T(128)}, u32[]{:S(2)}) copy-start(s32[64]{0:T(128)} %param.13) | copy-start | bytes 772
  56.6 8.2 %collective-permute-start.9 = (bf16[2,64,128]{2,1,0:T(8,128)(2,1)S(1)}, bf16[2,64,128]{2,1,0:T(8,128)(2,1)S(1)}, u32[]{:S(2)}, u32[]{:S(2)}) collective-permute-start(bf16[2,64,128]{2,1,0:T(8,128)(2,1)S(1)} %slice_select_fusion), channel_id=1, source_target_pairs={{0,32},{32,64},{64,96},{96,128},{128,160},{160,192},{192,224},{1,3... | collective-permute-start | bytes 98312 | tf_op jit(solution)/shard_map/ppermute | solution.py:502

commit v9 on v8

--- a/solution.py
+++ b/solution.py
@@ -343,9 +343,16 @@
             )
             staged_ref[t - LAG_MAX, :, span] = exposed.astype(jnp.bfloat16)
             totals[t] += by_lane(exposed)
-        at = t - LAG_MAX
-        copies.append(pltpu.make_async_copy(staged_ref.at[at], exposure_ref.at[t], sems.at[at]))
-        copies[-1].start()
+            if (at + CHUNK) % (paths // PIECES) == 0:
+                there = pl.ds(at + CHUNK - paths // PIECES, paths // PIECES)
+                copies.append(
+                    pltpu.make_async_copy(
+                        staged_ref.at[t - LAG_MAX, :, there],
+                        exposure_ref.at[t, :, there],
+                        sems.at[len(copies)],
+                    )
+                )
+                copies[-1].start()
     profile_ref[...] = profile_of(totals, paths_all, dates)
     for copy in copies:
         copy.wait()
@@ -430,7 +437,7 @@
         ),
         scratch_shapes=[
             pltpu.VMEM((dates - LAG_MAX, sets, paths), jnp.bfloat16),
-            pltpu.SemaphoreType.DMA((dates - LAG_MAX,)),
+            pltpu.SemaphoreType.DMA(((dates - LAG_MAX) * PIECES,)),
         ],
         input_output_aliases={len(args) - 1: 1},
         compiler_params=params(12),

time: 84 us -> 84.1 us (level)
  no operation moved by 1% of the time
where the time goes in v9:
time: 84.1 us; the launch traced here: 82.8 us
  Pallas kernels  27.2 us (32%)
  starting transfers between devices  25.6 us (30%)
  blocking collectives  15.6 us (19%)
  waiting for transfers between devices  12.4 us (15%)
  local copies, waits for them, and re-layouts  0.99 us (1%)
  between operations  0.85 us (1%)
    ppermute x8, starting transfers between devices, swapped(): lax.ppermute(value, 'path', [(i, i ^ step) for i in range(lax.axis_size('...  16.7 us
    all_to_all x1, blocking collectives, local(): lax.all_to_all(parts, 'path', 0, 0, tiled=True)  15.6 us
    pallas_call x3, Pallas kernels, sums_of(): pl.pallas_call(sums_kernel, in_specs=[SCALARS, *specs, IN_HBM, IN_HBM], o...  14.3 us
    ppermute x8, waiting for transfers between devices, swapped(): lax.ppermute(value, 'path', [(i, i ^ step) for i in range(lax.axis_size('...  11.5 us
    ppermute x2, starting transfers between devices, from_earlier(): return lax.ppermute(value, 'date', [(i, i + 1) for i in range(length - 1)])  8.94 us
    pallas_call x1, Pallas kernels, solved(): pl.pallas_call(functools.partial(solve_kernel, paths_all), in_specs=[ON_C...  3.81 us
    pallas_call x1, Pallas kernels, later_exposures(): pl.pallas_call(functools.partial(later_kernel, paths_all), in_specs=[SCAL...  3.7 us
    pallas_call x1, Pallas kernels, features_of(): pl.pallas_call(features_kernel, in_specs=[ON_CHIP, ON_CHIP], out_specs=ON...  2.16 us
  transfers between devices with their start and end apart: 10, of which 9 were waited for; matrix products, arithmetic and copies ran while one was open for 0% of the time, Pallas kernels for 25%

profile of v9, /device:TPU:2, one launch (start us, length us, event | category | flops | bytes accessed | tf_op | source)
XLA Modules:
  0.0 82.8 jit_solution(4186577184548119556)
XLA Ops:
  0.6 1.0 %slice.32 = bf16[2,16,4096]{2,1,0:T(8,128)(2,1)S(1)} slice(bf16[8,16,4096]{2,1,0:T(8,128)(2,1)} %refs_1_.3), slice={[6:8], [0:16], [0:4096]} | slice | bytes 524288 | tf_op jit(solution)/shard_map/slice | solution.py:522
  1.6 5.1 %collective-permute-start.1 = (bf16[2,16,4096]{2,1,0:T(8,128)(2,1)S(1)}, bf16[2,16,4096]{2,1,0:T(8,128)(2,1)S(1)}, u32[]{:S(2)}, u32[]{:S(2)}) collective-permute-start(bf16[2,16,4096]{2,1,0:T(8,128)(2,1)S(1)} %slice.32), channel_id=1, source_target_pairs={{0,32},{32,64},{64,96},{96,128},{128,160},{160,192},{192,224},{1,3... | collective-permute-start | bytes 786440 | tf_op jit(solution)/shard_map/ppermute | solution.py:509
  6.7 6.8 %sums.3 = (bf16[4,128,4096]{2,1,0:T(8,128)(2,1)S(1)}, f32[4,160,128]{2,1,0:T(8,128)S(1)}, bf16[128,64]{1,0:T(8,128)(2,1)S(1)}) custom-call(s32[1]{0:T(128)} %bitcast.4.first_ref, bf16[16,128]{1,0:T(8,128)(2,1)} %bitcast.22, f32[1,128]{1,0:T(1,128)} %bitcast.23, bf16[8,16,4096]{2,1,0:T(8,128)(2,1)} %refs_1_.3, bf16[8,64,4096]{2,1,0:T(8,128)(2,1)} %refs_2_.5), custom_call_target="tpu_custom_call" | custom-call | flops 41943040000 | bytes 8388608 | tf_op jit(solution)/shard_map/sums/pallas_call | solution.py:207
  13.5 0.1 collective-permute-start
  13.6 0.3 collective-permute-done.1.factors_ref
  13.9 3.7 %sums.5 = (bf16[2,128,4096]{2,1,0:T(8,128)(2,1)S(1)}, f32[2,160,128]{2,1,0:T(8,128)S(1)}) custom-call(s32[1]{0:T(128)} %bitcast.7.first_ref, bf16[128,64]{1,0:T(8,128)(2,1)S(1)} %get-tuple-element.29.refs_0_.weights_ref, bf16[8,16,4096]{2,1,0:T(8,128)(2,1)} %refs_1_.3, bf16[8,64,4096]{2,1,0:T(8,128)(2,1)} %refs_2_.5), custom_call_target="tpu_custom_call" | custom-call | flops 20971520000 | bytes 4194304 | tf_op jit(solution)/shard_map/sums/pallas_call | solution.py:207
  17.7 0.0 collective-permute-done
  17.7 1.7 %collective-permute-start.2 = (f32[2,160,128]{2,1,0:T(8,128)S(1)}, f32[2,160,128]{2,1,0:T(8,128)S(1)}, u32[]{:S(2)}, u32[]{:S(2)}) collective-permute-start(f32[2,160,128]{2,1,0:T(8,128)S(1)} %select_add_fusion), channel_id=1, source_target_pairs={{0,2},{1,3},{2,0},{3,1},{4,6},{5,7},{6,4},{7,5},{8,10},{9,11},{10,... | collective-permute-start | bytes 491528 | tf_op jit(solution)/shard_map/ppermute | solution.py:494
  19.4 3.7 %sums.4 = (bf16[2,128,4096]{2,1,0:T(8,128)(2,1)S(1)}, f32[2,160,128]{2,1,0:T(8,128)S(1)}) custom-call(s32[1]{0:T(128)} %bitcast.3.first_ref, bf16[128,64]{1,0:T(8,128)(2,1)S(1)} %get-tuple-element.29.refs_0_.weights_ref, bf16[8,16,4096]{2,1,0:T(8,128)(2,1)} %refs_1_.3, bf16[8,64,4096]{2,1,0:T(8,128)(2,1)} %refs_2_.5), custom_call_target="tpu_custom_call" | custom-call | flops 20971520000 | bytes 4194304 | tf_op jit(solution)/shard_map/sums/pallas_call | solution.py:207
  23.1 1.0 %collective-permute-done.2 = f32[2,160,128]{2,1,0:T(8,128)S(1)} collective-permute-done((f32[2,160,128]{2,1,0:T(8,128)S(1)}, f32[2,160,128]{2,1,0:T(8,128)S(1)}, u32[]{:S(2)}, u32[]{:S(2)}) %collective-permute-start.2) | collective-permute-done | bytes 163872 | tf_op jit(solution)/shard_map/ppermute | solution.py:494
  24.2 2.0 %collective-permute-start.3 = (f32[160,128]{1,0:T(8,128)S(1)}, f32[160,128]{1,0:T(8,128)S(1)}, u32[]{:S(2)}, u32[]{:S(2)}) collective-permute-start(f32[160,128]{1,0:T(8,128)S(1)} %select_bitcast_fusion), channel_id=1, source_target_pairs={{0,4},{1,5},{2,6},{3,7},{4,0},{5,1},{6,2},{7,3},{8,12},{9,13},{10,... | collective-permute-start | bytes 245768 | tf_op jit(solution)/shard_map/ppermute | solution.py:494
  26.2 2.5 %collective-permute-done.3 = f32[160,128]{1,0:T(8,128)S(1)} collective-permute-done((f32[160,128]{1,0:T(8,128)S(1)}, f32[160,128]{1,0:T(8,128)S(1)}, u32[]{:S(2)}, u32[]{:S(2)}) %collective-permute-start.3) | collective-permute-done | bytes 81952 | tf_op jit(solution)/shard_map/ppermute | solution.py:494
  28.7 3.5 %collective-permute-start.4 = (f32[160,128]{1,0:T(8,128)S(1)}, f32[160,128]{1,0:T(8,128)S(1)}, u32[]{:S(2)}, u32[]{:S(2)}) collective-permute-start(f32[160,128]{1,0:T(8,128)S(1)} %bitcast_add_fusion), channel_id=1, source_target_pairs={{0,8},{1,9},{2,10},{3,11},{4,12},{5,13},{6,14},{7,15},{8,0},{9,1},... | collective-permute-start | bytes 245768 | tf_op jit(solution)/shard_map/ppermute | solution.py:494
  32.3 2.4 %collective-permute-done.4 = f32[160,128]{1,0:T(8,128)S(1)} collective-permute-done((f32[160,128]{1,0:T(8,128)S(1)}, f32[160,128]{1,0:T(8,128)S(1)}, u32[]{:S(2)}, u32[]{:S(2)}) %collective-permute-start.4) | collective-permute-done | bytes 81952 | tf_op jit(solution)/shard_map/ppermute | solution.py:494
  34.7 6.1 %collective-permute-start.5 = (f32[160,128]{1,0:T(8,128)S(1)}, f32[160,128]{1,0:T(8,128)S(1)}, u32[]{:S(2)}, u32[]{:S(2)}) collective-permute-start(f32[160,128]{1,0:T(8,128)S(1)} %add.27.one_ref), channel_id=1, source_target_pairs={{0,24},{1,25},{2,26},{3,27},{4,28},{5,29},{6,30},{7,31},{8,16},{9,... | collective-permute-start | bytes 245768 | tf_op jit(solution)/shard_map/ppermute | solution.py:494
  40.8 2.2 %features.1.prior_features_ref = bf16[2,128,4096]{2,1,0:T(8,128)(2,1)S(1)} custom-call(bf16[128,64]{1,0:T(8,128)(2,1)S(1)} %get-tuple-element.29.refs_0_.weights_ref, bf16[2,16,4096]{2,1,0:T(8,128)(2,1)S(1)} %collective-permute-done.1.factors_ref), custom_call_target="tpu_custom_call" | custom-call | flops 2097152000 | bytes 2097152 | tf_op jit(solution)/shard_map/features/pallas_call | solution.py:174
  43.0 0.3 collective-permute-done.5.two_ref
  43.3 3.8 %solve.1 = bf16[64,128]{1,0:T(8,128)(2,1)S(1)} custom-call(f32[160,128]{1,0:T(8,128)S(1)} %add.27.one_ref, f32[160,128]{1,0:T(8,128)S(1)} %collective-permute-done.5.two_ref), custom_call_target="tpu_custom_call" | custom-call | tf_op jit(solution)/shard_map/solve/pallas_call | solution.py:259
  47.1 2.4 %collective-permute-start.6 = (bf16[1,64,128]{2,1,0:T(8,128)(2,1)S(1)}, bf16[1,64,128]{2,1,0:T(8,128)(2,1)S(1)}, u32[]{:S(2)}, u32[]{:S(2)}) collective-permute-start(bf16[1,64,128]{2,1,0:T(8,128)(2,1)S(1)} %bitcast.15), channel_id=1, source_target_pairs={{0,4},{1,5},{2,6},{3,7},{4,0},{5,1},{6,2},{7,3},{8,12},{9,13},{10,... | collective-permute-start | bytes 49160 | tf_op jit(solution)/shard_map/ppermute | solution.py:494
  49.5 1.7 %collective-permute-done.6 = bf16[1,64,128]{2,1,0:T(8,128)(2,1)S(1)} collective-permute-done((bf16[1,64,128]{2,1,0:T(8,128)(2,1)S(1)}, bf16[1,64,128]{2,1,0:T(8,128)(2,1)S(1)}, u32[]{:S(2)}, u32[]{:S(2)}) %collective-permute-start.6) | collective-permute-done | bytes 16416 | tf_op jit(solution)/shard_map/ppermute | solution.py:494
  51.2 0.8 collective-permute-start.7
  52.0 0.4 values.2.refs_0_
  52.4 2.8 %collective-permute-done.7.coefs_ref = bf16[2,64,128]{2,1,0:T(8,128)(2,1)S(1)} collective-permute-done((bf16[2,64,128]{2,1,0:T(8,128)(2,1)S(1)}, bf16[2,64,128]{2,1,0:T(8,128)(2,1)S(1)}, u32[]{:S(2)}, u32[]{:S(2)}) %collective-permute-start.7) | collective-permute-done | bytes 32800 | tf_op jit(solution)/shard_map/ppermute | solution.py:494
  55.3 0.1 collective-permute-start.8
  55.4 0.0 copy-start
  55.4 0.0 copy-start.1
  55.4 0.0 copy-start.2
  55.4 0.4 values.3.given_values_ref
  55.8 0.8 collective-permute-done.8.coefs_ref
  56.6 3.8 %collective-permute-start.9 = (bf16[2,64,128]{2,1,0:T(8,128)(2,1)S(1)}, bf16[2,64,128]{2,1,0:T(8,128)(2,1)S(1)}, u32[]{:S(2)}, u32[]{:S(2)}) collective-permute-start(bf16[2,64,128]{2,1,0:T(8,128)(2,1)S(1)} %slice_select_fusion), channel_id=1, source_target_pairs={{0,32},{32,64},{64,96},{96,128},{128,160},{160,192},{192,224},{1,3... | collective-permute-start | bytes 98312 | tf_op jit(solution)/shard_map/ppermute | solution.py:509
  60.5 0.0 copy-done
  60.5 0.0 copy-done.1
  60.5 0.0 copy-done.2
  60.5 3.7 %later.1 = (bf16[8,64,4096]{2,1,0:T(8,128)(2,1)}, bf16[8,64,4096]{2,1,0:T(8,128)(2,1)S(1)}, f32[8,64]{1,0:T(8,128)S(1)}) custom-call(s32[1]{0:T(128)} %bitcast.4.first_ref, s32[1,64]{1,0:T(1,128)S(1)} %bitcast.16, s32[1,64]{1,0:T(1,128)S(1)} %bitcast.18, s32[1,64]{1,0:T(1,128)S(1)} %bitcast.20, ...), custom_call_target="tpu_custom_call", output_to_operand_aliasing={{1}: (6, {})} | custom-call | flops 53687091200 | bytes 8388608 | tf_op jit(solution)/shard_map/later/pallas_call | solution.py:429
  64.2 0.6 collective-permute-done.9.prior_coefs_ref
  64.8 1.7 %first.1 = (bf16[8,64,4096]{2,1,0:T(8,128)(2,1)}, f32[32,1,512]{2,1,0:T(1,128)S(1)}) custom-call(s32[1,64]{1,0:T(1,128)S(1)} %bitcast.17, s32[1,64]{1,0:T(1,128)S(1)} %bitcast.19, s32[1,64]{1,0:T(1,128)S(1)} %bitcast.21, bf16[2,64,128]{2,1,0:T(8,128)(2,1)S(1)} %collective-permute-done.9.prior_coefs_ref, ...), custom_call_target="tpu_custom_call", output_to_operand_aliasing={{0}: (7, {})} | custom-call | tf_op jit(solution)/shard_map/first/pallas_call | solution.py:455
  66.5 15.6 %all_to_all.5.parts_ref = f32[32,1,512]{2,1,0:T(1,128)S(1)} all-to-all(f32[32,1,512]{2,1,0:T(1,128)S(1)} %get-tuple-element.45), channel_id=1, replica_groups=mesh['date'=8,'path'=32] {'path'}, dimensions={0} | all-to-all | bytes 131072 | tf_op jit(solution)/shard_map/all_to_all | solution.py:552
  82.1 0.7 total.1
  (10 shorter events, 0.1 us)
Async XLA Ops:
  1.6 12.3 %collective-permute-start.1 = (bf16[2,16,4096]{2,1,0:T(8,128)(2,1)S(1)}, bf16[2,16,4096]{2,1,0:T(8,128)(2,1)S(1)}, u32[]{:S(2)}, u32[]{:S(2)}) collective-permute-start(bf16[2,16,4096]{2,1,0:T(8,128)(2,1)S(1)} %slice.32), channel_id=1, source_target_pairs={{0,32},{32,64},{64,96},{96,128},{128,160},{160,192},{192,224},{1,3... | collective-permute-start | bytes 786440 | tf_op jit(solution)/shard_map/ppermute | solution.py:509
  13.5 4.2 %collective-permute-start = (f32[4,160,128]{2,1,0:T(8,128)S(1)}, f32[4,160,128]{2,1,0:T(8,128)S(1)}, u32[]{:S(2)}, u32[]{:S(2)}) collective-permute-start(f32[4,160,128]{2,1,0:T(8,128)S(1)} %get-tuple-element.31), channel_id=1, source_target_pairs={{0,1},{1,0},{2,3},{3,2},{4,5},{5,4},{6,7},{7,6},{8,9},{9,8},{10,11... | collective-permute-start | bytes 983048 | tf_op jit(solution)/shard_map/ppermute | solution.py:494
  17.7 6.4 %collective-permute-start.2 = (f32[2,160,128]{2,1,0:T(8,128)S(1)}, f32[2,160,128]{2,1,0:T(8,128)S(1)}, u32[]{:S(2)}, u32[]{:S(2)}) collective-permute-start(f32[2,160,128]{2,1,0:T(8,128)S(1)} %select_add_fusion), channel_id=1, source_target_pairs={{0,2},{1,3},{2,0},{3,1},{4,6},{5,7},{6,4},{7,5},{8,10},{9,11},{10,... | collective-permute-start | bytes 491528 | tf_op jit(solution)/shard_map/ppermute | solution.py:494
  24.2 4.5 %collective-permute-start.3 = (f32[160,128]{1,0:T(8,128)S(1)}, f32[160,128]{1,0:T(8,128)S(1)}, u32[]{:S(2)}, u32[]{:S(2)}) collective-permute-start(f32[160,128]{1,0:T(8,128)S(1)} %select_bitcast_fusion), channel_id=1, source_target_pairs={{0,4},{1,5},{2,6},{3,7},{4,0},{5,1},{6,2},{7,3},{8,12},{9,13},{10,... | collective-permute-start | bytes 245768 | tf_op jit(solution)/shard_map/ppermute | solution.py:494
  28.7 6.0 %collective-permute-start.4 = (f32[160,128]{1,0:T(8,128)S(1)}, f32[160,128]{1,0:T(8,128)S(1)}, u32[]{:S(2)}, u32[]{:S(2)}) collective-permute-start(f32[160,128]{1,0:T(8,128)S(1)} %bitcast_add_fusion), channel_id=1, source_target_pairs={{0,8},{1,9},{2,10},{3,11},{4,12},{5,13},{6,14},{7,15},{8,0},{9,1},... | collective-permute-start | bytes 245768 | tf_op jit(solution)/shard_map/ppermute | solution.py:494
  34.7 8.6 %collective-permute-start.5 = (f32[160,128]{1,0:T(8,128)S(1)}, f32[160,128]{1,0:T(8,128)S(1)}, u32[]{:S(2)}, u32[]{:S(2)}) collective-permute-start(f32[160,128]{1,0:T(8,128)S(1)} %add.27.one_ref), channel_id=1, source_target_pairs={{0,24},{1,25},{2,26},{3,27},{4,28},{5,29},{6,30},{7,31},{8,16},{9,... | collective-permute-start | bytes 245768 | tf_op jit(solution)/shard_map/ppermute | solution.py:494
  47.1 4.1 %collective-permute-start.6 = (bf16[1,64,128]{2,1,0:T(8,128)(2,1)S(1)}, bf16[1,64,128]{2,1,0:T(8,128)(2,1)S(1)}, u32[]{:S(2)}, u32[]{:S(2)}) collective-permute-start(bf16[1,64,128]{2,1,0:T(8,128)(2,1)S(1)} %bitcast.15), channel_id=1, source_target_pairs={{0,4},{1,5},{2,6},{3,7},{4,0},{5,1},{6,2},{7,3},{8,12},{9,13},{10,... | collective-permute-start | bytes 49160 | tf_op jit(solution)/shard_map/ppermute | solution.py:494
  51.2 4.0 %collective-permute-start.7 = (bf16[2,64,128]{2,1,0:T(8,128)(2,1)S(1)}, bf16[2,64,128]{2,1,0:T(8,128)(2,1)S(1)}, u32[]{:S(2)}, u32[]{:S(2)}) collective-permute-start(bf16[2,64,128]{2,1,0:T(8,128)(2,1)S(1)} %pad_maximum_fusion.1.coefs_ref), channel_id=1, source_target_pairs={{0,2},{1,3},{2,0},{3,1},{4,6},{5,7},{6,4},{7,5},{8,10},{9,11},{10,... | collective-permute-start | bytes 98312 | tf_op jit(solution)/shard_map/ppermute | solution.py:494
  55.3 1.3 %collective-permute-start.8 = (bf16[4,64,128]{2,1,0:T(8,128)(2,1)S(1)}, bf16[4,64,128]{2,1,0:T(8,128)(2,1)S(1)}, u32[]{:S(2)}, u32[]{:S(2)}) collective-permute-start(bf16[4,64,128]{2,1,0:T(8,128)(2,1)S(1)} %pad_maximum_fusion), channel_id=1, source_target_pairs={{0,1},{1,0},{2,3},{3,2},{4,5},{5,4},{6,7},{7,6},{8,9},{9,8},{10,11... | collective-permute-start | bytes 196616 | tf_op jit(solution)/shard_map/ppermute | solution.py:494
  55.4 5.1 %copy-start = (s32[64]{0:T(128)S(1)}, s32[64]{0:T(128)}, u32[]{:S(2)}) copy-start(s32[64]{0:T(128)} %param.11) | copy-start | bytes 772
  55.4 5.1 %copy-start.1 = (s32[64]{0:T(128)S(1)}, s32[64]{0:T(128)}, u32[]{:S(2)}) copy-start(s32[64]{0:T(128)} %param.12) | copy-start | bytes 772
  55.4 5.1 %copy-start.2 = (s32[64]{0:T(128)S(1)}, s32[64]{0:T(128)}, u32[]{:S(2)}) copy-start(s32[64]{0:T(128)} %param.13) | copy-start | bytes 772
  56.6 8.2 %collective-permute-start.9 = (bf16[2,64,128]{2,1,0:T(8,128)(2,1)S(1)}, bf16[2,64,128]{2,1,0:T(8,128)(2,1)S(1)}, u32[]{:S(2)}, u32[]{:S(2)}) collective-permute-start(bf16[2,64,128]{2,1,0:T(8,128)(2,1)S(1)} %slice_select_fusion), channel_id=1, source_target_pairs={{0,32},{32,64},{64,96},{96,128},{128,160},{160,192},{192,224},{1,3... | collective-permute-start | bytes 98312 | tf_op jit(solution)/shard_map/ppermute | solution.py:509
